TPU v7x, 32 devices: a whole 2x2x4 slice. The times are simulated.
32 devices in a mesh: dom: 8 (over z, y), feat: 4 (over x, core).
Axes of the slice: x: 2, y: 2, z: 4, core: 2. Of those that a mesh axis runs over, the one named last changes fastest.
Arguments:
- grad_pre2: bfloat16 [16384, 512], P('dom', 'feat'), may hold values from -6 to 6
- aggregated2: bfloat16 [16384, 512], P('dom', 'feat'), may hold values from -6 to 6
- weight2: bfloat16 [512, 512], P('feat'), may hold values from -0.25 to 0.25
- pre1: bfloat16 [16384, 512], P('dom', 'feat'), may hold values from -6 to 6
- aggregated1: bfloat16 [16384, 512], P('dom', 'feat'), may hold values from -6 to 6
- weight1: bfloat16 [512, 512], P('feat'), may hold values from -0.25 to 0.25
- blocks: bfloat16 [128, 6, 128, 128], P('dom'), may hold values from -0.21875 to 0.21875
- targets: int32 [128, 6], P('dom'), may hold values from 0 to 127, as said below
Outputs:
- grad_weight2: float32 [512, 512], P('feat')
- grad_weight1: float32 [512, 512], P('feat')
- grad_input: bfloat16 [16384, 512], P('dom', 'feat')
Inputs may be any that keep to these rules, and one draw needn't show every extreme that they name: `targets`: partition p holds row tiles p * 16 to p * 16 + 15. Entry 0 of a row tile's list is the tile itself. Every other entry names a tile of partition p + o with -2 <= o <= 2: one of that partition's last 8 tiles if o < 0, one of its first 8 tiles if o > 0, any of its tiles if o = 0. The first row tile of every partition names partitions p - 2, p - 1, p + 1 and p + 2 wherever they exist; the number of blocks that name another partition varies from tile to tile.
All inputs are finite; a program needn't handle non-finite values.
Results may differ from a plain program's by a relative error of at most 0.015.
Values may be sent and summed in bfloat16 or wider, within the bound.
No kernel may reach another device: no remote copies, remote signals or barrier semaphores. Data moves between devices by JAX's collectives and lax.ppermute only.
A program may use at most 64 MiB of HBM per device.

v0:
```python
import math

import jax
import jax.numpy as jnp
from jax import lax
from jax.sharding import PartitionSpec as P

REACH = 2


def from_behind(value, axis, steps):
    count = lax.axis_size(axis)
    initial, last = (max(0, -steps), min(count, count - steps))
    return lax.ppermute(value, axis, [(source, source + steps) for source in range(initial, last)])


def dense_backward(grad_pre, aggregated, weight, grad_scale):
    columns = lax.all_gather(grad_pre, "feat", axis=1, tiled=True)
    running = lax.dot_general(
        columns, weight, (((1,), (1,)), ((), ())), preferred_element_type=jnp.float32
    )
    term_part = (
        lax.dot_general(
            aggregated, columns, (((0,), (0,)), ((), ())), preferred_element_type=jnp.float32
        )
        * grad_scale
    )
    weight_grad = term_part
    running, weight_grad = (running, weight_grad)
    return (running.astype(jnp.bfloat16), weight_grad)


def spread_tiles(values, blocks, targets):
    tile_count = blocks.shape[0]
    count = blocks.shape[1]
    tile_size = blocks.shape[2]
    col_count = values.shape[1]
    sources = values.reshape(tile_count, tile_size, col_count)
    products = jnp.einsum("rkij,rjc->rkic", blocks, sources, preferred_element_type=jnp.float32)
    first_tile = lax.axis_index("dom") * tile_count
    relative = targets.reshape(-1) - first_tile + REACH * tile_count
    summed = jax.ops.segment_sum(
        products.reshape(tile_count * count, tile_size, col_count),
        relative,
        num_segments=(2 * REACH + 1) * tile_count,
    )
    half = tile_count // 2
    owned = summed[REACH * tile_count : (REACH + 1) * tile_count]
    lower_half = owned[:half]
    upper_half = owned[half:]
    upward_parts = [
        summed[(REACH + distance) * tile_count : (REACH + distance) * tile_count + half].astype(
            jnp.bfloat16
        )
        for distance in range(1, REACH + 1)
    ]
    downward_parts = [
        summed[
            (REACH - distance + 1) * tile_count - half : (REACH - distance + 1) * tile_count
        ].astype(jnp.bfloat16)
        for distance in range(1, REACH + 1)
    ]
    for distance in range(1, REACH + 1):
        lower_half = lower_half + from_behind(upward_parts[distance - 1], "dom", distance).astype(
            jnp.float32
        )
        upper_half = upper_half + from_behind(
            downward_parts[distance - 1], "dom", -distance
        ).astype(jnp.float32)
    return jnp.concatenate([lower_half, upper_half], axis=0).reshape(
        tile_count * tile_size, col_count
    )


def shards(grad_pre2, aggregated2, weight2, pre1, aggregated1, weight1, blocks, targets):
    grad_scale = 1.0 / math.sqrt(grad_pre2.shape[0] * lax.axis_size("dom"))
    grad_agg2, second_part = dense_backward(grad_pre2, aggregated2, weight2, grad_scale)
    grad_weight2 = lax.psum(second_part, "dom")
    grad_hidden1 = spread_tiles(grad_agg2, blocks, targets)
    grad_pre1 = jnp.where(pre1 > 0, grad_hidden1, 0.0).astype(jnp.bfloat16)
    grad_agg1, first_part = dense_backward(grad_pre1, aggregated1, weight1, grad_scale)
    grad_input = spread_tiles(grad_agg1, blocks, targets).astype(jnp.bfloat16)
    grad_weight1 = lax.psum(first_part, "dom")
    return (grad_weight2, grad_weight1, grad_input)


def solution(mesh):
    in_specs = (
        P("dom", "feat"),
        P("dom", "feat"),
        P("feat", None),
        P("dom", "feat"),
        P("dom", "feat"),
        P("feat", None),
        P("dom", None, None, None),
        P("dom", None),
    )
    out_specs = (P("feat", None), P("feat", None), P("dom", "feat"))
    return jax.shard_map(shards, mesh=mesh, in_specs=in_specs, out_specs=out_specs, check_vma=False)
```

profile of v0, /device:TPU:0, one launch (start us, length us, event | category | flops | bytes accessed | tf_op | source)
XLA Modules:
  0.0 258.0 jit_solution(4071336133382441389)
XLA Ops:
  9.0 26.1 %all-gather.3.cloned.1.call-done = bf16[2048,512]{1,0:T(8,128)(2,1)} async-done(((bf16[2048,128]{1,0:T(8,128)(2,1)}), bf16[2048,512]{1,0:T(8,128)(2,1)}) %all-gather.3.cloned.1.call-update) | async-done | bytes 2097168 | tf_op jit(solution)/shard_map/all_gather | solution.py:18
  35.1 2.3 convolution_convert_fusion.1
  37.4 3.6 %fusion.10 = f32[16,128,6,128]{3,1,2,0:T(8,128)} fusion(bf16[16,128,128,1]{2,1,3,0:T(8,128)(2,1)S(1)} %bitcast.37, bf16[16,6,128,128]{3,2,1,0:T(8,128)(2,1)S(1)} %copy-done), kind=kOutput, calls=%fused_computation.24 | convolution fusion | flops 402653184 | bytes 9961472 | tf_op jit(solution)/shard_map/rkij,rjc->rkic/dot_general | solution.py:39
  41.1 6.6 %copy.17 = f32[96,128,128]{2,1,0:T(8,128)} copy(f32[96,128,128]{1,2,0:T(8,128)} %bitcast.35) | data formatting | bytes 12582912 | tf_op jit(solution)/shard_map/reshape | solution.py:43
  47.7 3.0 %broadcast.32.clone = f32[80,128,128]{2,1,0:T(8,128)} broadcast(f32[]{:T(128)} %constant.3.clone.1), dimensions={} | broadcast | bytes 5242884 | tf_op jit(solution)/shard_map/broadcast.3
  50.7 19.8 %scatter_fusion = f32[80,128,128]{2,1,0:T(8,128)} fusion(f32[80,128,128]{2,1,0:T(8,128)} %broadcast.32.clone, s32[96]{0:T(128)S(1)} %reshape.49, f32[96,128,128]{2,1,0:T(8,128)} %copy.17), kind=kCustom, calls=%fused_computation | custom fusion | flops 1572864 | bytes 18874752 | tf_op jit(solution)/shard_map/scatter-add | solution.py:42
  70.4 3.0 %convert.18 = bf16[80,128,128]{2,1,0:T(8,128)(2,1)S(1)} convert(f32[80,128,128]{2,1,0:T(8,128)} %scatter_fusion) | non-fusion elementwise | flops 1310720 | bytes 7864320 | tf_op jit(solution)/shard_map/convert.9
  73.6 3.8 %collective-permute-start.1 = (bf16[8,128,128]{2,1,0:T(8,128)(2,1)S(1)}, bf16[8,128,128]{2,1,0:T(8,128)(2,1)S(1)}, u32[]{:S(2)}, u32[]{:S(2)}) collective-permute-start(bf16[8,128,128]{2,1,0:T(8,128)(2,1)S(1)} %get-tuple-element.22), channel_id=1, source_target_pairs={{0,8},{4,12},{8,16},{12,20},{16,24},{20,28},{1,9},{5,13},{9,17},{1... | collective-permute-start | bytes 786440 | tf_op jit(solution)/shard_map/ppermute | solution.py:14
  77.4 3.4 %collective-permute-start = (bf16[8,128,128]{2,1,0:T(8,128)(2,1)S(1)}, bf16[8,128,128]{2,1,0:T(8,128)(2,1)S(1)}, u32[]{:S(2)}, u32[]{:S(2)}) collective-permute-start(bf16[8,128,128]{2,1,0:T(8,128)(2,1)S(1)} %get-tuple-element.19), channel_id=1, source_target_pairs={{0,4},{4,8},{8,12},{12,16},{16,20},{20,24},{24,28},{1,5},{5,9},{9,... | collective-permute-start | bytes 786440 | tf_op jit(solution)/shard_map/ppermute | solution.py:14
  83.4 3.1 %collective-permute-done = bf16[8,128,128]{2,1,0:T(8,128)(2,1)S(1)} collective-permute-done((bf16[8,128,128]{2,1,0:T(8,128)(2,1)S(1)}, bf16[8,128,128]{2,1,0:T(8,128)(2,1)S(1)}, u32[]{:S(2)}, u32[]{:S(2)}) %collective-permute-start) | collective-permute-done | bytes 262176 | tf_op jit(solution)/shard_map/ppermute | solution.py:14
  86.4 5.4 %collective-permute-done.3 = bf16[8,128,128]{2,1,0:T(8,128)(2,1)S(1)} collective-permute-done((bf16[8,128,128]{2,1,0:T(8,128)(2,1)S(1)}, bf16[8,128,128]{2,1,0:T(8,128)(2,1)S(1)}, u32[]{:S(2)}, u32[]{:S(2)}) %collective-permute-start.3) | collective-permute-done | bytes 262176 | tf_op jit(solution)/shard_map/ppermute | solution.py:14
  94.4 2.9 %convolution_multiply_fusion.1 = f32[128,512]{1,0:T(8,128)} fusion(bf16[2048,128]{1,0:T(8,128)(2,1)} %param.9, bf16[2048,512]{1,0:T(8,128)(2,1)} %all-gather.3.cloned.1.call-done), kind=kOutput, calls=%fused_computation.6 | convolution fusion | flops 268500992 | bytes 2883584 | tf_op jit(solution)/shard_map/dot_general | solution.py:23
  97.4 23.5 %all-gather.5.cloned.1.call-done = bf16[2048,512]{1,0:T(8,128)(2,1)} async-done(((bf16[2048,128]{1,0:T(8,128)(2,1)}), bf16[2048,512]{1,0:T(8,128)(2,1)}) %all-gather.5.cloned.1.call-update) | async-done | bytes 2097168 | tf_op jit(solution)/shard_map/all_gather | solution.py:18
  120.8 2.3 convolution_convert_fusion
  123.1 3.6 %fusion.11 = f32[16,128,6,128]{3,1,2,0:T(8,128)} fusion(bf16[16,128,128,1]{2,1,3,0:T(8,128)(2,1)S(1)} %bitcast.38, bf16[16,6,128,128]{3,2,1,0:T(8,128)(2,1)S(1)} %copy-done), kind=kOutput, calls=%fused_computation.25 | convolution fusion | flops 402653184 | bytes 9961472 | tf_op jit(solution)/shard_map/rkij,rjc->rkic/dot_general | solution.py:39
  126.8 6.6 %copy.19 = f32[96,128,128]{2,1,0:T(8,128)} copy(f32[96,128,128]{1,2,0:T(8,128)} %bitcast.36) | data formatting | bytes 12582912 | tf_op jit(solution)/shard_map/reshape | solution.py:43
  133.4 3.0 %broadcast.32 = f32[80,128,128]{2,1,0:T(8,128)} broadcast(f32[]{:T(128)} %constant.3.clone.1), dimensions={} | broadcast | bytes 5242884 | tf_op jit(solution)/shard_map/broadcast.3
  136.4 19.8 %scatter_fusion.1 = f32[80,128,128]{2,1,0:T(8,128)} fusion(f32[80,128,128]{2,1,0:T(8,128)} %broadcast.32, s32[96]{0:T(128)S(1)} %reshape.49, f32[96,128,128]{2,1,0:T(8,128)} %copy.19), kind=kCustom, calls=%fused_computation.1 | custom fusion | flops 1572864 | bytes 18874752 | tf_op jit(solution)/shard_map/scatter-add | solution.py:42
  156.2 3.1 %convert.19 = bf16[80,128,128]{2,1,0:T(8,128)(2,1)S(1)} convert(f32[80,128,128]{2,1,0:T(8,128)} %scatter_fusion.1) | non-fusion elementwise | flops 1310720 | bytes 7864320 | tf_op jit(solution)/shard_map/convert.5
  160.3 3.7 %collective-permute-start.5 = (bf16[8,128,128]{2,1,0:T(8,128)(2,1)}, bf16[8,128,128]{2,1,0:T(8,128)(2,1)S(1)}, u32[]{:S(2)}, u32[]{:S(2)}) collective-permute-start(bf16[8,128,128]{2,1,0:T(8,128)(2,1)} %get-tuple-element.18), channel_id=1, source_target_pairs={{0,8},{4,12},{8,16},{12,20},{16,24},{20,28},{1,9},{5,13},{9,17},{1... | collective-permute-start | bytes 786440 | tf_op jit(solution)/shard_map/ppermute | solution.py:14
  164.0 4.1 %collective-permute-start.4 = (bf16[8,128,128]{2,1,0:T(8,128)(2,1)}, bf16[8,128,128]{2,1,0:T(8,128)(2,1)}, u32[]{:S(2)}, u32[]{:S(2)}) collective-permute-start(bf16[8,128,128]{2,1,0:T(8,128)(2,1)} %get-tuple-element.15), channel_id=1, source_target_pairs={{0,4},{4,8},{8,12},{12,16},{16,20},{20,24},{24,28},{1,5},{5,9},{9,... | collective-permute-start | bytes 786440 | tf_op jit(solution)/shard_map/ppermute | solution.py:14
  173.3 6.1 %collective-permute-done.7 = bf16[8,128,128]{2,1,0:T(8,128)(2,1)} collective-permute-done((bf16[8,128,128]{2,1,0:T(8,128)(2,1)}, bf16[8,128,128]{2,1,0:T(8,128)(2,1)}, u32[]{:S(2)}, u32[]{:S(2)}) %collective-permute-start.7) | collective-permute-done | bytes 262176 | tf_op jit(solution)/shard_map/ppermute | solution.py:14
  182.0 66.0 %all-reduce.3.cloned.1.call-done = (f32[128,512]{1,0:T(8,128)}, f32[128,512]{0,1:T(8,128)}) async-done(((f32[128,512]{1,0:T(8,128)}, f32[128,512]{0,1:T(8,128)}), (f32[128,512]{1,0:T(8,128)}, f32[128,512]{0,1:T(8,128)})) %all-reduce.3.cloned.1.call-update) | async-done | bytes 524304 | tf_op jit(solution)/shard_map/psum | solution.py:78
  248.0 1.8 copy.20
  (37 shorter events, 17.5 us)
Async XLA Ops:
  7.2 30.3 %copy-start = (bf16[16,6,128,128]{3,2,1,0:T(8,128)(2,1)S(1)}, bf16[16,6,128,128]{3,2,1,0:T(8,128)(2,1)}, u32[]{:S(2)}) copy-start(bf16[16,6,128,128]{3,2,1,0:T(8,128)(2,1)} %param.14) | copy-start | bytes 9437188
  7.2 27.9 %all-gather.3.cloned.1.call-start = ((), (), s32[]{:S(2)}) async-start(), calls=%async_computation | async-start | bytes 2621440 | tf_op jit(solution)/shard_map/all_gather | solution.py:18
  7.9 112.9 %all-gather.5.cloned.1.call-start = ((), (), s32[]{:S(2)}) async-start(), calls=%async_computation.1 | async-start | bytes 2621440 | tf_op jit(solution)/shard_map/all_gather | solution.py:18
  73.4 19.9 %copy-start.2 = (bf16[2048,128]{1,0:T(8,128)(2,1)S(1)}, bf16[2048,128]{1,0:T(8,128)(2,1)}, u32[]{:S(2)}) copy-start(bf16[2048,128]{1,0:T(8,128)(2,1)} %param.11) | copy-start | bytes 1572868
  73.6 9.8 %collective-permute-start.1 = (bf16[8,128,128]{2,1,0:T(8,128)(2,1)S(1)}, bf16[8,128,128]{2,1,0:T(8,128)(2,1)S(1)}, u32[]{:S(2)}, u32[]{:S(2)}) collective-permute-start(bf16[8,128,128]{2,1,0:T(8,128)(2,1)S(1)} %get-tuple-element.22), channel_id=1, source_target_pairs={{0,8},{4,12},{8,16},{12,20},{16,24},{20,28},{1,9},{5,13},{9,17},{1... | collective-permute-start | bytes 786440 | tf_op jit(solution)/shard_map/ppermute | solution.py:14
  77.4 9.1 %collective-permute-start = (bf16[8,128,128]{2,1,0:T(8,128)(2,1)S(1)}, bf16[8,128,128]{2,1,0:T(8,128)(2,1)S(1)}, u32[]{:S(2)}, u32[]{:S(2)}) collective-permute-start(bf16[8,128,128]{2,1,0:T(8,128)(2,1)S(1)} %get-tuple-element.19), channel_id=1, source_target_pairs={{0,4},{4,8},{8,12},{12,16},{16,20},{20,24},{24,28},{1,5},{5,9},{9,... | collective-permute-start | bytes 786440 | tf_op jit(solution)/shard_map/ppermute | solution.py:14
  80.8 11.1 %collective-permute-start.3 = (bf16[8,128,128]{2,1,0:T(8,128)(2,1)S(1)}, bf16[8,128,128]{2,1,0:T(8,128)(2,1)S(1)}, u32[]{:S(2)}, u32[]{:S(2)}) collective-permute-start(bf16[8,128,128]{2,1,0:T(8,128)(2,1)S(1)} %get-tuple-element.20), channel_id=1, source_target_pairs={{8,0},{12,4},{16,8},{20,12},{24,16},{28,20},{9,1},{13,5},{17,9},{2... | collective-permute-start | bytes 786440 | tf_op jit(solution)/shard_map/ppermute | solution.py:14
  82.1 9.8 %collective-permute-start.2 = (bf16[8,128,128]{2,1,0:T(8,128)(2,1)S(1)}, bf16[8,128,128]{2,1,0:T(8,128)(2,1)S(1)}, u32[]{:S(2)}, u32[]{:S(2)}) collective-permute-start(bf16[8,128,128]{2,1,0:T(8,128)(2,1)S(1)} %get-tuple-element.21), channel_id=1, source_target_pairs={{4,0},{8,4},{12,8},{16,12},{20,16},{24,20},{28,24},{5,1},{9,5},{13... | collective-permute-start | bytes 786440 | tf_op jit(solution)/shard_map/ppermute | solution.py:14
  93.3 27.6 %copy-start.4 = (bf16[128,512]{1,0:T(8,128)(2,1)S(1)}, bf16[128,512]{1,0:T(8,128)(2,1)}, u32[]{:S(2)}) copy-start(bf16[128,512]{1,0:T(8,128)(2,1)} %param.13) | copy-start | bytes 393220
  94.4 153.6 %all-reduce.3.cloned.1.call-start = ((), (), s32[]{:S(2)}) async-start(), calls=%async_computation.2 | async-start | bytes 1048576 | tf_op jit(solution)/shard_map/psum | solution.py:78
  156.2 14.5 %copy-start.1 = (bf16[2048,512]{1,0:T(8,128)(2,1)S(1)}, bf16[2048,512]{1,0:T(8,128)(2,1)}, u32[]{:S(2)}) copy-start(bf16[2048,512]{1,0:T(8,128)(2,1)} %all-gather.5.cloned.1.call-done) | copy-start | bytes 6291460
  156.2 14.5 %copy-start.3 = (bf16[2048,128]{1,0:T(8,128)(2,1)S(1)}, bf16[2048,128]{1,0:T(8,128)(2,1)}, u32[]{:S(2)}) copy-start(bf16[2048,128]{1,0:T(8,128)(2,1)} %param.12) | copy-start | bytes 1572868
  160.3 11.8 %collective-permute-start.5 = (bf16[8,128,128]{2,1,0:T(8,128)(2,1)}, bf16[8,128,128]{2,1,0:T(8,128)(2,1)S(1)}, u32[]{:S(2)}, u32[]{:S(2)}) collective-permute-start(bf16[8,128,128]{2,1,0:T(8,128)(2,1)} %get-tuple-element.18), channel_id=1, source_target_pairs={{0,8},{4,12},{8,16},{12,20},{16,24},{20,28},{1,9},{5,13},{9,17},{1... | collective-permute-start | bytes 786440 | tf_op jit(solution)/shard_map/ppermute | solution.py:14
  164.0 9.4 %collective-permute-start.4 = (bf16[8,128,128]{2,1,0:T(8,128)(2,1)}, bf16[8,128,128]{2,1,0:T(8,128)(2,1)}, u32[]{:S(2)}, u32[]{:S(2)}) collective-permute-start(bf16[8,128,128]{2,1,0:T(8,128)(2,1)} %get-tuple-element.15), channel_id=1, source_target_pairs={{0,4},{4,8},{8,12},{12,16},{16,20},{20,24},{24,28},{1,5},{5,9},{9,... | collective-permute-start | bytes 786440 | tf_op jit(solution)/shard_map/ppermute | solution.py:14
  168.1 11.4 %collective-permute-start.7 = (bf16[8,128,128]{2,1,0:T(8,128)(2,1)}, bf16[8,128,128]{2,1,0:T(8,128)(2,1)}, u32[]{:S(2)}, u32[]{:S(2)}) collective-permute-start(bf16[8,128,128]{2,1,0:T(8,128)(2,1)} %get-tuple-element.16), channel_id=1, source_target_pairs={{8,0},{12,4},{16,8},{20,12},{24,16},{28,20},{9,1},{13,5},{17,9},{2... | collective-permute-start | bytes 786440 | tf_op jit(solution)/shard_map/ppermute | solution.py:14
  169.3 10.1 %collective-permute-start.6 = (bf16[8,128,128]{2,1,0:T(8,128)(2,1)}, bf16[8,128,128]{2,1,0:T(8,128)(2,1)}, u32[]{:S(2)}, u32[]{:S(2)}) collective-permute-start(bf16[8,128,128]{2,1,0:T(8,128)(2,1)} %get-tuple-element.17), channel_id=1, source_target_pairs={{4,0},{8,4},{12,8},{16,12},{20,16},{24,20},{28,24},{5,1},{9,5},{13... | collective-permute-start | bytes 786440 | tf_op jit(solution)/shard_map/ppermute | solution.py:14
Sparse Core Ops, SparseCore 0:
  9.5 25.5 all-gather.2
  94.5 26.3 all-gather.4
  172.3 75.7 all-reduce.2
where the time goes:
time: 259 us; the launch traced here: 258 us
  waiting for transfers between devices  132 us (51%)
  other arithmetic  51.5 us (20%)
  local copies, waits for them, and re-layouts  24 us (9%)
  starting transfers between devices  20.2 us (8%)
  matrix products  16.3 us (6%)
  between operations  13.9 us (5%)
    psum x1, waiting for transfers between devices, shards(): grad_weight2 = lax.psum(second_part, 'dom')  66 us
    all_gather x2, waiting for transfers between devices, dense_backward(): columns = lax.all_gather(grad_pre, 'feat', axis=1, tiled=True)  49.6 us
    scatter-add x2, other arithmetic, spread_tiles(): jax.ops.segment_sum(products.reshape(tile_count * count, tile_size, col_c...  39.5 us
    ppermute x8, starting transfers between devices, from_behind(): lax.ppermute(value, axis, [(source, source + steps) for source in range(i...  20.1 us
    ppermute x8, waiting for transfers between devices, from_behind(): lax.ppermute(value, axis, [(source, source + steps) for source in range(i...  15.8 us
    reshape x2, local copies, waits for them, and re-layouts, spread_tiles(): products.reshape(tile_count * count, tile_size, col_count)  13.2 us
    another operation x3, other arithmetic  7.86 us
    dot_general x2, matrix products, spread_tiles(): jnp.einsum('rkij,rjc->rkic', blocks, sources, preferred_element_type=jnp....  7.29 us
  transfers between devices with their start and end apart: 11, of which 7 were waited for; matrix products, arithmetic and copies ran while one was open for 3% of the time, Pallas kernels for 0%

commit v1 on v0

v1 whole, which is shorter than its diff:
```python
import functools
import math

import jax
import jax.numpy as jnp
from jax import lax
from jax.experimental import pallas as pl
from jax.experimental.pallas import tpu as pltpu
from jax.sharding import PartitionSpec as P

REACH = 2
CHUNKS = 2
VMEM = pl.BlockSpec(memory_space=pltpu.VMEM)
ANY = pl.BlockSpec(memory_space=pl.ANY)
SMEM = pl.BlockSpec(memory_space=pltpu.SMEM)


def shifted(value, axis, steps):
    count = lax.axis_size(axis)
    first, last = max(0, -steps), min(count, count - steps)
    return lax.ppermute(value, axis, [(s, s + steps) for s in range(first, last)])


def flipped(value, axis, mask):
    count = lax.axis_size(axis)
    return lax.ppermute(value, axis, [(s, s ^ mask) for s in range(count)])


def gather_pieces(value, axis):
    pieces = {0: value}
    mask = lax.axis_size(axis) // 2
    while mask:
        pieces.update({m | mask: flipped(v, axis, mask) for m, v in list(pieces.items())})
        mask //= 2
    return [pieces[m] for m in sorted(pieces)]


def spread_kernel(tiles, slots_ref, *refs):
    chunks = len(tiles)
    pieces = refs[0].shape[0]
    weight_ref, blocks_hbm = refs[0], refs[1]
    piece_refs = refs[2 : 2 + chunks * pieces]
    own_ref = refs[2 + chunks * pieces]
    out_refs = refs[3 + chunks * pieces : -4]
    values, blocks, total, sems = refs[-4:]
    tile_count, count, size, _ = blocks.shape
    for r in range(tile_count):
        pltpu.make_async_copy(blocks_hbm.at[r], blocks.at[r], sems.at[r]).start()
    total[...] = jnp.zeros_like(total)
    for c, tile_list in enumerate(tiles):
        for i, r in enumerate(tile_list):
            rows = pl.ds(i * size, size)
            value = jnp.zeros((size, size), jnp.float32)
            for m in range(pieces):
                value += lax.dot_general(
                    piece_refs[c * pieces + m][rows, :],
                    weight_ref[m],
                    (((1,), (1,)), ((), ())),
                    preferred_element_type=jnp.float32,
                )
            values[r] = value.astype(values.dtype)

    def body(r, carry):
        pltpu.make_async_copy(blocks_hbm.at[r], blocks.at[r], sems.at[r]).wait()
        products = jnp.dot(
            blocks[r].reshape(count * size, size), values[r], preferred_element_type=jnp.float32
        )
        for k in range(count):
            slot = slots_ref[r, k]
            total[slot] += products[k * size : (k + 1) * size]
        return carry

    lax.fori_loop(0, tile_count, body, 0, unroll=2)
    own_ref[...] = total[:tile_count]
    per = out_refs[0].shape[0]
    for n, out in enumerate(out_refs):
        out[...] = total[tile_count + n * per : tile_count + (n + 1) * per].astype(out.dtype)


def spread(chunk_pieces, weight, blocks, slots, tiles):
    tile_count, count, size, _ = blocks.shape
    half = tile_count // 2
    per = half // CHUNKS
    remote = 2 * REACH * half
    outs = [jax.ShapeDtypeStruct((tile_count, size, size), jnp.float32)]
    outs += [jax.ShapeDtypeStruct((per, size, size), jnp.bfloat16)] * (remote // per)
    flat = [p for pieces in chunk_pieces for p in pieces]
    results = pl.pallas_call(
        functools.partial(spread_kernel, tiles),
        out_shape=outs,
        in_specs=[SMEM, VMEM, ANY] + [VMEM] * len(flat),
        out_specs=[VMEM] * len(outs),
        scratch_shapes=[
            pltpu.VMEM((tile_count, size, size), jnp.bfloat16),
            pltpu.VMEM(blocks.shape, jnp.bfloat16),
            pltpu.VMEM((tile_count + remote, size, size), jnp.float32),
            pltpu.SemaphoreType.DMA((tile_count,)),
        ],
        cost_estimate=pl.CostEstimate(
            flops=2 * tile_count * (count + weight.shape[0]) * size**3,
            bytes_accessed=blocks.size * 2 + tile_count * size * size * 16,
            transcendentals=0,
        ),
        compiler_params=pltpu.CompilerParams(vmem_limit_bytes=24 << 20),
        name="spread",
    )(slots, weight, blocks, *flat)
    own, sends = results[0], results[1:]
    parts = half // per
    steps = [1, 2, -1, -2]
    received = [[None] * parts for _ in steps]
    for c in range(parts):
        for d in (1, 3, 0, 2):
            received[d][c] = shifted(sends[d * parts + c], "dom", steps[d])
    chunks = []
    for c in range(parts):
        low = own[c * per : (c + 1) * per]
        high = own[half + c * per : half + (c + 1) * per]
        for distance in range(REACH):
            low = low + received[distance][c].astype(jnp.float32)
            high = high + received[REACH + distance][c].astype(jnp.float32)
        chunks.append(jnp.concatenate([low, high], axis=0))
    return chunks


def weight_kernel(scale, chunks, agg_ref, *refs):
    pieces = len(refs) // chunks
    out_ref = refs[-1]
    for m in range(pieces):
        total = None
        row = 0
        for c in range(chunks):
            piece = refs[c * pieces + m]
            rows = piece.shape[0]
            term = lax.dot_general(
                agg_ref[row : row + rows, :],
                piece[...],
                (((0,), (0,)), ((), ())),
                preferred_element_type=jnp.float32,
            )
            total = term if total is None else total + term
            row += rows
        out_ref[m] = (total * scale).astype(out_ref.dtype)


def weight_term(agg, chunk_pieces, scale):
    flat = [p for pieces in chunk_pieces for p in pieces]
    pieces = len(chunk_pieces[0])
    width = agg.shape[1]
    return pl.pallas_call(
        functools.partial(weight_kernel, scale, len(chunk_pieces)),
        out_shape=jax.ShapeDtypeStruct((pieces, width, width), jnp.bfloat16),
        in_specs=[VMEM] * (1 + len(flat)),
        out_specs=VMEM,
        cost_estimate=pl.CostEstimate(
            flops=2 * pieces * agg.shape[0] * width**2,
            bytes_accessed=agg.size * 2 * (1 + pieces),
            transcendentals=0,
        ),
        compiler_params=pltpu.CompilerParams(vmem_limit_bytes=12 << 20),
        name="weight_term",
    )(agg, *flat)


def dom_sum(value):
    count = lax.axis_size("dom")
    mask = 1
    while mask < count:
        other = flipped(value, "dom", mask)
        total = value.astype(jnp.float32) + other.astype(jnp.float32)
        mask *= 2
        value = total.astype(jnp.bfloat16) if mask < count else total
    return value


def unpermute(value):
    pieces, width, _ = value.shape
    index = lax.axis_index("feat")
    order = jnp.arange(pieces) ^ index
    return jnp.take(value, order, axis=0).transpose(1, 0, 2).reshape(width, pieces * width)


def permuted_weight(weight):
    width = weight.shape[0]
    pieces = weight.shape[1] // width
    index = lax.axis_index("feat")
    blocks = weight.reshape(width, pieces, width).transpose(1, 0, 2)
    return jnp.take(blocks, jnp.arange(pieces) ^ index, axis=0)


def shards(grad_pre2, aggregated2, weight2, pre1, aggregated1, weight1, blocks, targets):
    tile_count, _, size, _ = blocks.shape
    half = tile_count // 2
    per = half // CHUNKS
    scale = 1.0 / math.sqrt(grad_pre2.shape[0] * lax.axis_size("dom"))
    width = grad_pre2.shape[1]
    place = lax.axis_index("dom")
    part = targets // tile_count
    offset = part - place
    within = targets - part * tile_count
    slots = jnp.where(
        offset == 0,
        within,
        jnp.where(
            offset > 0,
            tile_count + (offset - 1) * half + within,
            tile_count + REACH * half + (-offset - 1) * half + within - half,
        ),
    ).astype(jnp.int32)
    tiles = [
        [base + c * per + i for base in (0, half) for i in range(per)] for c in range(CHUNKS)
    ]

    def chunked(array):
        tiled = array.reshape(tile_count, size, width)
        return [
            jnp.concatenate(
                [tiled[c * per : (c + 1) * per], tiled[half + c * per : half + (c + 1) * per]],
                axis=0,
            ).reshape(-1, width)
            for c in range(CHUNKS)
        ]

    w2, w1 = permuted_weight(weight2), permuted_weight(weight1)
    gathered2 = [gather_pieces(c, "feat") for c in chunked(grad_pre2)]
    hidden = spread(gathered2, w2, blocks, slots, tiles)
    second = weight_term(jnp.concatenate(chunked(aggregated2), axis=0), gathered2, scale)
    grad_pre1 = [
        jnp.where(p > 0, h.reshape(-1, width), 0.0).astype(jnp.bfloat16)
        for p, h in zip(chunked(pre1), hidden)
    ]
    gathered1 = [gather_pieces(c, "feat") for c in grad_pre1]
    inputs = spread(gathered1, w1, blocks, slots, tiles)
    first = weight_term(jnp.concatenate(chunked(aggregated1), axis=0), gathered1, scale)
    stacked = [c.astype(jnp.bfloat16).reshape(2, per, size, width) for c in inputs]
    grad_input = jnp.concatenate(stacked, axis=1).reshape(-1, width)
    return (unpermute(dom_sum(second)), unpermute(dom_sum(first)), grad_input)


def solution(mesh):
    in_specs = (
        P("dom", "feat"),
        P("dom", "feat"),
        P("feat", None),
        P("dom", "feat"),
        P("dom", "feat"),
        P("feat", None),
        P("dom", None, None, None),
        P("dom", None),
    )
    out_specs = (P("feat", None), P("feat", None), P("dom", "feat"))
    return jax.shard_map(shards, mesh=mesh, in_specs=in_specs, out_specs=out_specs, check_vma=False)
```

time: 259 us -> 135 us (0.52)
  waiting for transfers between devices: 132 us -> 20.1 us
  other arithmetic: 51.5 us -> 5.64 us
  starting transfers between devices: 20.2 us -> 62 us
  Pallas kernels: 0 us -> 26.1 us
  matrix products: 16.3 us -> 0 us
  between operations: 13.9 us -> 1.28 us
  local copies, waits for them, and re-layouts: 24 us -> 18.8 us
    psum x1 -> x0, waiting for transfers between devices: 66 us -> none  [shards(): grad_weight2 = lax.psum(second_part, 'dom')]
    all_gather x2 -> x0, waiting for transfers between devices: 49.6 us -> none  [dense_backward(): columns = lax.all_gather(grad_pre, 'feat', axis=1, tiled=True)]
    ppermute x8 -> x34, starting transfers between devices: 20.1 us -> 62 us  [the longest x16 39.7 us: shifted(): lax.ppermute(value, axis, [(s, s + steps) for s in range(first, last)])]
    scatter-add x2 -> x0, other arithmetic: 39.5 us -> none  [spread_tiles(): jax.ops.segment_sum(products.reshape(tile_count * count, tile_size, col_c...]
    pallas_call x0 -> x4, Pallas kernels: none -> 26.1 us  [the longest x2 23.3 us: spread(): pl.pallas_call(functools.partial(spread_kernel, tiles), out_shape=outs, i...]
    dot_general x6 -> x0, matrix products: 16.3 us -> none  [the longest x2 7.29 us: spread_tiles(): jnp.einsum('rkij,rjc->rkic', blocks, sources, preferred_element_type=jnp....]
    reshape x2, local copies, waits for them, and re-layouts: 13.2 us -> 2.69 us  [permuted_weight(): blocks = weight.reshape(width, pieces, width).transpose(1, 0, 2)]
    another operation x3 -> x1, other arithmetic: 7.86 us -> 1.39 us
  transfers between devices with their start and end apart: 11 -> 34, of which waited for: 7 -> 6; matrix products, arithmetic and copies ran while one was open for 3% -> 15% of each run, Pallas kernels for 0% -> 11%
where the time goes in v1:
time: 135 us; the launch traced here: 134 us
  starting transfers between devices  62 us (46%)
  Pallas kernels  26.1 us (19%)
  waiting for transfers between devices  20.1 us (15%)
  local copies, waits for them, and re-layouts  18.8 us (14%)
  other arithmetic  5.64 us (4%)
    ppermute x16, starting transfers between devices, shifted(): lax.ppermute(value, axis, [(s, s + steps) for s in range(first, last)])  39.7 us
    pallas_call x2, Pallas kernels, spread(): pl.pallas_call(functools.partial(spread_kernel, tiles), out_shape=outs, i...  23.3 us
    ppermute x18, starting transfers between devices, flipped(): return lax.ppermute(value, axis, [(s, s ^ mask) for s in range(count)])  22.3 us
    ppermute x18, waiting for transfers between devices, flipped(): return lax.ppermute(value, axis, [(s, s ^ mask) for s in range(count)])  12.2 us
    ppermute x16, waiting for transfers between devices, shifted(): lax.ppermute(value, axis, [(s, s + steps) for s in range(first, last)])  7.86 us
    unnamed x31, local copies, waits for them, and re-layouts  6.05 us
    slice x4, local copies, waits for them, and re-layouts, chunked(): tiled[c * per:(c + 1) * per]  5.34 us
    gather x2, local copies, waits for them, and re-layouts, permuted_weight(): return jnp.take(blocks, jnp.arange(pieces) ^ index, axis=0)  3.32 us
  transfers between devices with their start and end apart: 34, of which 6 were waited for; matrix products, arithmetic and copies ran while one was open for 15% of the time, Pallas kernels for 11%

profile of v1, /device:TPU:0, one launch (start us, length us, event | category | flops | bytes accessed | tf_op | source)
XLA Modules:
  0.0 133.9 jit_solution(15748611297985491782)
XLA Ops:
  1.8 3.0 %collective-permute-start.1 = (bf16[1024,128]{1,0:T(8,128)(2,1)S(1)}, bf16[1024,128]{1,0:T(8,128)(2,1)}, u32[]{:S(2)}, u32[]{:S(2)}) collective-permute-start(bf16[1024,128]{1,0:T(8,128)(2,1)S(1)} %bitcast.45), channel_id=1, source_target_pairs={{0,2},{1,3},{2,0},{3,1},{4,6},{5,7},{6,4},{7,5},{8,10},{9,11},{10,... | collective-permute-start | bytes 786440 | tf_op jit(solution)/shard_map/ppermute | solution.py:26
  13.4 2.1 %gather_fusion.3 = bf16[4,128,128]{2,1,0:T(8,128)(2,1)} fusion(bf16[4,128,128]{2,1,0:T(8,128)(2,1)} %bitcast.59, s32[1024]{0:T(1024)S(1)} %pad_clamp_fusion), kind=kCustom, calls=%fused_computation.3.clone | custom fusion | bytes 262160 | tf_op jit(solution)/shard_map/jit(_take)/gather | solution.py:187
  15.5 1.9 %fusion.7 = (bf16[512,128]{1,0:T(8,128)(2,1)}, bf16[512,128]{1,0:T(8,128)(2,1)}, bf16[512,128]{1,0:T(8,128)(2,1)}, bf16[512,128]{1,0:T(8,128)(2,1)}) fusion(bf16[2048,128]{1,0:T(8,128)(2,1)} %param.13), kind=kLoop, calls=%fused_computation.52 | loop fusion | bytes 1048576 | tf_op jit(solution)/shard_map/slice | solution.py:217
  23.4 11.7 %spread.2 = (f32[16,128,128]{2,1,0:T(8,128)S(1)}, bf16[4,128,128]{2,1,0:T(8,128)(2,1)S(1)}, bf16[4,128,128]{2,1,0:T(8,128)(2,1)S(1)}, bf16[4,128,128]{2,1,0:T(8,...) custom-call(s32[16,6]{1,0:T(8,128)S(1)} %select_select_fusion.slots_, ...), custom_call_target="tpu_custom_call" | custom-call | flops 671088640 | bytes 7340032 | tf_op jit(solution)/shard_map/spread/pallas_call | solution.py:88
  35.1 3.7 %collective-permute-start.9 = (bf16[4,128,128]{2,1,0:T(8,128)(2,1)S(1)}, bf16[4,128,128]{2,1,0:T(8,128)(2,1)S(1)}, u32[]{:S(2)}, u32[]{:S(2)}) collective-permute-start(bf16[4,128,128]{2,1,0:T(8,128)(2,1)S(1)} %get-tuple-element.24), channel_id=1, source_target_pairs={{0,4},{4,8},{8,12},{12,16},{16,20},{20,24},{24,28},{1,5},{5,9},{9,... | collective-permute-start | bytes 393224 | tf_op jit(solution)/shard_map/ppermute | solution.py:21
  38.8 3.5 %collective-permute-start.10 = (bf16[4,128,128]{2,1,0:T(8,128)(2,1)S(1)}, bf16[4,128,128]{2,1,0:T(8,128)(2,1)S(1)}, u32[]{:S(2)}, u32[]{:S(2)}) collective-permute-start(bf16[4,128,128]{2,1,0:T(8,128)(2,1)S(1)} %get-tuple-element.25), channel_id=1, source_target_pairs={{0,8},{4,12},{8,16},{12,20},{16,24},{20,28},{1,9},{5,13},{9,17},{1... | collective-permute-start | bytes 393224 | tf_op jit(solution)/shard_map/ppermute | solution.py:21
  45.0 4.6 %collective-permute-start.16 = (bf16[4,128,128]{2,1,0:T(8,128)(2,1)S(1)}, bf16[4,128,128]{2,1,0:T(8,128)(2,1)S(1)}, u32[]{:S(2)}, u32[]{:S(2)}) collective-permute-start(bf16[4,128,128]{2,1,0:T(8,128)(2,1)S(1)} %get-tuple-element.28), channel_id=1, source_target_pairs={{0,4},{4,8},{8,12},{12,16},{16,20},{20,24},{24,28},{1,5},{5,9},{9,... | collective-permute-start | bytes 393224 | tf_op jit(solution)/shard_map/ppermute | solution.py:21
  49.6 4.6 %collective-permute-start.17 = (bf16[4,128,128]{2,1,0:T(8,128)(2,1)S(1)}, bf16[4,128,128]{2,1,0:T(8,128)(2,1)S(1)}, u32[]{:S(2)}, u32[]{:S(2)}) collective-permute-start(bf16[4,128,128]{2,1,0:T(8,128)(2,1)S(1)} %get-tuple-element.29), channel_id=1, source_target_pairs={{0,8},{4,12},{8,16},{12,20},{16,24},{20,28},{1,9},{5,13},{9,17},{1... | collective-permute-start | bytes 393224 | tf_op jit(solution)/shard_map/ppermute | solution.py:21
  56.8 2.0 %weight_term.2 = bf16[4,128,128]{2,1,0:T(8,128)(2,1)S(1)} custom-call(bf16[2048,128]{1,0:T(8,128)(2,1)S(1)} %pad_maximum_fusion.agg_ref, bf16[1024,128]{1,0:T(8,128)(2,1)S(1)} %bitcast.48, bf16[1024,128]{1,0:T(8,128)(2,1)} %collective-permute-done.refs_1_.refs_3_, bf16[1024,128]{1,0:T(8,128)(2,1)} %collective-permute-done.1.refs_2_.refs_4_, ...), custom_call_target="tpu_custom_call" | custom-call | flops 268435456 | bytes 2621440 | tf_op jit(solution)/shard_map/weight_term/pallas_call | solution.py:149
  58.8 3.1 %collective-permute-start.6 = (bf16[4,128,128]{2,1,0:T(8,128)(2,1)S(1)}, bf16[4,128,128]{2,1,0:T(8,128)(2,1)S(1)}, u32[]{:S(2)}, u32[]{:S(2)}) collective-permute-start(bf16[4,128,128]{2,1,0:T(8,128)(2,1)S(1)} %weight_term.2), channel_id=1, source_target_pairs={{0,4},{4,0},{8,12},{12,8},{16,20},{20,16},{24,28},{28,24},{1,5},{5... | collective-permute-start | bytes 393224 | tf_op jit(solution)/shard_map/ppermute | solution.py:26
  62.0 3.3 %collective-permute-done.19 = bf16[4,128,128]{2,1,0:T(8,128)(2,1)S(1)} collective-permute-done((bf16[4,128,128]{2,1,0:T(8,128)(2,1)S(1)}, bf16[4,128,128]{2,1,0:T(8,128)(2,1)S(1)}, u32[]{:S(2)}, u32[]{:S(2)}) %collective-permute-start.19) | collective-permute-done | bytes 131104 | tf_op jit(solution)/shard_map/ppermute | solution.py:21
  67.8 1.8 %collective-permute-start.7 = (bf16[4,128,128]{2,1,0:T(8,128)(2,1)S(1)}, bf16[4,128,128]{2,1,0:T(8,128)(2,1)S(1)}, u32[]{:S(2)}, u32[]{:S(2)}) collective-permute-start(bf16[4,128,128]{2,1,0:T(8,128)(2,1)S(1)} %add_convert_fusion.7), channel_id=1, source_target_pairs={{0,8},{4,12},{8,0},{12,4},{16,24},{20,28},{24,16},{28,20},{1,9},{5... | collective-permute-start | bytes 393224 | tf_op jit(solution)/shard_map/ppermute | solution.py:26
  70.2 4.3 %collective-permute-done.14.refs_2_.refs_4_ = bf16[1024,128]{1,0:T(8,128)(2,1)S(1)} collective-permute-done((bf16[1024,128]{1,0:T(8,128)(2,1)S(1)}, bf16[1024,128]{1,0:T(8,128)(2,1)S(1)}, u32[]{:S(2)}, u32[]{:S(2)}) %collective-permute-start.14) | collective-permute-done | bytes 262176 | tf_op jit(solution)/shard_map/ppermute | solution.py:26
  74.6 2.8 %collective-permute-done.21.refs_6_.refs_8_ = bf16[1024,128]{1,0:T(8,128)(2,1)S(1)} collective-permute-done((bf16[1024,128]{1,0:T(8,128)(2,1)S(1)}, bf16[1024,128]{1,0:T(8,128)(2,1)S(1)}, u32[]{:S(2)}, u32[]{:S(2)}) %collective-permute-start.21) | collective-permute-done | bytes 262176 | tf_op jit(solution)/shard_map/ppermute | solution.py:26
  77.4 1.9 %collective-permute-start.8 = (bf16[4,128,128]{2,1,0:T(8,128)(2,1)S(1)}, bf16[4,128,128]{2,1,0:T(8,128)(2,1)S(1)}, u32[]{:S(2)}, u32[]{:S(2)}) collective-permute-start(bf16[4,128,128]{2,1,0:T(8,128)(2,1)S(1)} %add_convert_fusion.6), channel_id=1, source_target_pairs={{0,16},{4,20},{8,24},{12,28},{16,0},{20,4},{24,8},{28,12},{1,17},{... | collective-permute-start | bytes 393224 | tf_op jit(solution)/shard_map/ppermute | solution.py:26
  79.5 11.7 %spread.3 = (f32[16,128,128]{2,1,0:T(8,128)S(1)}, bf16[4,128,128]{2,1,0:T(8,128)(2,1)}, bf16[4,128,128]{2,1,0:T(8,128)(2,1)S(1)}, bf16[4,128,128]{2,1,0:T(8,128)...) custom-call(s32[16,6]{1,0:T(8,128)S(1)} %select_select_fusion.slots_, ...), custom_call_target="tpu_custom_call" | custom-call | flops 671088640 | bytes 7340032 | tf_op jit(solution)/shard_map/spread/pallas_call | solution.py:88
  91.2 2.1 %collective-permute-start.26 = (bf16[4,128,128]{2,1,0:T(8,128)(2,1)}, bf16[4,128,128]{2,1,0:T(8,128)(2,1)S(1)}, u32[]{:S(2)}, u32[]{:S(2)}) collective-permute-start(bf16[4,128,128]{2,1,0:T(8,128)(2,1)} %get-tuple-element.33), channel_id=1, source_target_pairs={{0,4},{4,8},{8,12},{12,16},{16,20},{20,24},{24,28},{1,5},{5,9},{9,... | collective-permute-start | bytes 393224 | tf_op jit(solution)/shard_map/ppermute | solution.py:21
  93.3 3.5 %collective-permute-start.27 = (bf16[4,128,128]{2,1,0:T(8,128)(2,1)}, bf16[4,128,128]{2,1,0:T(8,128)(2,1)S(1)}, u32[]{:S(2)}, u32[]{:S(2)}) collective-permute-start(bf16[4,128,128]{2,1,0:T(8,128)(2,1)} %get-tuple-element.34), channel_id=1, source_target_pairs={{0,8},{4,12},{8,16},{12,20},{16,24},{20,28},{1,9},{5,13},{9,17},{1... | collective-permute-start | bytes 393224 | tf_op jit(solution)/shard_map/ppermute | solution.py:21
  98.9 2.7 %collective-permute-start.23 = (bf16[4,128,128]{2,1,0:T(8,128)(2,1)S(1)}, bf16[4,128,128]{2,1,0:T(8,128)(2,1)S(1)}, u32[]{:S(2)}, u32[]{:S(2)}) collective-permute-start(bf16[4,128,128]{2,1,0:T(8,128)(2,1)S(1)} %weight_term.3), channel_id=1, source_target_pairs={{0,4},{4,0},{8,12},{12,8},{16,20},{20,16},{24,28},{28,24},{1,5},{5... | collective-permute-start | bytes 393224 | tf_op jit(solution)/shard_map/ppermute | solution.py:26
  103.5 1.9 %collective-permute-start.30 = (bf16[4,128,128]{2,1,0:T(8,128)(2,1)}, bf16[4,128,128]{2,1,0:T(8,128)(2,1)S(1)}, u32[]{:S(2)}, u32[]{:S(2)}) collective-permute-start(bf16[4,128,128]{2,1,0:T(8,128)(2,1)} %copy-done.4), channel_id=1, source_target_pairs={{0,4},{4,8},{8,12},{12,16},{16,20},{20,24},{24,28},{1,5},{5,9},{9,... | collective-permute-start | bytes 393224 | tf_op jit(solution)/shard_map/ppermute | solution.py:21
  105.5 5.5 %collective-permute-start.31 = (bf16[4,128,128]{2,1,0:T(8,128)(2,1)}, bf16[4,128,128]{2,1,0:T(8,128)(2,1)S(1)}, u32[]{:S(2)}, u32[]{:S(2)}) collective-permute-start(bf16[4,128,128]{2,1,0:T(8,128)(2,1)} %copy-done.3), channel_id=1, source_target_pairs={{0,8},{4,12},{8,16},{12,20},{16,24},{20,28},{1,9},{5,13},{9,17},{1... | collective-permute-start | bytes 393224 | tf_op jit(solution)/shard_map/ppermute | solution.py:21
  113.7 4.4 %collective-permute-start.24 = (bf16[4,128,128]{2,1,0:T(8,128)(2,1)S(1)}, bf16[4,128,128]{2,1,0:T(8,128)(2,1)S(1)}, u32[]{:S(2)}, u32[]{:S(2)}) collective-permute-start(bf16[4,128,128]{2,1,0:T(8,128)(2,1)S(1)} %add_convert_fusion.5), channel_id=1, source_target_pairs={{0,8},{4,12},{8,0},{12,4},{16,24},{20,28},{24,16},{28,20},{1,9},{5... | collective-permute-start | bytes 393224 | tf_op jit(solution)/shard_map/ppermute | solution.py:26
  118.1 4.6 %collective-permute-done.33 = bf16[4,128,128]{2,1,0:T(8,128)(2,1)S(1)} collective-permute-done((bf16[4,128,128]{2,1,0:T(8,128)(2,1)S(1)}, bf16[4,128,128]{2,1,0:T(8,128)(2,1)S(1)}, u32[]{:S(2)}, u32[]{:S(2)}) %collective-permute-start.33) | collective-permute-done | bytes 131104 | tf_op jit(solution)/shard_map/ppermute | solution.py:21
  126.5 4.7 %collective-permute-done.25 = bf16[4,128,128]{2,1,0:T(8,128)(2,1)S(1)} collective-permute-done((bf16[4,128,128]{2,1,0:T(8,128)(2,1)S(1)}, bf16[4,128,128]{2,1,0:T(8,128)(2,1)S(1)}, u32[]{:S(2)}, u32[]{:S(2)}) %collective-permute-start.25) | collective-permute-done | bytes 131104 | tf_op jit(solution)/shard_map/ppermute | solution.py:26
  (117 shorter events, 37.2 us)
Async XLA Ops:
  1.8 18.5 %collective-permute-start.1 = (bf16[1024,128]{1,0:T(8,128)(2,1)S(1)}, bf16[1024,128]{1,0:T(8,128)(2,1)}, u32[]{:S(2)}, u32[]{:S(2)}) collective-permute-start(bf16[1024,128]{1,0:T(8,128)(2,1)S(1)} %bitcast.45), channel_id=1, source_target_pairs={{0,2},{1,3},{2,0},{3,1},{4,6},{5,7},{6,4},{7,5},{8,10},{9,11},{10,... | collective-permute-start | bytes 786440 | tf_op jit(solution)/shard_map/ppermute | solution.py:26
  4.9 17.3 %collective-permute-start = (bf16[1024,128]{1,0:T(8,128)(2,1)S(1)}, bf16[1024,128]{1,0:T(8,128)(2,1)}, u32[]{:S(2)}, u32[]{:S(2)}) collective-permute-start(bf16[1024,128]{1,0:T(8,128)(2,1)S(1)} %bitcast.46), channel_id=1, source_target_pairs={{0,1},{1,0},{2,3},{3,2},{4,5},{5,4},{6,7},{7,6},{8,9},{9,8},{10,11... | collective-permute-start | bytes 786440 | tf_op jit(solution)/shard_map/ppermute | solution.py:26
  5.6 14.9 %collective-permute-start.4 = (bf16[1024,128]{1,0:T(8,128)(2,1)}, bf16[1024,128]{1,0:T(8,128)(2,1)}, u32[]{:S(2)}, u32[]{:S(2)}) collective-permute-start(bf16[1024,128]{1,0:T(8,128)(2,1)} %bitcast.11.refs_4_.refs_6_), channel_id=1, source_target_pairs={{0,2},{1,3},{2,0},{3,1},{4,6},{5,7},{6,4},{7,5},{8,10},{9,11},{10,... | collective-permute-start | bytes 786440 | tf_op jit(solution)/shard_map/ppermute | solution.py:26
  5.7 16.5 %collective-permute-start.3 = (bf16[1024,128]{1,0:T(8,128)(2,1)}, bf16[1024,128]{1,0:T(8,128)(2,1)}, u32[]{:S(2)}, u32[]{:S(2)}) collective-permute-start(bf16[1024,128]{1,0:T(8,128)(2,1)} %bitcast.11.refs_4_.refs_6_), channel_id=1, source_target_pairs={{0,1},{1,0},{2,3},{3,2},{4,5},{5,4},{6,7},{7,6},{8,9},{9,8},{10,11... | collective-permute-start | bytes 786440 | tf_op jit(solution)/shard_map/ppermute | solution.py:26
  35.1 14.5 %collective-permute-start.9 = (bf16[4,128,128]{2,1,0:T(8,128)(2,1)S(1)}, bf16[4,128,128]{2,1,0:T(8,128)(2,1)S(1)}, u32[]{:S(2)}, u32[]{:S(2)}) collective-permute-start(bf16[4,128,128]{2,1,0:T(8,128)(2,1)S(1)} %get-tuple-element.24), channel_id=1, source_target_pairs={{0,4},{4,8},{8,12},{12,16},{16,20},{20,24},{24,28},{1,5},{5,9},{9,... | collective-permute-start | bytes 393224 | tf_op jit(solution)/shard_map/ppermute | solution.py:21
  38.8 15.3 %collective-permute-start.10 = (bf16[4,128,128]{2,1,0:T(8,128)(2,1)S(1)}, bf16[4,128,128]{2,1,0:T(8,128)(2,1)S(1)}, u32[]{:S(2)}, u32[]{:S(2)}) collective-permute-start(bf16[4,128,128]{2,1,0:T(8,128)(2,1)S(1)} %get-tuple-element.25), channel_id=1, source_target_pairs={{0,8},{4,12},{8,16},{12,20},{16,24},{20,28},{1,9},{5,13},{9,17},{1... | collective-permute-start | bytes 393224 | tf_op jit(solution)/shard_map/ppermute | solution.py:21
  42.3 13.2 %collective-permute-start.11 = (bf16[4,128,128]{2,1,0:T(8,128)(2,1)S(1)}, bf16[4,128,128]{2,1,0:T(8,128)(2,1)S(1)}, u32[]{:S(2)}, u32[]{:S(2)}) collective-permute-start(bf16[4,128,128]{2,1,0:T(8,128)(2,1)S(1)} %get-tuple-element.26), channel_id=1, source_target_pairs={{4,0},{8,4},{12,8},{16,12},{20,16},{24,20},{28,24},{5,1},{9,5},{13... | collective-permute-start | bytes 393224 | tf_op jit(solution)/shard_map/ppermute | solution.py:21
  43.7 15.1 %collective-permute-start.12 = (bf16[4,128,128]{2,1,0:T(8,128)(2,1)S(1)}, bf16[4,128,128]{2,1,0:T(8,128)(2,1)S(1)}, u32[]{:S(2)}, u32[]{:S(2)}) collective-permute-start(bf16[4,128,128]{2,1,0:T(8,128)(2,1)S(1)} %get-tuple-element.27), channel_id=1, source_target_pairs={{8,0},{12,4},{16,8},{20,12},{24,16},{28,20},{9,1},{13,5},{17,9},{2... | collective-permute-start | bytes 393224 | tf_op jit(solution)/shard_map/ppermute | solution.py:21
  45.0 17.0 %collective-permute-start.16 = (bf16[4,128,128]{2,1,0:T(8,128)(2,1)S(1)}, bf16[4,128,128]{2,1,0:T(8,128)(2,1)S(1)}, u32[]{:S(2)}, u32[]{:S(2)}) collective-permute-start(bf16[4,128,128]{2,1,0:T(8,128)(2,1)S(1)} %get-tuple-element.28), channel_id=1, source_target_pairs={{0,4},{4,8},{8,12},{12,16},{16,20},{20,24},{24,28},{1,5},{5,9},{9,... | collective-permute-start | bytes 393224 | tf_op jit(solution)/shard_map/ppermute | solution.py:21
  49.6 12.4 %collective-permute-start.17 = (bf16[4,128,128]{2,1,0:T(8,128)(2,1)S(1)}, bf16[4,128,128]{2,1,0:T(8,128)(2,1)S(1)}, u32[]{:S(2)}, u32[]{:S(2)}) collective-permute-start(bf16[4,128,128]{2,1,0:T(8,128)(2,1)S(1)} %get-tuple-element.29), channel_id=1, source_target_pairs={{0,8},{4,12},{8,16},{12,20},{16,24},{20,28},{1,9},{5,13},{9,17},{1... | collective-permute-start | bytes 393224 | tf_op jit(solution)/shard_map/ppermute | solution.py:21
  55.4 9.8 %collective-permute-start.19 = (bf16[4,128,128]{2,1,0:T(8,128)(2,1)S(1)}, bf16[4,128,128]{2,1,0:T(8,128)(2,1)S(1)}, u32[]{:S(2)}, u32[]{:S(2)}) collective-permute-start(bf16[4,128,128]{2,1,0:T(8,128)(2,1)S(1)} %get-tuple-element.31), channel_id=1, source_target_pairs={{8,0},{12,4},{16,8},{20,12},{24,16},{28,20},{9,1},{13,5},{17,9},{2... | collective-permute-start | bytes 393224 | tf_op jit(solution)/shard_map/ppermute | solution.py:21
  67.2 10.2 %collective-permute-start.21 = (bf16[1024,128]{1,0:T(8,128)(2,1)S(1)}, bf16[1024,128]{1,0:T(8,128)(2,1)S(1)}, u32[]{:S(2)}, u32[]{:S(2)}) collective-permute-start(bf16[1024,128]{1,0:T(8,128)(2,1)S(1)} %bitcast.41), channel_id=1, source_target_pairs={{0,2},{1,3},{2,0},{3,1},{4,6},{5,7},{6,4},{7,5},{8,10},{9,11},{10,... | collective-permute-start | bytes 786440 | tf_op jit(solution)/shard_map/ppermute | solution.py:26
  69.7 9.8 %collective-permute-start.13 = (bf16[1024,128]{1,0:T(8,128)(2,1)S(1)}, bf16[1024,128]{1,0:T(8,128)(2,1)S(1)}, u32[]{:S(2)}, u32[]{:S(2)}) collective-permute-start(bf16[1024,128]{1,0:T(8,128)(2,1)S(1)} %bitcast.38), channel_id=1, source_target_pairs={{0,1},{1,0},{2,3},{3,2},{4,5},{5,4},{6,7},{7,6},{8,9},{9,8},{10,11... | collective-permute-start | bytes 786440 | tf_op jit(solution)/shard_map/ppermute | solution.py:26
  69.8 9.7 %collective-permute-start.20 = (bf16[1024,128]{1,0:T(8,128)(2,1)S(1)}, bf16[1024,128]{1,0:T(8,128)(2,1)S(1)}, u32[]{:S(2)}, u32[]{:S(2)}) collective-permute-start(bf16[1024,128]{1,0:T(8,128)(2,1)S(1)} %bitcast.42), channel_id=1, source_target_pairs={{0,1},{1,0},{2,3},{3,2},{4,5},{5,4},{6,7},{7,6},{8,9},{9,8},{10,11... | collective-permute-start | bytes 786440 | tf_op jit(solution)/shard_map/ppermute | solution.py:26
  77.4 24.1 %collective-permute-start.8 = (bf16[4,128,128]{2,1,0:T(8,128)(2,1)S(1)}, bf16[4,128,128]{2,1,0:T(8,128)(2,1)S(1)}, u32[]{:S(2)}, u32[]{:S(2)}) collective-permute-start(bf16[4,128,128]{2,1,0:T(8,128)(2,1)S(1)} %add_convert_fusion.6), channel_id=1, source_target_pairs={{0,16},{4,20},{8,24},{12,28},{16,0},{20,4},{24,8},{28,12},{1,17},{... | collective-permute-start | bytes 393224 | tf_op jit(solution)/shard_map/ppermute | solution.py:26
  91.2 12.3 %collective-permute-start.26 = (bf16[4,128,128]{2,1,0:T(8,128)(2,1)}, bf16[4,128,128]{2,1,0:T(8,128)(2,1)S(1)}, u32[]{:S(2)}, u32[]{:S(2)}) collective-permute-start(bf16[4,128,128]{2,1,0:T(8,128)(2,1)} %get-tuple-element.33), channel_id=1, source_target_pairs={{0,4},{4,8},{8,12},{12,16},{16,20},{20,24},{24,28},{1,5},{5,9},{9,... | collective-permute-start | bytes 393224 | tf_op jit(solution)/shard_map/ppermute | solution.py:21
  93.3 12.2 %collective-permute-start.27 = (bf16[4,128,128]{2,1,0:T(8,128)(2,1)}, bf16[4,128,128]{2,1,0:T(8,128)(2,1)S(1)}, u32[]{:S(2)}, u32[]{:S(2)}) collective-permute-start(bf16[4,128,128]{2,1,0:T(8,128)(2,1)} %get-tuple-element.34), channel_id=1, source_target_pairs={{0,8},{4,12},{8,16},{12,20},{16,24},{20,28},{1,9},{5,13},{9,17},{1... | collective-permute-start | bytes 393224 | tf_op jit(solution)/shard_map/ppermute | solution.py:21
  96.8 14.2 %collective-permute-start.28 = (bf16[4,128,128]{2,1,0:T(8,128)(2,1)}, bf16[4,128,128]{2,1,0:T(8,128)(2,1)S(1)}, u32[]{:S(2)}, u32[]{:S(2)}) collective-permute-start(bf16[4,128,128]{2,1,0:T(8,128)(2,1)} %get-tuple-element.35), channel_id=1, source_target_pairs={{4,0},{8,4},{12,8},{16,12},{20,16},{24,20},{28,24},{5,1},{9,5},{13... | collective-permute-start | bytes 393224 | tf_op jit(solution)/shard_map/ppermute | solution.py:21
  98.9 13.5 %collective-permute-start.23 = (bf16[4,128,128]{2,1,0:T(8,128)(2,1)S(1)}, bf16[4,128,128]{2,1,0:T(8,128)(2,1)S(1)}, u32[]{:S(2)}, u32[]{:S(2)}) collective-permute-start(bf16[4,128,128]{2,1,0:T(8,128)(2,1)S(1)} %weight_term.3), channel_id=1, source_target_pairs={{0,4},{4,0},{8,12},{12,8},{16,20},{20,16},{24,28},{28,24},{1,5},{5... | collective-permute-start | bytes 393224 | tf_op jit(solution)/shard_map/ppermute | solution.py:26
  102.2 11.5 %collective-permute-start.29 = (bf16[4,128,128]{2,1,0:T(8,128)(2,1)}, bf16[4,128,128]{2,1,0:T(8,128)(2,1)S(1)}, u32[]{:S(2)}, u32[]{:S(2)}) collective-permute-start(bf16[4,128,128]{2,1,0:T(8,128)(2,1)} %copy-done.5), channel_id=1, source_target_pairs={{8,0},{12,4},{16,8},{20,12},{24,16},{28,20},{9,1},{13,5},{17,9},{2... | collective-permute-start | bytes 393224 | tf_op jit(solution)/shard_map/ppermute | solution.py:21
  103.5 14.6 %collective-permute-start.30 = (bf16[4,128,128]{2,1,0:T(8,128)(2,1)}, bf16[4,128,128]{2,1,0:T(8,128)(2,1)S(1)}, u32[]{:S(2)}, u32[]{:S(2)}) collective-permute-start(bf16[4,128,128]{2,1,0:T(8,128)(2,1)} %copy-done.4), channel_id=1, source_target_pairs={{0,4},{4,8},{8,12},{12,16},{16,20},{20,24},{24,28},{1,5},{5,9},{9,... | collective-permute-start | bytes 393224 | tf_op jit(solution)/shard_map/ppermute | solution.py:21
  105.5 12.6 %collective-permute-start.31 = (bf16[4,128,128]{2,1,0:T(8,128)(2,1)}, bf16[4,128,128]{2,1,0:T(8,128)(2,1)S(1)}, u32[]{:S(2)}, u32[]{:S(2)}) collective-permute-start(bf16[4,128,128]{2,1,0:T(8,128)(2,1)} %copy-done.3), channel_id=1, source_target_pairs={{0,8},{4,12},{8,16},{12,20},{16,24},{20,28},{1,9},{5,13},{9,17},{1... | collective-permute-start | bytes 393224 | tf_op jit(solution)/shard_map/ppermute | solution.py:21
  112.4 10.3 %collective-permute-start.33 = (bf16[4,128,128]{2,1,0:T(8,128)(2,1)S(1)}, bf16[4,128,128]{2,1,0:T(8,128)(2,1)S(1)}, u32[]{:S(2)}, u32[]{:S(2)}) collective-permute-start(bf16[4,128,128]{2,1,0:T(8,128)(2,1)S(1)} %get-tuple-element.40), channel_id=1, source_target_pairs={{8,0},{12,4},{16,8},{20,12},{24,16},{28,20},{9,1},{13,5},{17,9},{2... | collective-permute-start | bytes 393224 | tf_op jit(solution)/shard_map/ppermute | solution.py:21
  113.7 10.4 %collective-permute-start.24 = (bf16[4,128,128]{2,1,0:T(8,128)(2,1)S(1)}, bf16[4,128,128]{2,1,0:T(8,128)(2,1)S(1)}, u32[]{:S(2)}, u32[]{:S(2)}) collective-permute-start(bf16[4,128,128]{2,1,0:T(8,128)(2,1)S(1)} %add_convert_fusion.5), channel_id=1, source_target_pairs={{0,8},{4,12},{8,0},{12,4},{16,24},{20,28},{24,16},{28,20},{1,9},{5... | collective-permute-start | bytes 393224 | tf_op jit(solution)/shard_map/ppermute | solution.py:26
  (23 other events, 261.4 us)

commit v2 on v0

v2 whole, which is shorter than its diff:
```python
import functools
import math

import jax
import jax.numpy as jnp
from jax import lax
from jax.experimental import pallas as pl
from jax.experimental.pallas import tpu as pltpu
from jax.sharding import PartitionSpec as P


REACH = 2
VMEM = pl.BlockSpec(memory_space=pltpu.VMEM)
ANY = pl.BlockSpec(memory_space=pl.ANY)
SMEM = pl.BlockSpec(memory_space=pltpu.SMEM)


def exchanged(value, axis, partner):
    count = lax.axis_size(axis)
    pairs = [(s, partner(s)) for s in range(count) if 0 <= partner(s) < count]
    return lax.ppermute(value, axis, pairs)


SWAPS = [
    lambda s: ((s + 1) ^ 1) - 1,
    lambda s: s ^ 1,
    lambda s: ((s + 2) ^ 2) - 2,
    lambda s: s ^ 2,
]


def after(value, *earlier):
    return lax.optimization_barrier((value, *earlier))[0]


def gather_pieces(chunks, axis, earlier=()):
    held = [{0: chunk} for chunk in chunks]
    mask = lax.axis_size(axis) // 2
    first = True
    while mask:
        moves = [list(pieces) for pieces in held]
        for step in range(len(moves[0])):
            for c, (pieces, move) in enumerate(zip(held, moves)):
                m = move[step]
                got = exchanged(pieces[m], axis, lambda s, mask=mask: s ^ mask)
                pieces[m | mask] = after(got, *earlier) if first and earlier and c == 0 else got
        first = False
        mask //= 2
    return [[pieces[m] for m in sorted(pieces)] for pieces in held]


def prepare_kernel(targets_hbm, blocks_hbm, *refs):
    count = (len(refs) - 5) // 2
    weight_refs, slots_ref, blocks_ref = refs[:count], refs[count], refs[count + 1]
    outs, (targets_ref, target_sem, block_sem) = refs[count + 2 : -3], refs[-3:]
    block_copy = pltpu.make_async_copy(blocks_hbm, blocks_ref, block_sem)
    target_copy = pltpu.make_async_copy(targets_hbm, targets_ref, target_sem)
    block_copy.start()
    target_copy.start()
    place = lax.axis_index("feat")
    for weight_ref, out in zip(weight_refs, outs):
        width, total = weight_ref.shape
        for m in range(total // width):
            start = pl.multiple_of((place ^ m) * width, width)
            out[m * width : (m + 1) * width, :] = weight_ref[:, pl.ds(start, width)].T
    tile_count, entries = slots_ref.shape
    half = tile_count // 2
    index = lax.axis_index("dom")
    odd, upper = index & 1, (index & 2) // 2
    target_copy.wait()

    def body(r, carry):
        for k in range(entries):
            target = targets_ref[r, k]
            part = lax.div(target, jnp.int32(tile_count))
            offset = part - index
            within = target - part * tile_count
            up = offset > 0
            near = jnp.where(up, 1 - odd, odd)
            far = 2 + jnp.where(up, 1 - upper, upper)
            swap = jnp.where(jnp.abs(offset) == 1, near, far)
            outer = tile_count + swap * half + jnp.where(up, within, within - half)
            slots_ref[r, k] = jnp.where(offset == 0, within, outer)
        return carry

    lax.fori_loop(0, tile_count, body, 0)
    block_copy.wait()


def prepare(targets, blocks, weights):
    outs = [
        jax.ShapeDtypeStruct(targets.shape, jnp.int32),
        jax.ShapeDtypeStruct(blocks.shape, blocks.dtype),
    ]
    outs += [jax.ShapeDtypeStruct(w.shape[::-1], w.dtype) for w in weights]
    return pl.pallas_call(
        prepare_kernel,
        out_shape=outs,
        in_specs=[ANY, pl.BlockSpec(memory_space=pltpu.HBM)] + [VMEM] * len(weights),
        out_specs=[SMEM] + [VMEM] * (len(outs) - 1),
        scratch_shapes=[
            pltpu.SMEM(targets.shape, jnp.int32),
            pltpu.SemaphoreType.DMA,
            pltpu.SemaphoreType.DMA,
        ],
        compiler_params=pltpu.CompilerParams(vmem_limit_bytes=8 << 20),
        cost_estimate=pl.CostEstimate(flops=0, bytes_accessed=4 * blocks.size, transcendentals=0),
        name="prepare",
    )(targets, blocks, *weights)


def spread_kernel(chunks, slots_ref, weights, blocks, *refs):
    width = weights.shape[1]
    pieces = weights.shape[0] // width
    piece_refs, (own_ref, *sends, values, total) = (
        refs[: chunks * pieces],
        refs[chunks * pieces :],
    )
    tile_count, count, size, _ = blocks.shape
    total[...] = jnp.zeros_like(total)
    group = 2
    per = tile_count // chunks // group

    def value_body(i, carry, c):
        rows = pl.ds(pl.multiple_of(i * group * size, group * size), group * size)
        left = jnp.concatenate(
            [piece_refs[c * pieces + m][rows, :] for m in range(pieces)], axis=1
        )
        value = jnp.dot(left, weights[...], preferred_element_type=jnp.float32)
        tiles = pl.ds(c * per * group + i * group, group)
        values[tiles] = value.astype(values.dtype).reshape(group, size, width)
        return carry

    for c in range(chunks):
        lax.fori_loop(0, per, functools.partial(value_body, c=c), 0, unroll=2)

    def body(r, carry):
        value = values[r]
        for k in range(count):
            slot = slots_ref[r, k]
            total[slot] += jnp.dot(blocks[r, k], value, preferred_element_type=jnp.float32)
        return carry

    lax.fori_loop(0, tile_count, body, 0, unroll=4)
    own_ref[...] = total[:tile_count]
    half = sends[0].shape[0]
    for n, send in enumerate(sends):
        start = tile_count + n * half
        send[...] = total[start : start + half].astype(send.dtype)


def spread(chunk_pieces, weight, blocks, slots):
    tile_count, count, size, _ = blocks.shape
    half = tile_count // 2
    width = weight.shape[1]
    outs = [jax.ShapeDtypeStruct((tile_count, size, width), jnp.float32)]
    outs += [jax.ShapeDtypeStruct((half, size, width), jnp.bfloat16)] * len(SWAPS)
    flat = [p for pieces in chunk_pieces for p in pieces]
    return pl.pallas_call(
        functools.partial(spread_kernel, len(chunk_pieces)),
        out_shape=outs,
        in_specs=[SMEM] + [VMEM] * (2 + len(flat)),
        out_specs=[VMEM] * len(outs),
        scratch_shapes=[
            pltpu.VMEM((tile_count, size, width), jnp.bfloat16),
            pltpu.VMEM((tile_count + 2 * REACH * half, size, width), jnp.float32),
        ],
        cost_estimate=pl.CostEstimate(
            flops=2 * tile_count * size * width * (count * size + weight.shape[0]),
            bytes_accessed=blocks.size * 2 + tile_count * size * width * 16,
            transcendentals=0,
        ),
        compiler_params=pltpu.CompilerParams(vmem_limit_bytes=16 << 20),
        name="spread",
    )(slots, weight, blocks, *flat)


def join_kernel(masked, own, next_over, across, next_apart, apart, *refs):
    tile_count, size, _ = own.shape
    half = tile_count // 2
    index = lax.axis_index("dom")
    odd, upper = (index & 1) == 1, (index & 2) == 2
    if masked:
        mask, *outs = refs
    else:
        value, other, summed, out = refs
        outs = [out.at[: half * size, :], out.at[half * size :, :]]
        summed[...] = value[...].astype(jnp.float32) + other[...].astype(jnp.float32)

    def write(side, near, far):
        out = outs[side]
        for t in range(half):
            total = own[side * half + t]
            total += near[t].astype(jnp.float32) + far[t].astype(jnp.float32)
            if masked:
                first = (side * half + t) * size
                total = jnp.where(mask[first : first + size, :] > 0, total, 0.0)
            out[t * size : (t + 1) * size, :] = total.astype(out.dtype)

    for is_odd in (False, True):
        for is_upper in (False, True):

            @pl.when((odd == is_odd) & (upper == is_upper))
            def _(is_odd=is_odd, is_upper=is_upper):
                near = [across, next_over] if is_odd else [next_over, across]
                far = [apart, next_apart] if is_upper else [next_apart, apart]
                write(0, near[0], far[0])
                write(1, near[1], far[1])


def boundary(own, sends):
    got = [exchanged(send, "dom", swap) for send, swap in zip(sends, SWAPS)]
    return own, *got


def join(sums, outs, mask=None, terms=()):
    masked = mask is not None
    args = [*sums, mask] if masked else [*sums, *terms]
    return pl.pallas_call(
        functools.partial(join_kernel, masked),
        out_shape=outs,
        in_specs=[VMEM] * len(args),
        out_specs=[VMEM] * len(outs),
        compiler_params=pltpu.CompilerParams(vmem_limit_bytes=8 << 20),
        cost_estimate=pl.CostEstimate(
            flops=0, bytes_accessed=12 * sums[0].size, transcendentals=0
        ),
        name="join",
    )(*args)


def weight_kernel(scale, chunks, agg_ref, *refs):
    pieces = len(refs) // chunks
    out_ref = refs[-1]
    width = agg_ref.shape[1]
    place = lax.axis_index("feat")
    for m in range(pieces):
        total = jnp.zeros((width, width), jnp.float32)
        row = 0
        for c in range(chunks):
            piece = refs[c * pieces + m]
            rows = piece.shape[0]
            total += lax.dot_general(
                agg_ref[row : row + rows, :],
                piece[...],
                (((0,), (0,)), ((), ())),
                preferred_element_type=jnp.float32,
            )
            row += rows
        start = pl.multiple_of((place ^ m) * width, width)
        out_ref[:, pl.ds(start, width)] = (total * scale).astype(out_ref.dtype)


def weight_term(agg, chunk_pieces, scale):
    flat = [p for pieces in chunk_pieces for p in pieces]
    pieces = len(chunk_pieces[0])
    width = agg.shape[1]
    return pl.pallas_call(
        functools.partial(weight_kernel, scale, len(chunk_pieces)),
        out_shape=jax.ShapeDtypeStruct((width, pieces * width), jnp.bfloat16),
        in_specs=[VMEM] * (1 + len(flat)),
        out_specs=VMEM,
        cost_estimate=pl.CostEstimate(
            flops=2 * pieces * agg.shape[0] * width**2,
            bytes_accessed=agg.size * 2 * (1 + pieces),
            transcendentals=0,
        ),
        compiler_params=pltpu.CompilerParams(vmem_limit_bytes=8 << 20),
        name="weight_term",
    )(agg, *flat)


def sum_steps(value, waits=()):
    masks = [1]
    mask = lax.axis_size("dom") // 2
    while mask > 1:
        masks.append(mask)
        mask //= 2
    waits = list(waits)
    for n, mask in enumerate(masks):
        other = exchanged(value, "dom", lambda s, mask=mask: s ^ mask)
        if waits:
            other = after(other, *waits.pop(0))
        if n + 1 == len(masks):
            return value, other
        total = value.astype(jnp.float32) + other.astype(jnp.float32)
        value = total.astype(jnp.bfloat16)


def shards(grad_pre2, aggregated2, weight2, pre1, aggregated1, weight1, blocks, targets):
    nodes, width = grad_pre2.shape
    scale = 1.0 / math.sqrt(nodes * lax.axis_size("dom"))
    rows = nodes // 2
    half = jax.ShapeDtypeStruct((rows, width), jnp.bfloat16)
    slots, blocks, weight2, weight1 = prepare(targets, blocks, [weight2, weight1])
    gathered2 = gather_pieces(
        [grad_pre2[:rows], lax.optimization_barrier(grad_pre2)[rows:]], "feat", [weight2]
    )
    own, *sends = spread(gathered2, weight2, blocks, slots)
    second = weight_term(after(aggregated2, sends[0]), gathered2, scale)
    sums = boundary(own, sends)
    sums = [*sums[:2], *lax.optimization_barrier((second, *sums[2:]))[1:]]
    grad_pre1 = join(sums, [half, half], mask=pre1)
    gathered1 = gather_pieces(grad_pre1, "feat")
    first = weight_term(aggregated1, gathered1, scale)
    own, *sends = spread(gathered1, weight1, blocks, slots)
    second = sum_steps(after(second, grad_pre1[0]), [[gathered1[0][2]], [sends[0]]])
    second = second[0].astype(jnp.float32) + second[1].astype(jnp.float32)
    sums = boundary(own, sends)
    outs = [
        jax.ShapeDtypeStruct(first.shape, jnp.float32),
        jax.ShapeDtypeStruct((nodes, width), jnp.bfloat16),
    ]
    first, grad_input = join(sums, outs, terms=sum_steps(first))
    return (second, first, grad_input)


def solution(mesh):
    in_specs = (
        P("dom", "feat"),
        P("dom", "feat"),
        P("feat", None),
        P("dom", "feat"),
        P("dom", "feat"),
        P("feat", None),
        P("dom", None, None, None),
        P("dom", None),
    )
    out_specs = (P("feat", None), P("feat", None), P("dom", "feat"))
    return jax.shard_map(shards, mesh=mesh, in_specs=in_specs, out_specs=out_specs, check_vma=False)
```

time: 259 us -> 89.5 us (0.35)
  waiting for transfers between devices: 132 us -> 31.1 us
  other arithmetic: 51.5 us -> 0.87 us
  local copies, waits for them, and re-layouts: 24 us -> 6.41 us
  starting transfers between devices: 20.2 us -> 37.1 us
  matrix products: 16.3 us -> 0 us
  between operations: 13.9 us -> 0.82 us
  Pallas kernels: 0 us -> 12.9 us
    psum x1 -> x0, waiting for transfers between devices: 66 us -> none  [shards(): grad_weight2 = lax.psum(second_part, 'dom')]
    all_gather x2 -> x0, waiting for transfers between devices: 49.6 us -> none  [dense_backward(): columns = lax.all_gather(grad_pre, 'feat', axis=1, tiled=True)]
    scatter-add x2 -> x0, other arithmetic: 39.5 us -> none  [spread_tiles(): jax.ops.segment_sum(products.reshape(tile_count * count, tile_size, col_c...]
    ppermute x8 -> x26, starting transfers between devices: 20.1 us -> 37.1 us  [exchanged(): return lax.ppermute(value, axis, pairs)]
    dot_general x6 -> x0, matrix products: 16.3 us -> none  [the longest x2 7.29 us: spread_tiles(): jnp.einsum('rkij,rjc->rkic', blocks, sources, preferred_element_type=jnp....]
    ppermute x8 -> x26, waiting for transfers between devices: 15.8 us -> 31.1 us  [exchanged(): return lax.ppermute(value, axis, pairs)]
    reshape x2 -> x0, local copies, waits for them, and re-layouts: 13.2 us -> none  [spread_tiles(): products.reshape(tile_count * count, tile_size, col_count)]
    pallas_call x0 -> x7, Pallas kernels: none -> 12.9 us  [the longest x2 7.42 us: spread(): pl.pallas_call(functools.partial(spread_kernel, len(chunk_pieces)), out_s...]
  transfers between devices with their start and end apart: 11 -> 26, of which waited for: 7 -> 10; matrix products, arithmetic and copies ran while one was open for 3% -> 3% of each run, Pallas kernels for 0% -> 9%
where the time goes in v2:
time: 89.5 us; the launch traced here: 89.2 us
  starting transfers between devices  37.1 us (41%)
  waiting for transfers between devices  31.1 us (35%)
  Pallas kernels  12.9 us (14%)
  local copies, waits for them, and re-layouts  6.41 us (7%)
    ppermute x26, starting transfers between devices, exchanged(): return lax.ppermute(value, axis, pairs)  37.1 us
    ppermute x26, waiting for transfers between devices, exchanged(): return lax.ppermute(value, axis, pairs)  31.1 us
    pallas_call x2, Pallas kernels, spread(): pl.pallas_call(functools.partial(spread_kernel, len(chunk_pieces)), out_s...  7.42 us
    unnamed x13, local copies, waits for them, and re-layouts  4.48 us
    pallas_call x1, Pallas kernels, prepare(): pl.pallas_call(prepare_kernel, out_shape=outs, in_specs=[ANY, pl.BlockSpe...  2.52 us
  transfers between devices with their start and end apart: 26, of which 10 were waited for; matrix products, arithmetic and copies ran while one was open for 3% of the time, Pallas kernels for 9%

profile of v2, /device:TPU:0, one launch (start us, length us, event | category | flops | bytes accessed | tf_op | source)
XLA Modules:
  0.0 89.2 jit_solution(13940105495514995753)
XLA Ops:
  0.6 1.0 %slice.6.refs_0_ = bf16[1024,128]{1,0:T(8,128)(2,1)S(1)} slice(bf16[2048,128]{1,0:T(8,128)(2,1)} %param.8), slice={[0:1024], [0:128]} | slice | bytes 524288 | tf_op jit(solution)/shard_map/slice | solution.py:297
  1.6 3.0 %collective-permute-start.1 = (bf16[1024,128]{1,0:T(8,128)(2,1)S(1)}, bf16[1024,128]{1,0:T(8,128)(2,1)S(1)}, u32[]{:S(2)}, u32[]{:S(2)}) collective-permute-start(bf16[1024,128]{1,0:T(8,128)(2,1)S(1)} %slice.6.refs_0_), channel_id=1, source_target_pairs={{0,2},{1,3},{2,0},{3,1},{4,6},{5,7},{6,4},{7,5},{8,10},{9,11},{10,... | collective-permute-start | bytes 786440 | tf_op jit(solution)/shard_map/ppermute | solution.py:21
  4.6 1.0 %slice.8.refs_4_ = bf16[1024,128]{1,0:T(8,128)(2,1)S(1)} slice(bf16[2048,128]{1,0:T(8,128)(2,1)} %param.8), slice={[1024:2048], [0:128]} | slice | bytes 524288 | tf_op jit(solution)/shard_map/slice | solution.py:297
  7.0 1.9 %copy-done = bf16[16,6,128,128]{3,2,1,0:T(8,128)(2,1)S(1)} copy-done((bf16[16,6,128,128]{3,2,1,0:T(8,128)(2,1)S(1)}, bf16[16,6,128,128]{3,2,1,0:T(8,128)(2,1)}, u32[]{:S(2)}) %copy-start) | copy-done | bytes 3145752
  8.9 0.9 %copy-done.4 = bf16[128,512]{1,0:T(8,128)(2,1)S(1)} copy-done((bf16[128,512]{1,0:T(8,128)(2,1)S(1)}, bf16[128,512]{1,0:T(8,128)(2,1)}, u32[]{:S(2)}) %copy-start.4) | copy-done | bytes 131096
  10.7 2.5 %prepare.1 = (s32[16,6]{1,0:T(8,128)S(1)}, bf16[16,6,128,128]{3,2,1,0:T(8,128)(2,1)S(1)}, bf16[512,128]{1,0:T(8,128)(2,1)S(1)}, bf16[512,128]{1,0:T(8,128)(2,1)S(1)}) custom-call(s32[16,6]{1,0:T(8,128)S(1)} %copy.11.targets_hbm, bf16[16,6,128,128]{3,2,1,0:T(8,128)(2,1)S(1)} %copy-done, bf16[128,512]{1,0:T(8,128)(2,1)S(1)} %copy-done.4, ...), custom_call_target="tpu_custom_call" | custom-call | bytes 6291456 | tf_op jit(solution)/shard_map/prepare/pallas_call | solution.py:96
  13.3 3.3 %collective-permute-done.4.refs_6_ = bf16[1024,128]{1,0:T(8,128)(2,1)S(1)} collective-permute-done((bf16[1024,128]{1,0:T(8,128)(2,1)S(1)}, bf16[1024,128]{1,0:T(8,128)(2,1)S(1)}, u32[]{:S(2)}, u32[]{:S(2)}) %collective-permute-start.4) | collective-permute-done | bytes 262176 | tf_op jit(solution)/shard_map/ppermute | solution.py:21
  17.1 1.0 %collective-permute-done.5.refs_7_ = bf16[1024,128]{1,0:T(8,128)(2,1)S(1)} collective-permute-done((bf16[1024,128]{1,0:T(8,128)(2,1)S(1)}, bf16[1024,128]{1,0:T(8,128)(2,1)S(1)}, u32[]{:S(2)}, u32[]{:S(2)}) %collective-permute-start.5) | collective-permute-done | bytes 262176 | tf_op jit(solution)/shard_map/ppermute | solution.py:21
  18.5 3.7 %spread.2 = (f32[16,128,128]{2,1,0:T(8,128)S(1)}, bf16[8,128,128]{2,1,0:T(8,128)(2,1)S(1)}, bf16[8,128,128]{2,1,0:T(8,128)(2,1)S(1)}, bf16[8,128,128]{2,1,0:T(8,128)(2,1)S(1)}, bf16[8,128,128]{2,1,0:T(8,128)(2,1)S(1)}) custom-call(s32[16,6]{1,0:T(8,128)S(1)} %get-tuple-element.29.slots_ref, bf16[512,128]{1,0:T(8,128)(2,1)S(1)} %get-tuple-element.30.weights, ...), custom_call_target="tpu_custom_call" | custom-call | flops 671088640 | bytes 7340032 | tf_op jit(solution)/shard_map/spread/pallas_call | solution.py:159
  22.2 1.8 %collective-permute-start.7 = (bf16[8,128,128]{2,1,0:T(8,128)(2,1)S(1)}, bf16[8,128,128]{2,1,0:T(8,128)(2,1)S(1)}, u32[]{:S(2)}, u32[]{:S(2)}) collective-permute-start(bf16[8,128,128]{2,1,0:T(8,128)(2,1)S(1)} %get-tuple-element.36), channel_id=1, source_target_pairs={{0,4},{4,0},{8,12},{12,8},{16,20},{20,16},{24,28},{28,24},{1,5},{5... | collective-permute-start | bytes 786440 | tf_op jit(solution)/shard_map/ppermute | solution.py:21
  24.7 4.5 %collective-permute-start.9 = (bf16[8,128,128]{2,1,0:T(8,128)(2,1)S(1)}, bf16[8,128,128]{2,1,0:T(8,128)(2,1)S(1)}, u32[]{:S(2)}, u32[]{:S(2)}) collective-permute-start(bf16[8,128,128]{2,1,0:T(8,128)(2,1)S(1)} %get-tuple-element.38), channel_id=1, source_target_pairs={{0,8},{4,12},{8,0},{12,4},{16,24},{20,28},{24,16},{28,20},{1,9},{5... | collective-permute-start | bytes 786440 | tf_op jit(solution)/shard_map/ppermute | solution.py:21
  30.7 5.7 %collective-permute-done.9.apart = bf16[8,128,128]{2,1,0:T(8,128)(2,1)S(1)} collective-permute-done((bf16[8,128,128]{2,1,0:T(8,128)(2,1)S(1)}, bf16[8,128,128]{2,1,0:T(8,128)(2,1)S(1)}, u32[]{:S(2)}, u32[]{:S(2)}) %collective-permute-start.9) | collective-permute-done | bytes 262176 | tf_op jit(solution)/shard_map/ppermute | solution.py:21
  36.7 1.6 %collective-permute-start.16 = (bf16[1024,128]{1,0:T(8,128)(2,1)S(1)}, bf16[1024,128]{1,0:T(8,128)(2,1)S(1)}, u32[]{:S(2)}, u32[]{:S(2)}) collective-permute-start(bf16[1024,128]{1,0:T(8,128)(2,1)S(1)} %get-tuple-element.46.refs_4_), channel_id=1, source_target_pairs={{0,2},{1,3},{2,0},{3,1},{4,6},{5,7},{6,4},{7,5},{8,10},{9,11},{10,... | collective-permute-start | bytes 786440 | tf_op jit(solution)/shard_map/ppermute | solution.py:21
  38.8 5.9 %collective-permute-start.10 = (bf16[128,512]{1,0:T(8,128)(2,1)S(1)}, bf16[128,512]{1,0:T(8,128)(2,1)S(1)}, u32[]{:S(2)}, u32[]{:S(2)}) collective-permute-start(bf16[128,512]{1,0:T(8,128)(2,1)S(1)} %weight_term.2), channel_id=1, source_target_pairs={{0,4},{4,0},{8,12},{12,8},{16,20},{20,16},{24,28},{28,24},{1,5},{5... | collective-permute-start | bytes 393224 | tf_op jit(solution)/shard_map/ppermute | solution.py:21
  45.6 2.8 %collective-permute-done.11.refs_2_ = bf16[1024,128]{1,0:T(8,128)(2,1)S(1)} collective-permute-done((bf16[1024,128]{1,0:T(8,128)(2,1)S(1)}, bf16[1024,128]{1,0:T(8,128)(2,1)S(1)}, u32[]{:S(2)}, u32[]{:S(2)}) %collective-permute-start.11) | collective-permute-done | bytes 262176 | tf_op jit(solution)/shard_map/ppermute | solution.py:21
  48.5 7.0 %collective-permute-start.12 = (bf16[128,512]{1,0:T(8,128)(2,1)S(1)}, bf16[128,512]{1,0:T(8,128)(2,1)S(1)}, u32[]{:S(2)}, u32[]{:S(2)}) collective-permute-start(bf16[128,512]{1,0:T(8,128)(2,1)S(1)} %add_convert_fusion.3), channel_id=1, source_target_pairs={{0,16},{4,20},{8,24},{12,28},{16,0},{20,4},{24,8},{28,12},{1,17},{... | collective-permute-start | bytes 393224 | tf_op jit(solution)/shard_map/ppermute | solution.py:21
  56.3 1.6 %collective-permute-start.23 = (bf16[128,512]{1,0:T(8,128)(2,1)S(1)}, bf16[128,512]{1,0:T(8,128)(2,1)S(1)}, u32[]{:S(2)}, u32[]{:S(2)}) collective-permute-start(bf16[128,512]{1,0:T(8,128)(2,1)S(1)} %weight_term.3), channel_id=1, source_target_pairs={{0,4},{4,0},{8,12},{12,8},{16,20},{20,16},{24,28},{28,24},{1,5},{5... | collective-permute-start | bytes 393224 | tf_op jit(solution)/shard_map/ppermute | solution.py:21
  57.9 3.7 %spread.3 = (f32[16,128,128]{2,1,0:T(8,128)S(1)}, bf16[8,128,128]{2,1,0:T(8,128)(2,1)S(1)}, bf16[8,128,128]{2,1,0:T(8,128)(2,1)S(1)}, bf16[8,128,128]{2,1,0:T(8,128)(2,1)S(1)}, bf16[8,128,128]{2,1,0:T(8,128)(2,1)S(1)}) custom-call(s32[16,6]{1,0:T(8,128)S(1)} %get-tuple-element.29.slots_ref, bf16[512,128]{1,0:T(8,128)(2,1)S(1)} %get-tuple-element.45.weights, ...), custom_call_target="tpu_custom_call" | custom-call | flops 671088640 | bytes 7340032 | tf_op jit(solution)/shard_map/spread/pallas_call | solution.py:159
  62.5 4.0 %collective-permute-start.24 = (bf16[128,512]{1,0:T(8,128)(2,1)S(1)}, bf16[128,512]{1,0:T(8,128)(2,1)S(1)}, u32[]{:S(2)}, u32[]{:S(2)}) collective-permute-start(bf16[128,512]{1,0:T(8,128)(2,1)S(1)} %add_convert_fusion.1), channel_id=1, source_target_pairs={{0,16},{4,20},{8,24},{12,28},{16,0},{20,4},{24,8},{28,12},{1,17},{... | collective-permute-start | bytes 393224 | tf_op jit(solution)/shard_map/ppermute | solution.py:21
  68.0 11.2 %collective-permute-done.24 = bf16[128,512]{1,0:T(8,128)(2,1)S(1)} collective-permute-done((bf16[128,512]{1,0:T(8,128)(2,1)S(1)}, bf16[128,512]{1,0:T(8,128)(2,1)S(1)}, u32[]{:S(2)}, u32[]{:S(2)}) %collective-permute-start.24) | collective-permute-done | bytes 131104 | tf_op jit(solution)/shard_map/ppermute | solution.py:21
  79.3 2.1 %collective-permute-start.25 = (bf16[128,512]{1,0:T(8,128)(2,1)S(1)}, bf16[128,512]{1,0:T(8,128)(2,1)S(1)}, u32[]{:S(2)}, u32[]{:S(2)}) collective-permute-start(bf16[128,512]{1,0:T(8,128)(2,1)S(1)} %add_convert_fusion.refs_0_), channel_id=1, source_target_pairs={{0,8},{4,12},{8,0},{12,4},{16,24},{20,28},{24,16},{28,20},{1,9},{5... | collective-permute-start | bytes 393224 | tf_op jit(solution)/shard_map/ppermute | solution.py:21
  82.1 4.6 %collective-permute-done.22.apart = bf16[8,128,128]{2,1,0:T(8,128)(2,1)S(1)} collective-permute-done((bf16[8,128,128]{2,1,0:T(8,128)(2,1)S(1)}, bf16[8,128,128]{2,1,0:T(8,128)(2,1)S(1)}, u32[]{:S(2)}, u32[]{:S(2)}) %collective-permute-start.22) | collective-permute-done | bytes 262176 | tf_op jit(solution)/shard_map/ppermute | solution.py:21
  86.7 1.4 %collective-permute-done.25.refs_1_ = bf16[128,512]{1,0:T(8,128)(2,1)S(1)} collective-permute-done((bf16[128,512]{1,0:T(8,128)(2,1)S(1)}, bf16[128,512]{1,0:T(8,128)(2,1)S(1)}, u32[]{:S(2)}, u32[]{:S(2)}) %collective-permute-start.25) | collective-permute-done | bytes 131104 | tf_op jit(solution)/shard_map/ppermute | solution.py:21
  88.1 1.1 %join.3 = (f32[128,512]{1,0:T(8,128)}, bf16[2048,128]{1,0:T(8,128)(2,1)}) custom-call(f32[16,128,128]{2,1,0:T(8,128)S(1)} %get-tuple-element.49.own, bf16[8,128,128]{2,1,0:T(8,128)(2,1)S(1)} %collective-permute-done.19.next_over, bf16[8,128,128]{2,1,0:T(8,128)(2,1)S(1)} %collective-permute-done.20.across, ...), custom_call_target="tpu_custom_call" | custom-call | bytes 3145728 | tf_op jit(solution)/shard_map/join/pallas_call | solution.py:219
  (55 shorter events, 11.1 us)
Async XLA Ops:
  1.6 11.7 %collective-permute-start.1 = (bf16[1024,128]{1,0:T(8,128)(2,1)S(1)}, bf16[1024,128]{1,0:T(8,128)(2,1)S(1)}, u32[]{:S(2)}, u32[]{:S(2)}) collective-permute-start(bf16[1024,128]{1,0:T(8,128)(2,1)S(1)} %slice.6.refs_0_), channel_id=1, source_target_pairs={{0,2},{1,3},{2,0},{3,1},{4,6},{5,7},{6,4},{7,5},{8,10},{9,11},{10,... | collective-permute-start | bytes 786440 | tf_op jit(solution)/shard_map/ppermute | solution.py:21
  5.6 11.0 %collective-permute-start.4 = (bf16[1024,128]{1,0:T(8,128)(2,1)S(1)}, bf16[1024,128]{1,0:T(8,128)(2,1)S(1)}, u32[]{:S(2)}, u32[]{:S(2)}) collective-permute-start(bf16[1024,128]{1,0:T(8,128)(2,1)S(1)} %slice.8.refs_4_), channel_id=1, source_target_pairs={{0,2},{1,3},{2,0},{3,1},{4,6},{5,7},{6,4},{7,5},{8,10},{9,11},{10,... | collective-permute-start | bytes 786440 | tf_op jit(solution)/shard_map/ppermute | solution.py:21
  5.7 11.4 %collective-permute-start = (bf16[1024,128]{1,0:T(8,128)(2,1)S(1)}, bf16[1024,128]{1,0:T(8,128)(2,1)S(1)}, u32[]{:S(2)}, u32[]{:S(2)}) collective-permute-start(bf16[1024,128]{1,0:T(8,128)(2,1)S(1)} %slice.6.refs_0_), channel_id=1, source_target_pairs={{0,1},{1,0},{2,3},{3,2},{4,5},{5,4},{6,7},{7,6},{8,9},{9,8},{10,11... | collective-permute-start | bytes 786440 | tf_op jit(solution)/shard_map/ppermute | solution.py:21
  5.8 11.3 %collective-permute-start.3 = (bf16[1024,128]{1,0:T(8,128)(2,1)S(1)}, bf16[1024,128]{1,0:T(8,128)(2,1)S(1)}, u32[]{:S(2)}, u32[]{:S(2)}) collective-permute-start(bf16[1024,128]{1,0:T(8,128)(2,1)S(1)} %slice.8.refs_4_), channel_id=1, source_target_pairs={{0,1},{1,0},{2,3},{3,2},{4,5},{5,4},{6,7},{7,6},{8,9},{9,8},{10,11... | collective-permute-start | bytes 786440 | tf_op jit(solution)/shard_map/ppermute | solution.py:21
  22.2 8.5 %collective-permute-start.7 = (bf16[8,128,128]{2,1,0:T(8,128)(2,1)S(1)}, bf16[8,128,128]{2,1,0:T(8,128)(2,1)S(1)}, u32[]{:S(2)}, u32[]{:S(2)}) collective-permute-start(bf16[8,128,128]{2,1,0:T(8,128)(2,1)S(1)} %get-tuple-element.36), channel_id=1, source_target_pairs={{0,4},{4,0},{8,12},{12,8},{16,20},{20,16},{24,28},{28,24},{1,5},{5... | collective-permute-start | bytes 786440 | tf_op jit(solution)/shard_map/ppermute | solution.py:21
  24.0 6.6 %collective-permute-start.8 = (bf16[8,128,128]{2,1,0:T(8,128)(2,1)S(1)}, bf16[8,128,128]{2,1,0:T(8,128)(2,1)S(1)}, u32[]{:S(2)}, u32[]{:S(2)}) collective-permute-start(bf16[8,128,128]{2,1,0:T(8,128)(2,1)S(1)} %get-tuple-element.37), channel_id=1, source_target_pairs={{8,16},{12,20},{16,8},{20,12},{9,17},{13,21},{17,9},{21,13},{10,18... | collective-permute-start | bytes 786440 | tf_op jit(solution)/shard_map/ppermute | solution.py:21
  24.7 11.6 %collective-permute-start.9 = (bf16[8,128,128]{2,1,0:T(8,128)(2,1)S(1)}, bf16[8,128,128]{2,1,0:T(8,128)(2,1)S(1)}, u32[]{:S(2)}, u32[]{:S(2)}) collective-permute-start(bf16[8,128,128]{2,1,0:T(8,128)(2,1)S(1)} %get-tuple-element.38), channel_id=1, source_target_pairs={{0,8},{4,12},{8,0},{12,4},{16,24},{20,28},{24,16},{28,20},{1,9},{5... | collective-permute-start | bytes 786440 | tf_op jit(solution)/shard_map/ppermute | solution.py:21
  29.2 7.2 %collective-permute-start.6 = (bf16[8,128,128]{2,1,0:T(8,128)(2,1)S(1)}, bf16[8,128,128]{2,1,0:T(8,128)(2,1)S(1)}, u32[]{:S(2)}, u32[]{:S(2)}) collective-permute-start(bf16[8,128,128]{2,1,0:T(8,128)(2,1)S(1)} %get-tuple-element.33), channel_id=1, source_target_pairs={{4,8},{8,4},{12,16},{16,12},{20,24},{24,20},{5,9},{9,5},{13,17},{1... | collective-permute-start | bytes 786440 | tf_op jit(solution)/shard_map/ppermute | solution.py:21
  36.7 8.9 %collective-permute-start.16 = (bf16[1024,128]{1,0:T(8,128)(2,1)S(1)}, bf16[1024,128]{1,0:T(8,128)(2,1)S(1)}, u32[]{:S(2)}, u32[]{:S(2)}) collective-permute-start(bf16[1024,128]{1,0:T(8,128)(2,1)S(1)} %get-tuple-element.46.refs_4_), channel_id=1, source_target_pairs={{0,2},{1,3},{2,0},{3,1},{4,6},{5,7},{6,4},{7,5},{8,10},{9,11},{10,... | collective-permute-start | bytes 786440 | tf_op jit(solution)/shard_map/ppermute | solution.py:21
  38.3 10.2 %collective-permute-start.11 = (bf16[1024,128]{1,0:T(8,128)(2,1)S(1)}, bf16[1024,128]{1,0:T(8,128)(2,1)S(1)}, u32[]{:S(2)}, u32[]{:S(2)}) collective-permute-start(bf16[1024,128]{1,0:T(8,128)(2,1)S(1)} %get-tuple-element.42.refs_0_), channel_id=1, source_target_pairs={{0,2},{1,3},{2,0},{3,1},{4,6},{5,7},{6,4},{7,5},{8,10},{9,11},{10,... | collective-permute-start | bytes 786440 | tf_op jit(solution)/shard_map/ppermute | solution.py:21
  38.8 9.6 %collective-permute-start.10 = (bf16[128,512]{1,0:T(8,128)(2,1)S(1)}, bf16[128,512]{1,0:T(8,128)(2,1)S(1)}, u32[]{:S(2)}, u32[]{:S(2)}) collective-permute-start(bf16[128,512]{1,0:T(8,128)(2,1)S(1)} %weight_term.2), channel_id=1, source_target_pairs={{0,4},{4,0},{8,12},{12,8},{16,20},{20,16},{24,28},{28,24},{1,5},{5... | collective-permute-start | bytes 393224 | tf_op jit(solution)/shard_map/ppermute | solution.py:21
  44.7 10.8 %collective-permute-start.15 = (bf16[1024,128]{1,0:T(8,128)(2,1)S(1)}, bf16[1024,128]{1,0:T(8,128)(2,1)S(1)}, u32[]{:S(2)}, u32[]{:S(2)}) collective-permute-start(bf16[1024,128]{1,0:T(8,128)(2,1)S(1)} %get-tuple-element.46.refs_4_), channel_id=1, source_target_pairs={{0,1},{1,0},{2,3},{3,2},{4,5},{5,4},{6,7},{7,6},{8,9},{9,8},{10,11... | collective-permute-start | bytes 786440 | tf_op jit(solution)/shard_map/ppermute | solution.py:21
  44.7 10.8 %collective-permute-start.13 = (bf16[1024,128]{1,0:T(8,128)(2,1)S(1)}, bf16[1024,128]{1,0:T(8,128)(2,1)S(1)}, u32[]{:S(2)}, u32[]{:S(2)}) collective-permute-start(bf16[1024,128]{1,0:T(8,128)(2,1)S(1)} %get-tuple-element.42.refs_0_), channel_id=1, source_target_pairs={{0,1},{1,0},{2,3},{3,2},{4,5},{5,4},{6,7},{7,6},{8,9},{9,8},{10,11... | collective-permute-start | bytes 786440 | tf_op jit(solution)/shard_map/ppermute | solution.py:21
  45.6 9.9 %collective-permute-start.17 = (bf16[1024,128]{1,0:T(8,128)(2,1)S(1)}, bf16[1024,128]{1,0:T(8,128)(2,1)S(1)}, u32[]{:S(2)}, u32[]{:S(2)}) collective-permute-start(bf16[1024,128]{1,0:T(8,128)(2,1)S(1)} %collective-permute-done.16.refs_6_), channel_id=1, source_target_pairs={{0,1},{1,0},{2,3},{3,2},{4,5},{5,4},{6,7},{7,6},{8,9},{9,8},{10,11... | collective-permute-start | bytes 786440 | tf_op jit(solution)/shard_map/ppermute | solution.py:21
  48.4 7.1 %collective-permute-start.14 = (bf16[1024,128]{1,0:T(8,128)(2,1)S(1)}, bf16[1024,128]{1,0:T(8,128)(2,1)S(1)}, u32[]{:S(2)}, u32[]{:S(2)}) collective-permute-start(bf16[1024,128]{1,0:T(8,128)(2,1)S(1)} %collective-permute-done.11.refs_2_), channel_id=1, source_target_pairs={{0,1},{1,0},{2,3},{3,2},{4,5},{5,4},{6,7},{7,6},{8,9},{9,8},{10,11... | collective-permute-start | bytes 786440 | tf_op jit(solution)/shard_map/ppermute | solution.py:21
  48.5 14.0 %collective-permute-start.12 = (bf16[128,512]{1,0:T(8,128)(2,1)S(1)}, bf16[128,512]{1,0:T(8,128)(2,1)S(1)}, u32[]{:S(2)}, u32[]{:S(2)}) collective-permute-start(bf16[128,512]{1,0:T(8,128)(2,1)S(1)} %add_convert_fusion.3), channel_id=1, source_target_pairs={{0,16},{4,20},{8,24},{12,28},{16,0},{20,4},{24,8},{28,12},{1,17},{... | collective-permute-start | bytes 393224 | tf_op jit(solution)/shard_map/ppermute | solution.py:21
  56.3 6.2 %collective-permute-start.23 = (bf16[128,512]{1,0:T(8,128)(2,1)S(1)}, bf16[128,512]{1,0:T(8,128)(2,1)S(1)}, u32[]{:S(2)}, u32[]{:S(2)}) collective-permute-start(bf16[128,512]{1,0:T(8,128)(2,1)S(1)} %weight_term.3), channel_id=1, source_target_pairs={{0,4},{4,0},{8,12},{12,8},{16,20},{20,16},{24,28},{28,24},{1,5},{5... | collective-permute-start | bytes 393224 | tf_op jit(solution)/shard_map/ppermute | solution.py:21
  61.6 25.1 %collective-permute-start.19 = (bf16[8,128,128]{2,1,0:T(8,128)(2,1)S(1)}, bf16[8,128,128]{2,1,0:T(8,128)(2,1)S(1)}, u32[]{:S(2)}, u32[]{:S(2)}) collective-permute-start(bf16[8,128,128]{2,1,0:T(8,128)(2,1)S(1)} %get-tuple-element.47), channel_id=1, source_target_pairs={{4,8},{8,4},{12,16},{16,12},{20,24},{24,20},{5,9},{9,5},{13,17},{1... | collective-permute-start | bytes 786440 | tf_op jit(solution)/shard_map/ppermute | solution.py:21
  62.5 16.7 %collective-permute-start.24 = (bf16[128,512]{1,0:T(8,128)(2,1)S(1)}, bf16[128,512]{1,0:T(8,128)(2,1)S(1)}, u32[]{:S(2)}, u32[]{:S(2)}) collective-permute-start(bf16[128,512]{1,0:T(8,128)(2,1)S(1)} %add_convert_fusion.1), channel_id=1, source_target_pairs={{0,16},{4,20},{8,24},{12,28},{16,0},{20,4},{24,8},{28,12},{1,17},{... | collective-permute-start | bytes 393224 | tf_op jit(solution)/shard_map/ppermute | solution.py:21
  66.6 12.7 %collective-permute-start.18 = (bf16[128,512]{1,0:T(8,128)(2,1)S(1)}, bf16[128,512]{1,0:T(8,128)(2,1)S(1)}, u32[]{:S(2)}, u32[]{:S(2)}) collective-permute-start(bf16[128,512]{1,0:T(8,128)(2,1)S(1)} %add_convert_fusion.2), channel_id=1, source_target_pairs={{0,8},{4,12},{8,0},{12,4},{16,24},{20,28},{24,16},{28,20},{1,9},{5... | collective-permute-start | bytes 393224 | tf_op jit(solution)/shard_map/ppermute | solution.py:21
  67.1 15.0 %collective-permute-start.20 = (bf16[8,128,128]{2,1,0:T(8,128)(2,1)S(1)}, bf16[8,128,128]{2,1,0:T(8,128)(2,1)S(1)}, u32[]{:S(2)}, u32[]{:S(2)}) collective-permute-start(bf16[8,128,128]{2,1,0:T(8,128)(2,1)S(1)} %get-tuple-element.50), channel_id=1, source_target_pairs={{0,4},{4,0},{8,12},{12,8},{16,20},{20,16},{24,28},{28,24},{1,5},{5... | collective-permute-start | bytes 786440 | tf_op jit(solution)/shard_map/ppermute | solution.py:21
  67.3 14.8 %collective-permute-start.21 = (bf16[8,128,128]{2,1,0:T(8,128)(2,1)S(1)}, bf16[8,128,128]{2,1,0:T(8,128)(2,1)S(1)}, u32[]{:S(2)}, u32[]{:S(2)}) collective-permute-start(bf16[8,128,128]{2,1,0:T(8,128)(2,1)S(1)} %get-tuple-element.51), channel_id=1, source_target_pairs={{8,16},{12,20},{16,8},{20,12},{9,17},{13,21},{17,9},{21,13},{10,18... | collective-permute-start | bytes 786440 | tf_op jit(solution)/shard_map/ppermute | solution.py:21
  79.2 7.5 %collective-permute-start.22 = (bf16[8,128,128]{2,1,0:T(8,128)(2,1)S(1)}, bf16[8,128,128]{2,1,0:T(8,128)(2,1)S(1)}, u32[]{:S(2)}, u32[]{:S(2)}) collective-permute-start(bf16[8,128,128]{2,1,0:T(8,128)(2,1)S(1)} %get-tuple-element.52), channel_id=1, source_target_pairs={{0,8},{4,12},{8,0},{12,4},{16,24},{20,28},{24,16},{28,20},{1,9},{5... | collective-permute-start | bytes 786440 | tf_op jit(solution)/shard_map/ppermute | solution.py:21
  79.3 8.8 %collective-permute-start.25 = (bf16[128,512]{1,0:T(8,128)(2,1)S(1)}, bf16[128,512]{1,0:T(8,128)(2,1)S(1)}, u32[]{:S(2)}, u32[]{:S(2)}) collective-permute-start(bf16[128,512]{1,0:T(8,128)(2,1)S(1)} %add_convert_fusion.refs_0_), channel_id=1, source_target_pairs={{0,8},{4,12},{8,0},{12,4},{16,24},{20,28},{24,16},{28,20},{1,9},{5... | collective-permute-start | bytes 393224 | tf_op jit(solution)/shard_map/ppermute | solution.py:21
  (8 other events, 75.0 us)

commit v3 on v2

v3 whole, which is shorter than its diff:
```python
import functools
import math

import jax
import jax.numpy as jnp
from jax import lax
from jax.experimental import pallas as pl
from jax.experimental.pallas import tpu as pltpu
from jax.sharding import PartitionSpec as P


VMEM = pl.BlockSpec(memory_space=pltpu.VMEM)
ANY = pl.BlockSpec(memory_space=pl.ANY)
SMEM = pl.BlockSpec(memory_space=pltpu.SMEM)


def exchanged(value, axis, partner):
    count = lax.axis_size(axis)
    pairs = [(s, partner(s)) for s in range(count) if 0 <= partner(s) < count]
    return lax.ppermute(value, axis, pairs)


SWAPS = [
    lambda s: ((s + 1) ^ 1) - 1,
    lambda s: s ^ 1,
    lambda s: ((s + 2) ^ 2) - 2,
    lambda s: s ^ 2,
]


def after(value, *earlier):
    return lax.optimization_barrier((value, *earlier))[0]


def gather_pieces(chunks, axis, earlier=()):
    held = [{0: chunk} for chunk in chunks]
    mask = lax.axis_size(axis) // 2
    first = True
    while mask:
        moves = [list(pieces) for pieces in held]
        for step in range(len(moves[0])):
            for c, (pieces, move) in enumerate(zip(held, moves)):
                m = move[step]
                got = exchanged(pieces[m], axis, lambda s, mask=mask: s ^ mask)
                pieces[m | mask] = after(got, *earlier) if first and earlier and c == 0 else got
        first = False
        mask //= 2
    return [[pieces[m] for m in sorted(pieces)] for pieces in held]


def prepare_kernel(targets_hbm, blocks_hbm, *refs):
    count = (len(refs) - 5) // 2
    weight_refs, slots_ref, blocks_ref = refs[:count], refs[count], refs[count + 1]
    outs, (targets_ref, target_sem, block_sem) = refs[count + 2 : -3], refs[-3:]
    block_copy = pltpu.make_async_copy(blocks_hbm, blocks_ref, block_sem)
    target_copy = pltpu.make_async_copy(targets_hbm, targets_ref, target_sem)
    block_copy.start()
    target_copy.start()
    place = lax.axis_index("feat")
    for weight_ref, out in zip(weight_refs, outs):
        width, total = weight_ref.shape
        for m in range(total // width):
            start = pl.multiple_of((place ^ m) * width, width)
            out[m * width : (m + 1) * width, :] = weight_ref[:, pl.ds(start, width)].T
    tile_count, entries = slots_ref.shape
    half = tile_count // 2
    index = lax.axis_index("dom")
    odd, upper = index & 1, (index & 2) // 2
    target_copy.wait()

    def body(r, carry):
        for k in range(entries):
            target = targets_ref[r, k]
            part = lax.div(target, jnp.int32(tile_count))
            offset = part - index
            within = target - part * tile_count
            up = offset > 0
            near = jnp.where(up, 1 - odd, odd)
            far = 2 + jnp.where(up, 1 - upper, upper)
            swap = jnp.where(jnp.abs(offset) == 1, near, far)
            outer = tile_count + swap * half + jnp.where(up, within, within - half)
            slots_ref[r, k] = jnp.where(offset == 0, within, outer)
        return carry

    lax.fori_loop(0, tile_count, body, 0)
    block_copy.wait()


def prepare(targets, blocks, weights):
    outs = [
        jax.ShapeDtypeStruct(targets.shape, jnp.int32),
        jax.ShapeDtypeStruct(blocks.shape, blocks.dtype),
    ]
    outs += [jax.ShapeDtypeStruct(w.shape[::-1], w.dtype) for w in weights]
    return pl.pallas_call(
        prepare_kernel,
        out_shape=outs,
        in_specs=[ANY, pl.BlockSpec(memory_space=pltpu.HBM)] + [VMEM] * len(weights),
        out_specs=[SMEM] + [VMEM] * (len(outs) - 1),
        scratch_shapes=[
            pltpu.SMEM(targets.shape, jnp.int32),
            pltpu.SemaphoreType.DMA,
            pltpu.SemaphoreType.DMA,
        ],
        compiler_params=pltpu.CompilerParams(vmem_limit_bytes=8 << 20),
        cost_estimate=pl.CostEstimate(flops=0, bytes_accessed=4 * blocks.size, transcendentals=0),
        name="prepare",
    )(targets, blocks, *weights)


def unrolling(count):
    return max(n for n in range(1, 7) if count % n == 0)


def spread_kernel(first, tiles, slots_ref, weights, blocks, *refs):
    last = tiles[1] == blocks.shape[0]
    width = weights.shape[1]
    pieces = weights.shape[0] // width
    piece_refs, refs = refs[:pieces], refs[pieces:]
    total, sends, values = refs[0 if first else 1], refs[1 if first else 2 : -1], refs[-1]
    tile_count, count, size, _ = blocks.shape
    if first:
        total[...] = jnp.zeros_like(total)
    group = 2
    for i in range((tiles[1] - tiles[0]) // group):
        rows = slice(i * group * size, (i + 1) * group * size)
        left = jnp.concatenate([piece[rows, :] for piece in piece_refs], axis=1)
        value = jnp.dot(left, weights[...], preferred_element_type=jnp.float32)
        value = value.astype(values.dtype).reshape(group, size, width)
        values[i * group : (i + 1) * group] = value

    def body(i, carry):
        value = values[i]
        r = tiles[0] + i
        for k in range(count):
            slot = slots_ref[r, k]
            total[slot] += jnp.dot(blocks[r, k], value, preferred_element_type=jnp.float32)
        return carry

    lax.fori_loop(0, tiles[1] - tiles[0], body, 0, unroll=unrolling(tiles[1] - tiles[0]))
    half = tile_count // 2
    for n, send in enumerate(sends if last else ()):
        start = tile_count + n * half
        send[...] = total[start : start + half].astype(send.dtype)


def spread(tiles, pieces, weight, blocks, slots, total=None):
    tile_count, count, size, _ = blocks.shape
    half = tile_count // 2
    width = weight.shape[1]
    held = tiles[1] - tiles[0]
    outs = [
        jax.ShapeDtypeStruct((tile_count + len(SWAPS) * half, size, width), jnp.float32)
    ]
    if tiles[1] == tile_count:
        outs += [jax.ShapeDtypeStruct((half, size, width), jnp.bfloat16)] * len(SWAPS)
    args = [slots, weight, blocks, *pieces]
    aliases = {}
    if total is not None:
        aliases[len(args)] = 0
        args.append(total)
    return pl.pallas_call(
        functools.partial(spread_kernel, total is None, tiles),
        out_shape=outs,
        in_specs=[SMEM] + [VMEM] * (len(args) - 1),
        out_specs=[VMEM] * len(outs),
        input_output_aliases=aliases,
        scratch_shapes=[pltpu.VMEM((held, size, width), jnp.bfloat16)],
        cost_estimate=pl.CostEstimate(
            flops=2 * held * size * width * (count * size + weight.shape[0]),
            bytes_accessed=held * size * width * 2 * (count + 8),
            transcendentals=0,
        ),
        compiler_params=pltpu.CompilerParams(vmem_limit_bytes=16 << 20),
        name="spread",
    )(*args)


def join_kernel(masked, tile_count, own, next_over, across, next_apart, apart, *refs):
    size = own.shape[1]
    half = tile_count // 2
    index = lax.axis_index("dom")
    odd, upper = (index & 1) == 1, (index & 2) == 2
    if masked:
        mask, *outs = refs
    else:
        outs = refs
    places = [(out, i) for out in outs for i in range(out.shape[0] // size)]

    def write(tile, near, far):
        total = own[tile]
        total += near[tile % half].astype(jnp.float32) + far[tile % half].astype(jnp.float32)
        if masked:
            total = jnp.where(mask[tile * size : (tile + 1) * size, :] > 0, total, 0.0)
        out, i = places[tile]
        out[i * size : (i + 1) * size, :] = total.astype(out.dtype)

    for is_odd in (False, True):
        for is_upper in (False, True):

            @pl.when((odd == is_odd) & (upper == is_upper))
            def _(is_odd=is_odd, is_upper=is_upper):
                near = [across, next_over] if is_odd else [next_over, across]
                far = [apart, next_apart] if is_upper else [next_apart, apart]
                for tile in range(tile_count):
                    write(tile, near[tile // half], far[tile // half])


def boundary(own, sends):
    got = [exchanged(send, "dom", swap) for send, swap in zip(sends, SWAPS)]
    return own, *got


def join(sums, outs, mask=None):
    masked = mask is not None
    args = [*sums, mask] if masked else list(sums)
    return pl.pallas_call(
        functools.partial(join_kernel, masked, 2 * sums[1].shape[0]),
        out_shape=outs,
        in_specs=[VMEM] * len(args),
        out_specs=[VMEM] * len(outs),
        compiler_params=pltpu.CompilerParams(vmem_limit_bytes=8 << 20),
        cost_estimate=pl.CostEstimate(
            flops=0, bytes_accessed=12 * sums[1].size, transcendentals=0
        ),
        name="join",
    )(*args)


def term(left, right):
    return lax.dot_general(left, right, (((0,), (0,)), ((), ())), preferred_element_type=jnp.float32)


def second_kernel(scale, cuts, agg, *refs):
    *chunks, out = refs
    count = len(chunks) // len(cuts)
    for m in range(count):
        total = None
        for c, (first, last) in enumerate(cuts):
            part = term(agg[first:last, :], chunks[c * count + m][...])
            total = part if total is None else total + part
        out[m] = (total * scale).astype(out.dtype)


def first_kernel(scale, cuts, seconds, *refs):
    count = seconds.shape[0]
    pieces, chunks, (keep, send) = refs[:count], refs[count:-2], refs[-2:]
    odd = (lax.axis_index("dom") & 1) == 1
    for m in range(count):
        total = None
        for (first, last), chunk in zip(cuts, chunks):
            part = term(pieces[m][first:last, :], chunk[...])
            total = part if total is None else total + part
        total = (total * scale).astype(send.dtype)
        keep[m] = jnp.where(odd, seconds[m], total)
        send[m] = jnp.where(odd, total, seconds[m])


def parted_kernel(kept, got, second_out, *blocks):
    odd = (lax.axis_index("dom") & 1) == 1
    place = lax.axis_index("feat")
    width = kept.shape[1]
    for m, block in enumerate(blocks):
        block[...] = jnp.where(odd, got[m], kept[m])
        columns = pl.ds(pl.multiple_of((place ^ m) * width, width), width)
        second_out[:, columns] = jnp.where(odd, kept[m], got[m]).astype(second_out.dtype)


def placed_kernel(*refs):
    *blocks, out = refs
    place = lax.axis_index("feat")
    width = out.shape[0]
    for m, block in enumerate(blocks):
        columns = pl.ds(pl.multiple_of((place ^ m) * width, width), width)
        out[:, columns] = block[...].astype(out.dtype)


def small_call(kernel, outs, args, flops=0):
    return pl.pallas_call(
        kernel,
        out_shape=outs,
        in_specs=[VMEM] * len(args),
        out_specs=jax.tree.map(lambda _: VMEM, outs),
        cost_estimate=pl.CostEstimate(
            flops=flops, bytes_accessed=sum(2 * a.size for a in args), transcendentals=0
        ),
        compiler_params=pltpu.CompilerParams(vmem_limit_bytes=8 << 20),
    )(*args)


def added(value, other):
    return (value.astype(jnp.float32) + other.astype(jnp.float32)).astype(jnp.bfloat16)


def dom_sums(keep, send):
    value = added(keep, exchanged(send, "dom", lambda s: s ^ 1))
    mask = lax.axis_size("dom") // 2
    while mask > 1:
        other = exchanged(value, "dom", lambda s, mask=mask: s ^ mask)
        value = added(value, other)
        mask //= 2
    return value, exchanged(value, "dom", lambda s: s ^ 1)


def shards(grad_pre2, aggregated2, weight2, pre1, aggregated1, weight1, blocks, targets):
    nodes, width = grad_pre2.shape
    scale = 1.0 / math.sqrt(nodes * lax.axis_size("dom"))
    tile_count, _, size, _ = blocks.shape
    cut = tile_count * 5 // 8
    tiles = [(0, cut), (cut, tile_count)]
    cuts = [(t[0] * size, t[1] * size) for t in tiles]
    parts = [jax.ShapeDtypeStruct((r[1] - r[0], width), jnp.bfloat16) for r in cuts]
    slots, blocks, weight2, weight1 = prepare(targets, blocks, [weight2, weight1])

    chunks = [grad_pre2[: cuts[0][1]], lax.optimization_barrier(grad_pre2)[cuts[0][1] :]]
    gathered = gather_pieces(chunks, "feat", [weight2])
    count = len(gathered[0])
    flops = 2 * nodes * count * width**2
    grads = jax.ShapeDtypeStruct((count, width, width), jnp.bfloat16)
    wide = jax.ShapeDtypeStruct((width, count * width), jnp.float32)
    own, *sends = layer(tiles, gathered, weight2, blocks, slots)
    sums = boundary(own, sends)
    (held,) = gather_pieces([aggregated1], "feat")
    seconds = small_call(
        functools.partial(second_kernel, scale, cuts),
        grads,
        [after(aggregated2, sends[0]), *gathered[0], *gathered[1]],
        flops,
    )
    grad_pre1 = join(sums, parts, mask=pre1)

    gathered = gather_pieces(grad_pre1, "feat")
    keep, send = small_call(
        functools.partial(first_kernel, scale, cuts),
        [grads, grads],
        [seconds, *held, *grad_pre1],
        flops,
    )
    kept, got = dom_sums(keep, send)
    own, *sends = layer(tiles, gathered, weight1, blocks, slots)
    sums = boundary(own, sends)
    block = jax.ShapeDtypeStruct((width, width), jnp.bfloat16)
    second, *firsts = small_call(parted_kernel, [wide, *[block] * count], [kept, got])
    firsts = [firsts[0]] + [
        exchanged(firsts[m], "feat", lambda s, m=m: s ^ m) for m in range(1, count)
    ]
    first = small_call(placed_kernel, wide, firsts)
    (grad_input,) = join(sums, [jax.ShapeDtypeStruct((nodes, width), jnp.bfloat16)])
    return (second, first, grad_input)


def layer(tiles, gathered, weight, blocks, slots):
    total = None
    for part, pieces in zip(tiles, gathered):
        total, *sends = spread(part, pieces, weight, blocks, slots, total)
    return total, *sends


def solution(mesh):
    in_specs = (
        P("dom", "feat"),
        P("dom", "feat"),
        P("feat", None),
        P("dom", "feat"),
        P("dom", "feat"),
        P("feat", None),
        P("dom", None, None, None),
        P("dom", None),
    )
    out_specs = (P("feat", None), P("feat", None), P("dom", "feat"))
    return jax.shard_map(shards, mesh=mesh, in_specs=in_specs, out_specs=out_specs, check_vma=False)
```

time: 89.5 us -> 101 us (1.13)
  waiting for transfers between devices: 31.1 us -> 40.8 us
  starting transfers between devices: 37.1 us -> 38.6 us
  Pallas kernels: 12.9 us -> 14.2 us
    ppermute x26 -> x30, waiting for transfers between devices: 31.1 us -> 40.8 us  [exchanged(): return lax.ppermute(value, axis, pairs)]
    ppermute x26 -> x30, starting transfers between devices: 37.1 us -> 38.6 us  [exchanged(): return lax.ppermute(value, axis, pairs)]
    pallas_call x6 -> x10, Pallas kernels: 10.4 us -> 11.7 us  [the longest x4 7.3 us: spread(): pl.pallas_call(functools.partial(spread_kernel, total is None, tiles), ou...]
  transfers between devices with their start and end apart: 26 -> 30, of which waited for: 10 -> 9; matrix products, arithmetic and copies ran while one was open for 3% -> 2% of each run, Pallas kernels for 9% -> 12%
where the time goes in v3:
time: 101 us
  waiting for transfers between devices  40.8 us (40%)
  starting transfers between devices  38.6 us (38%)
  Pallas kernels  14.2 us (14%)
  local copies, waits for them, and re-layouts  6.41 us (6%)
    ppermute x30, waiting for transfers between devices, exchanged(): return lax.ppermute(value, axis, pairs)  40.8 us
    ppermute x30, starting transfers between devices, exchanged(): return lax.ppermute(value, axis, pairs)  38.6 us
    pallas_call x4, Pallas kernels, spread(): pl.pallas_call(functools.partial(spread_kernel, total is None, tiles), ou...  7.3 us
    unnamed x13, local copies, waits for them, and re-layouts  4.48 us
    pallas_call x4, Pallas kernels, small_call(): pl.pallas_call(kernel, out_shape=outs, in_specs=[VMEM] * len(args), out_s...  3.06 us
    pallas_call x1, Pallas kernels, prepare(): pl.pallas_call(prepare_kernel, out_shape=outs, in_specs=[ANY, pl.BlockSpe...  2.52 us
  transfers between devices with their start and end apart: 30, of which 9 were waited for; matrix products, arithmetic and copies ran while one was open for 2% of the time, Pallas kernels for 12%

profile of v3, /device:TPU:0, one launch (start us, length us, event | category | flops | bytes accessed | tf_op | source)
XLA Modules:
  0.0 101.1 jit_solution(9499031223343733295)
XLA Ops:
  1.6 3.0 %collective-permute-start.4 = (bf16[1280,128]{1,0:T(8,128)(2,1)S(1)}, bf16[1280,128]{1,0:T(8,128)(2,1)S(1)}, u32[]{:S(2)}, u32[]{:S(2)}) collective-permute-start(bf16[1280,128]{1,0:T(8,128)(2,1)S(1)} %slice.7.refs_0_), channel_id=1, source_target_pairs={{0,2},{1,3},{2,0},{3,1},{4,6},{5,7},{6,4},{7,5},{8,10},{9,11},{10,... | collective-permute-start | bytes 983048 | tf_op jit(solution)/shard_map/ppermute | solution.py:20
  5.7 2.0 %collective-permute-start.1 = (bf16[768,128]{1,0:T(8,128)(2,1)S(1)}, bf16[768,128]{1,0:T(8,128)(2,1)S(1)}, u32[]{:S(2)}, u32[]{:S(2)}) collective-permute-start(bf16[768,128]{1,0:T(8,128)(2,1)S(1)} %slice.8.refs_0_.refs_4_), channel_id=1, source_target_pairs={{0,2},{1,3},{2,0},{3,1},{4,6},{5,7},{6,4},{7,5},{8,10},{9,11},{10,... | collective-permute-start | bytes 589832 | tf_op jit(solution)/shard_map/ppermute | solution.py:20
  8.5 1.9 %copy-done = bf16[16,6,128,128]{3,2,1,0:T(8,128)(2,1)S(1)} copy-done((bf16[16,6,128,128]{3,2,1,0:T(8,128)(2,1)S(1)}, bf16[16,6,128,128]{3,2,1,0:T(8,128)(2,1)}, u32[]{:S(2)}) %copy-start) | copy-done | bytes 3145752
  12.2 2.5 %prepare.1 = (s32[16,6]{1,0:T(8,128)S(1)}, bf16[16,6,128,128]{3,2,1,0:T(8,128)(2,1)S(1)}, bf16[512,128]{1,0:T(8,128)(2,1)S(1)}, bf16[512,128]{1,0:T(8,128)(2,1)S(1)}) custom-call(s32[16,6]{1,0:T(8,128)S(1)} %copy.13.targets_hbm, bf16[16,6,128,128]{3,2,1,0:T(8,128)(2,1)S(1)} %copy-done, bf16[128,512]{1,0:T(8,128)(2,1)S(1)} %copy-done.4, ...), custom_call_target="tpu_custom_call" | custom-call | bytes 6291456 | tf_op jit(solution)/shard_map/prepare/pallas_call | solution.py:95
  15.4 12.5 %collective-permute-done.1.refs_2_.refs_6_ = bf16[768,128]{1,0:T(8,128)(2,1)S(1)} collective-permute-done((bf16[768,128]{1,0:T(8,128)(2,1)S(1)}, bf16[768,128]{1,0:T(8,128)(2,1)S(1)}, u32[]{:S(2)}, u32[]{:S(2)}) %collective-permute-start.1) | collective-permute-done | bytes 196640 | tf_op jit(solution)/shard_map/ppermute | solution.py:20
  27.8 2.2 %spread.4.refs_4_ = f32[48,128,128]{2,1,0:T(8,128)S(1)} custom-call(s32[16,6]{1,0:T(8,128)S(1)} %get-tuple-element.28.slots_ref, bf16[512,128]{1,0:T(8,128)(2,1)S(1)} %get-tuple-element.29.weights, bf16[16,6,128,128]{3,2,1,0:T(8,128)(2,1)S(1)} %get-tuple-element.30.blocks, bf16[1280,128]{1,0:T(8,128)(2,1)S(1)} %slice.7.refs_0_, ...), custom_call_target="tpu_custom_call" | custom-call | flops 419430400 | bytes 4587520 | tf_op jit(solution)/shard_map/spread/pallas_call | solution.py:162
  30.1 1.5 %spread.5 = (f32[48,128,128]{2,1,0:T(8,128)S(1)}, bf16[8,128,128]{2,1,0:T(8,128)(2,1)S(1)}, bf16[8,128,128]{2,1,0:T(8,128)(2,1)S(1)}, bf16[8,128,128]{2,1,0:T(8,128)(2,1)S(1)}, bf16[8,128,128]{2,1,0:T(8,128)(2,1)S(1)}) custom-call(s32[16,6]{1,0:T(8,128)S(1)} %get-tuple-element.28.slots_ref, ...), custom_call_target="tpu_custom_call", output_to_operand_aliasing={{0}: (7, {})} | custom-call | flops 251658240 | bytes 2752512 | tf_op jit(solution)/shard_map/spread/pallas_call | solution.py:162
  32.9 4.4 %collective-permute-start.10 = (bf16[8,128,128]{2,1,0:T(8,128)(2,1)S(1)}, bf16[8,128,128]{2,1,0:T(8,128)(2,1)S(1)}, u32[]{:S(2)}, u32[]{:S(2)}) collective-permute-start(bf16[8,128,128]{2,1,0:T(8,128)(2,1)S(1)} %get-tuple-element.35), channel_id=1, source_target_pairs={{0,4},{4,0},{8,12},{12,8},{16,20},{20,16},{24,28},{28,24},{1,5},{5... | collective-permute-start | bytes 786440 | tf_op jit(solution)/shard_map/ppermute | solution.py:20
  38.0 7.0 %collective-permute-start.12 = (bf16[8,128,128]{2,1,0:T(8,128)(2,1)S(1)}, bf16[8,128,128]{2,1,0:T(8,128)(2,1)S(1)}, u32[]{:S(2)}, u32[]{:S(2)}) collective-permute-start(bf16[8,128,128]{2,1,0:T(8,128)(2,1)S(1)} %get-tuple-element.37), channel_id=1, source_target_pairs={{0,8},{4,12},{8,0},{12,4},{16,24},{20,28},{24,16},{28,20},{1,9},{5... | collective-permute-start | bytes 786440 | tf_op jit(solution)/shard_map/ppermute | solution.py:20
  45.8 2.2 %collective-permute-done.10.across = bf16[8,128,128]{2,1,0:T(8,128)(2,1)S(1)} collective-permute-done((bf16[8,128,128]{2,1,0:T(8,128)(2,1)S(1)}, bf16[8,128,128]{2,1,0:T(8,128)(2,1)S(1)}, u32[]{:S(2)}, u32[]{:S(2)}) %collective-permute-start.10) | collective-permute-done | bytes 262176 | tf_op jit(solution)/shard_map/ppermute | solution.py:20
  48.0 3.1 %collective-permute-done.12.apart = bf16[8,128,128]{2,1,0:T(8,128)(2,1)S(1)} collective-permute-done((bf16[8,128,128]{2,1,0:T(8,128)(2,1)S(1)}, bf16[8,128,128]{2,1,0:T(8,128)(2,1)S(1)}, u32[]{:S(2)}, u32[]{:S(2)}) %collective-permute-start.12) | collective-permute-done | bytes 262176 | tf_op jit(solution)/shard_map/ppermute | solution.py:20
  52.2 1.7 %collective-permute-start.13 = (bf16[4,128,128]{2,1,0:T(8,128)(2,1)S(1)}, bf16[4,128,128]{2,1,0:T(8,128)(2,1)S(1)}, u32[]{:S(2)}, u32[]{:S(2)}) collective-permute-start(bf16[4,128,128]{2,1,0:T(8,128)(2,1)S(1)} %get-tuple-element.41), channel_id=1, source_target_pairs={{0,4},{4,0},{8,12},{12,8},{16,20},{20,16},{24,28},{28,24},{1,5},{5... | collective-permute-start | bytes 393224 | tf_op jit(solution)/shard_map/ppermute | solution.py:20
  54.0 1.5 %collective-permute-start.21 = (bf16[768,128]{1,0:T(8,128)(2,1)S(1)}, bf16[768,128]{1,0:T(8,128)(2,1)S(1)}, u32[]{:S(2)}, u32[]{:S(2)}) collective-permute-start(bf16[768,128]{1,0:T(8,128)(2,1)S(1)} %get-tuple-element.39.refs_5_.refs_0_), channel_id=1, source_target_pairs={{0,2},{1,3},{2,0},{3,1},{4,6},{5,7},{6,4},{7,5},{8,10},{9,11},{10,... | collective-permute-start | bytes 589832 | tf_op jit(solution)/shard_map/ppermute | solution.py:20
  57.3 2.8 %collective-permute-start.14 = (bf16[4,128,128]{2,1,0:T(8,128)(2,1)S(1)}, bf16[4,128,128]{2,1,0:T(8,128)(2,1)S(1)}, u32[]{:S(2)}, u32[]{:S(2)}) collective-permute-start(bf16[4,128,128]{2,1,0:T(8,128)(2,1)S(1)} %add_convert_fusion.2), channel_id=1, source_target_pairs={{0,16},{4,20},{8,24},{12,28},{16,0},{20,4},{24,8},{28,12},{1,17},{... | collective-permute-start | bytes 393224 | tf_op jit(solution)/shard_map/ppermute | solution.py:20
  60.1 6.1 %collective-permute-done.24.refs_2_ = bf16[1280,128]{1,0:T(8,128)(2,1)S(1)} collective-permute-done((bf16[1280,128]{1,0:T(8,128)(2,1)S(1)}, bf16[1280,128]{1,0:T(8,128)(2,1)S(1)}, u32[]{:S(2)}, u32[]{:S(2)}) %collective-permute-start.24) | collective-permute-done | bytes 327712 | tf_op jit(solution)/shard_map/ppermute | solution.py:20
  66.8 1.3 %collective-permute-start.15 = (bf16[4,128,128]{2,1,0:T(8,128)(2,1)S(1)}, bf16[4,128,128]{2,1,0:T(8,128)(2,1)S(1)}, u32[]{:S(2)}, u32[]{:S(2)}) collective-permute-start(bf16[4,128,128]{2,1,0:T(8,128)(2,1)S(1)} %add_convert_fusion.1), channel_id=1, source_target_pairs={{0,8},{4,12},{8,0},{12,4},{16,24},{20,28},{24,16},{28,20},{1,9},{5... | collective-permute-start | bytes 393224 | tf_op jit(solution)/shard_map/ppermute | solution.py:20
  68.1 2.2 %spread.6.refs_4_ = f32[48,128,128]{2,1,0:T(8,128)S(1)} custom-call(s32[16,6]{1,0:T(8,128)S(1)} %get-tuple-element.28.slots_ref, bf16[512,128]{1,0:T(8,128)(2,1)S(1)} %get-tuple-element.47.weights, bf16[16,6,128,128]{3,2,1,0:T(8,128)(2,1)S(1)} %get-tuple-element.30.blocks, bf16[1280,128]{1,0:T(8,128)(2,1)S(1)} %get-tuple-element.38.refs_4_.refs_0_, ...), custom_call_target="tpu_custom_call" | custom-call | flops 419430400 | bytes 4587520 | tf_op jit(solution)/shard_map/spread/pallas_call | solution.py:162
  70.3 1.5 %spread.7 = (f32[48,128,128]{2,1,0:T(8,128)S(1)}, bf16[8,128,128]{2,1,0:T(8,128)(2,1)S(1)}, bf16[8,128,128]{2,1,0:T(8,128)(2,1)S(1)}, bf16[8,128,128]{2,1,0:T(8,128)(2,1)S(1)}, bf16[8,128,128]{2,1,0:T(8,128)(2,1)S(1)}) custom-call(s32[16,6]{1,0:T(8,128)S(1)} %get-tuple-element.28.slots_ref, ...), custom_call_target="tpu_custom_call", output_to_operand_aliasing={{0}: (7, {})} | custom-call | flops 251658240 | bytes 2752512 | tf_op jit(solution)/shard_map/spread/pallas_call | solution.py:162
  72.5 3.7 %collective-permute-start.27 = (bf16[8,128,128]{2,1,0:T(8,128)(2,1)S(1)}, bf16[8,128,128]{2,1,0:T(8,128)(2,1)S(1)}, u32[]{:S(2)}, u32[]{:S(2)}) collective-permute-start(bf16[8,128,128]{2,1,0:T(8,128)(2,1)S(1)} %get-tuple-element.50), channel_id=1, source_target_pairs={{0,4},{4,0},{8,12},{12,8},{16,20},{20,16},{24,28},{28,24},{1,5},{5... | collective-permute-start | bytes 786440 | tf_op jit(solution)/shard_map/ppermute | solution.py:20
  76.9 4.3 %collective-permute-start.29 = (bf16[8,128,128]{2,1,0:T(8,128)(2,1)S(1)}, bf16[8,128,128]{2,1,0:T(8,128)(2,1)S(1)}, u32[]{:S(2)}, u32[]{:S(2)}) collective-permute-start(bf16[8,128,128]{2,1,0:T(8,128)(2,1)S(1)} %get-tuple-element.52), channel_id=1, source_target_pairs={{0,8},{4,12},{8,0},{12,4},{16,24},{20,28},{24,16},{28,20},{1,9},{5... | collective-permute-start | bytes 786440 | tf_op jit(solution)/shard_map/ppermute | solution.py:20
  81.3 8.5 %collective-permute-done.16.got = bf16[4,128,128]{2,1,0:T(8,128)(2,1)S(1)} collective-permute-done((bf16[4,128,128]{2,1,0:T(8,128)(2,1)S(1)}, bf16[4,128,128]{2,1,0:T(8,128)(2,1)S(1)}, u32[]{:S(2)}, u32[]{:S(2)}) %collective-permute-start.16) | collective-permute-done | bytes 131104 | tf_op jit(solution)/shard_map/ppermute | solution.py:20
  91.8 1.5 %collective-permute-start.18 = (bf16[128,128]{1,0:T(8,128)(2,1)S(1)}, bf16[128,128]{1,0:T(8,128)(2,1)S(1)}, u32[]{:S(2)}, u32[]{:S(2)}) collective-permute-start(bf16[128,128]{1,0:T(8,128)(2,1)S(1)} %get-tuple-element.45), channel_id=1, source_target_pairs={{0,2},{1,3},{2,0},{3,1},{4,6},{5,7},{6,4},{7,5},{8,10},{9,11},{10,... | collective-permute-start | bytes 98312 | tf_op jit(solution)/shard_map/ppermute | solution.py:20
  93.3 2.4 %collective-permute-done.18.refs_2_ = bf16[128,128]{1,0:T(8,128)(2,1)S(1)} collective-permute-done((bf16[128,128]{1,0:T(8,128)(2,1)S(1)}, bf16[128,128]{1,0:T(8,128)(2,1)S(1)}, u32[]{:S(2)}, u32[]{:S(2)}) %collective-permute-start.18) | collective-permute-done | bytes 32800 | tf_op jit(solution)/shard_map/ppermute | solution.py:20
  95.8 3.5 %collective-permute-done.19.refs_3_ = bf16[128,128]{1,0:T(8,128)(2,1)S(1)} collective-permute-done((bf16[128,128]{1,0:T(8,128)(2,1)S(1)}, bf16[128,128]{1,0:T(8,128)(2,1)S(1)}, u32[]{:S(2)}, u32[]{:S(2)}) %collective-permute-start.19) | collective-permute-done | bytes 32800 | tf_op jit(solution)/shard_map/ppermute | solution.py:20
  (65 shorter events, 16.9 us)
Async XLA Ops:
  1.6 13.1 %collective-permute-start.4 = (bf16[1280,128]{1,0:T(8,128)(2,1)S(1)}, bf16[1280,128]{1,0:T(8,128)(2,1)S(1)}, u32[]{:S(2)}, u32[]{:S(2)}) collective-permute-start(bf16[1280,128]{1,0:T(8,128)(2,1)S(1)} %slice.7.refs_0_), channel_id=1, source_target_pairs={{0,2},{1,3},{2,0},{3,1},{4,6},{5,7},{6,4},{7,5},{8,10},{9,11},{10,... | collective-permute-start | bytes 983048 | tf_op jit(solution)/shard_map/ppermute | solution.py:20
  4.7 28.2 %collective-permute-start.7 = (bf16[2048,128]{1,0:T(8,128)(2,1)}, bf16[2048,128]{1,0:T(8,128)(2,1)S(1)}, u32[]{:S(2)}, u32[]{:S(2)}) collective-permute-start(bf16[2048,128]{1,0:T(8,128)(2,1)} %refs_0_.5), channel_id=1, source_target_pairs={{0,2},{1,3},{2,0},{3,1},{4,6},{5,7},{6,4},{7,5},{8,10},{9,11},{10,... | collective-permute-start | bytes 1572872 | tf_op jit(solution)/shard_map/ppermute | solution.py:20
  5.7 22.1 %collective-permute-start.1 = (bf16[768,128]{1,0:T(8,128)(2,1)S(1)}, bf16[768,128]{1,0:T(8,128)(2,1)S(1)}, u32[]{:S(2)}, u32[]{:S(2)}) collective-permute-start(bf16[768,128]{1,0:T(8,128)(2,1)S(1)} %slice.8.refs_0_.refs_4_), channel_id=1, source_target_pairs={{0,2},{1,3},{2,0},{3,1},{4,6},{5,7},{6,4},{7,5},{8,10},{9,11},{10,... | collective-permute-start | bytes 589832 | tf_op jit(solution)/shard_map/ppermute | solution.py:20
  7.7 20.1 %collective-permute-start.3 = (bf16[1280,128]{1,0:T(8,128)(2,1)S(1)}, bf16[1280,128]{1,0:T(8,128)(2,1)S(1)}, u32[]{:S(2)}, u32[]{:S(2)}) collective-permute-start(bf16[1280,128]{1,0:T(8,128)(2,1)S(1)} %slice.7.refs_0_), channel_id=1, source_target_pairs={{0,1},{1,0},{2,3},{3,2},{4,5},{5,4},{6,7},{7,6},{8,9},{9,8},{10,11... | collective-permute-start | bytes 983048 | tf_op jit(solution)/shard_map/ppermute | solution.py:20
  14.7 13.1 %collective-permute-start.5 = (bf16[1280,128]{1,0:T(8,128)(2,1)S(1)}, bf16[1280,128]{1,0:T(8,128)(2,1)S(1)}, u32[]{:S(2)}, u32[]{:S(2)}) collective-permute-start(bf16[1280,128]{1,0:T(8,128)(2,1)S(1)} %collective-permute-done.4.refs_2_), channel_id=1, source_target_pairs={{0,1},{1,0},{2,3},{3,2},{4,5},{5,4},{6,7},{7,6},{8,9},{9,8},{10,11... | collective-permute-start | bytes 983048 | tf_op jit(solution)/shard_map/ppermute | solution.py:20
  15.3 14.8 %collective-permute-start = (bf16[768,128]{1,0:T(8,128)(2,1)S(1)}, bf16[768,128]{1,0:T(8,128)(2,1)S(1)}, u32[]{:S(2)}, u32[]{:S(2)}) collective-permute-start(bf16[768,128]{1,0:T(8,128)(2,1)S(1)} %slice.8.refs_0_.refs_4_), channel_id=1, source_target_pairs={{0,1},{1,0},{2,3},{3,2},{4,5},{5,4},{6,7},{7,6},{8,9},{9,8},{10,11... | collective-permute-start | bytes 589832 | tf_op jit(solution)/shard_map/ppermute | solution.py:20
  31.6 6.5 %collective-permute-start.9 = (bf16[8,128,128]{2,1,0:T(8,128)(2,1)S(1)}, bf16[8,128,128]{2,1,0:T(8,128)(2,1)S(1)}, u32[]{:S(2)}, u32[]{:S(2)}) collective-permute-start(bf16[8,128,128]{2,1,0:T(8,128)(2,1)S(1)} %get-tuple-element.32), channel_id=1, source_target_pairs={{4,8},{8,4},{12,16},{16,12},{20,24},{24,20},{5,9},{9,5},{13,17},{1... | collective-permute-start | bytes 786440 | tf_op jit(solution)/shard_map/ppermute | solution.py:20
  32.3 19.2 %collective-permute-start.6 = (bf16[2048,128]{1,0:T(8,128)(2,1)S(1)}, bf16[2048,128]{1,0:T(8,128)(2,1)S(1)}, u32[]{:S(2)}, u32[]{:S(2)}) collective-permute-start(bf16[2048,128]{1,0:T(8,128)(2,1)S(1)} %copy-done.3), channel_id=1, source_target_pairs={{0,1},{1,0},{2,3},{3,2},{4,5},{5,4},{6,7},{7,6},{8,9},{9,8},{10,11... | collective-permute-start | bytes 1572872 | tf_op jit(solution)/shard_map/ppermute | solution.py:20
  32.8 18.6 %collective-permute-start.8 = (bf16[2048,128]{1,0:T(8,128)(2,1)S(1)}, bf16[2048,128]{1,0:T(8,128)(2,1)S(1)}, u32[]{:S(2)}, u32[]{:S(2)}) collective-permute-start(bf16[2048,128]{1,0:T(8,128)(2,1)S(1)} %collective-permute-done.7.refs_2_), channel_id=1, source_target_pairs={{0,1},{1,0},{2,3},{3,2},{4,5},{5,4},{6,7},{7,6},{8,9},{9,8},{10,11... | collective-permute-start | bytes 1572872 | tf_op jit(solution)/shard_map/ppermute | solution.py:20
  32.9 15.1 %collective-permute-start.10 = (bf16[8,128,128]{2,1,0:T(8,128)(2,1)S(1)}, bf16[8,128,128]{2,1,0:T(8,128)(2,1)S(1)}, u32[]{:S(2)}, u32[]{:S(2)}) collective-permute-start(bf16[8,128,128]{2,1,0:T(8,128)(2,1)S(1)} %get-tuple-element.35), channel_id=1, source_target_pairs={{0,4},{4,0},{8,12},{12,8},{16,20},{20,16},{24,28},{28,24},{1,5},{5... | collective-permute-start | bytes 786440 | tf_op jit(solution)/shard_map/ppermute | solution.py:20
  37.4 10.6 %collective-permute-start.11 = (bf16[8,128,128]{2,1,0:T(8,128)(2,1)S(1)}, bf16[8,128,128]{2,1,0:T(8,128)(2,1)S(1)}, u32[]{:S(2)}, u32[]{:S(2)}) collective-permute-start(bf16[8,128,128]{2,1,0:T(8,128)(2,1)S(1)} %get-tuple-element.36), channel_id=1, source_target_pairs={{8,16},{12,20},{16,8},{20,12},{9,17},{13,21},{17,9},{21,13},{10,18... | collective-permute-start | bytes 786440 | tf_op jit(solution)/shard_map/ppermute | solution.py:20
  38.0 13.0 %collective-permute-start.12 = (bf16[8,128,128]{2,1,0:T(8,128)(2,1)S(1)}, bf16[8,128,128]{2,1,0:T(8,128)(2,1)S(1)}, u32[]{:S(2)}, u32[]{:S(2)}) collective-permute-start(bf16[8,128,128]{2,1,0:T(8,128)(2,1)S(1)} %get-tuple-element.37), channel_id=1, source_target_pairs={{0,8},{4,12},{8,0},{12,4},{16,24},{20,28},{24,16},{28,20},{1,9},{5... | collective-permute-start | bytes 786440 | tf_op jit(solution)/shard_map/ppermute | solution.py:20
  52.2 5.0 %collective-permute-start.13 = (bf16[4,128,128]{2,1,0:T(8,128)(2,1)S(1)}, bf16[4,128,128]{2,1,0:T(8,128)(2,1)S(1)}, u32[]{:S(2)}, u32[]{:S(2)}) collective-permute-start(bf16[4,128,128]{2,1,0:T(8,128)(2,1)S(1)} %get-tuple-element.41), channel_id=1, source_target_pairs={{0,4},{4,0},{8,12},{12,8},{16,20},{20,16},{24,28},{28,24},{1,5},{5... | collective-permute-start | bytes 393224 | tf_op jit(solution)/shard_map/ppermute | solution.py:20
  54.0 12.8 %collective-permute-start.21 = (bf16[768,128]{1,0:T(8,128)(2,1)S(1)}, bf16[768,128]{1,0:T(8,128)(2,1)S(1)}, u32[]{:S(2)}, u32[]{:S(2)}) collective-permute-start(bf16[768,128]{1,0:T(8,128)(2,1)S(1)} %get-tuple-element.39.refs_5_.refs_0_), channel_id=1, source_target_pairs={{0,2},{1,3},{2,0},{3,1},{4,6},{5,7},{6,4},{7,5},{8,10},{9,11},{10,... | collective-permute-start | bytes 589832 | tf_op jit(solution)/shard_map/ppermute | solution.py:20
  55.5 10.8 %collective-permute-start.24 = (bf16[1280,128]{1,0:T(8,128)(2,1)S(1)}, bf16[1280,128]{1,0:T(8,128)(2,1)S(1)}, u32[]{:S(2)}, u32[]{:S(2)}) collective-permute-start(bf16[1280,128]{1,0:T(8,128)(2,1)S(1)} %get-tuple-element.38.refs_4_.refs_0_), channel_id=1, source_target_pairs={{0,2},{1,3},{2,0},{3,1},{4,6},{5,7},{6,4},{7,5},{8,10},{9,11},{10,... | collective-permute-start | bytes 983048 | tf_op jit(solution)/shard_map/ppermute | solution.py:20
  57.3 9.5 %collective-permute-start.14 = (bf16[4,128,128]{2,1,0:T(8,128)(2,1)S(1)}, bf16[4,128,128]{2,1,0:T(8,128)(2,1)S(1)}, u32[]{:S(2)}, u32[]{:S(2)}) collective-permute-start(bf16[4,128,128]{2,1,0:T(8,128)(2,1)S(1)} %add_convert_fusion.2), channel_id=1, source_target_pairs={{0,16},{4,20},{8,24},{12,28},{16,0},{20,4},{24,8},{28,12},{1,17},{... | collective-permute-start | bytes 393224 | tf_op jit(solution)/shard_map/ppermute | solution.py:20
  60.1 8.0 %collective-permute-start.23 = (bf16[1280,128]{1,0:T(8,128)(2,1)S(1)}, bf16[1280,128]{1,0:T(8,128)(2,1)S(1)}, u32[]{:S(2)}, u32[]{:S(2)}) collective-permute-start(bf16[1280,128]{1,0:T(8,128)(2,1)S(1)} %get-tuple-element.38.refs_4_.refs_0_), channel_id=1, source_target_pairs={{0,1},{1,0},{2,3},{3,2},{4,5},{5,4},{6,7},{7,6},{8,9},{9,8},{10,11... | collective-permute-start | bytes 983048 | tf_op jit(solution)/shard_map/ppermute | solution.py:20
  66.2 4.1 %collective-permute-start.20 = (bf16[768,128]{1,0:T(8,128)(2,1)S(1)}, bf16[768,128]{1,0:T(8,128)(2,1)S(1)}, u32[]{:S(2)}, u32[]{:S(2)}) collective-permute-start(bf16[768,128]{1,0:T(8,128)(2,1)S(1)} %get-tuple-element.39.refs_5_.refs_0_), channel_id=1, source_target_pairs={{0,1},{1,0},{2,3},{3,2},{4,5},{5,4},{6,7},{7,6},{8,9},{9,8},{10,11... | collective-permute-start | bytes 589832 | tf_op jit(solution)/shard_map/ppermute | solution.py:20
  66.8 14.4 %collective-permute-start.15 = (bf16[4,128,128]{2,1,0:T(8,128)(2,1)S(1)}, bf16[4,128,128]{2,1,0:T(8,128)(2,1)S(1)}, u32[]{:S(2)}, u32[]{:S(2)}) collective-permute-start(bf16[4,128,128]{2,1,0:T(8,128)(2,1)S(1)} %add_convert_fusion.1), channel_id=1, source_target_pairs={{0,8},{4,12},{8,0},{12,4},{16,24},{20,28},{24,16},{28,20},{1,9},{5... | collective-permute-start | bytes 393224 | tf_op jit(solution)/shard_map/ppermute | solution.py:20
  71.8 28.3 %collective-permute-start.26 = (bf16[8,128,128]{2,1,0:T(8,128)(2,1)S(1)}, bf16[8,128,128]{2,1,0:T(8,128)(2,1)S(1)}, u32[]{:S(2)}, u32[]{:S(2)}) collective-permute-start(bf16[8,128,128]{2,1,0:T(8,128)(2,1)S(1)} %get-tuple-element.49), channel_id=1, source_target_pairs={{4,8},{8,4},{12,16},{16,12},{20,24},{24,20},{5,9},{9,5},{13,17},{1... | collective-permute-start | bytes 786440 | tf_op jit(solution)/shard_map/ppermute | solution.py:20
  72.5 27.6 %collective-permute-start.27 = (bf16[8,128,128]{2,1,0:T(8,128)(2,1)S(1)}, bf16[8,128,128]{2,1,0:T(8,128)(2,1)S(1)}, u32[]{:S(2)}, u32[]{:S(2)}) collective-permute-start(bf16[8,128,128]{2,1,0:T(8,128)(2,1)S(1)} %get-tuple-element.50), channel_id=1, source_target_pairs={{0,4},{4,0},{8,12},{12,8},{16,20},{20,16},{24,28},{28,24},{1,5},{5... | collective-permute-start | bytes 786440 | tf_op jit(solution)/shard_map/ppermute | solution.py:20
  76.2 23.9 %collective-permute-start.28 = (bf16[8,128,128]{2,1,0:T(8,128)(2,1)S(1)}, bf16[8,128,128]{2,1,0:T(8,128)(2,1)S(1)}, u32[]{:S(2)}, u32[]{:S(2)}) collective-permute-start(bf16[8,128,128]{2,1,0:T(8,128)(2,1)S(1)} %get-tuple-element.51), channel_id=1, source_target_pairs={{8,16},{12,20},{16,8},{20,12},{9,17},{13,21},{17,9},{21,13},{10,18... | collective-permute-start | bytes 786440 | tf_op jit(solution)/shard_map/ppermute | solution.py:20
  76.9 23.2 %collective-permute-start.29 = (bf16[8,128,128]{2,1,0:T(8,128)(2,1)S(1)}, bf16[8,128,128]{2,1,0:T(8,128)(2,1)S(1)}, u32[]{:S(2)}, u32[]{:S(2)}) collective-permute-start(bf16[8,128,128]{2,1,0:T(8,128)(2,1)S(1)} %get-tuple-element.52), channel_id=1, source_target_pairs={{0,8},{4,12},{8,0},{12,4},{16,24},{20,28},{24,16},{28,20},{1,9},{5... | collective-permute-start | bytes 786440 | tf_op jit(solution)/shard_map/ppermute | solution.py:20
  81.2 8.6 %collective-permute-start.16 = (bf16[4,128,128]{2,1,0:T(8,128)(2,1)S(1)}, bf16[4,128,128]{2,1,0:T(8,128)(2,1)S(1)}, u32[]{:S(2)}, u32[]{:S(2)}) collective-permute-start(bf16[4,128,128]{2,1,0:T(8,128)(2,1)S(1)} %add_convert_fusion.kept), channel_id=1, source_target_pairs={{0,4},{4,0},{8,12},{12,8},{16,20},{20,16},{24,28},{28,24},{1,5},{5... | collective-permute-start | bytes 393224 | tf_op jit(solution)/shard_map/ppermute | solution.py:20
  (12 other events, 58.3 us)

commit v4 on v3

--- a/solution.py
+++ b/solution.py
@@ -184,7 +184,18 @@
     if masked:
         mask, *outs = refs
     else:
-        outs = refs
+        grad, other, second, first, *outs = refs
+
+        @pl.when(odd)
+        def _():
+            second[...] = grad[...].astype(second.dtype)
+            first[...] = other[...].astype(first.dtype)
+
+        @pl.when(jnp.logical_not(odd))
+        def _():
+            second[...] = other[...].astype(second.dtype)
+            first[...] = grad[...].astype(first.dtype)
+
     places = [(out, i) for out in outs for i in range(out.shape[0] // size)]
 
     def write(tile, near, far):
@@ -211,9 +222,9 @@
     return own, *got
 
 
-def join(sums, outs, mask=None):
+def join(sums, outs, mask=None, extra=()):
     masked = mask is not None
-    args = [*sums, mask] if masked else list(sums)
+    args = [*sums, mask] if masked else [*sums, *extra]
     return pl.pallas_call(
         functools.partial(join_kernel, masked, 2 * sums[1].shape[0]),
         out_shape=outs,
@@ -256,23 +267,21 @@
         send[m] = jnp.where(odd, total, seconds[m])
 
 
-def parted_kernel(kept, got, second_out, *blocks):
+def parted_kernel(value, other, total, *blocks):
+    for m, block in enumerate(blocks):
+        sums = value[m].astype(jnp.float32) + other[m].astype(jnp.float32)
+        total[m] = sums.astype(total.dtype)
+        block[...] = total[m]
+
+
+def placed_kernel(total, *refs):
+    *blocks, out = refs
     odd = (lax.axis_index("dom") & 1) == 1
     place = lax.axis_index("feat")
-    width = kept.shape[1]
-    for m, block in enumerate(blocks):
-        block[...] = jnp.where(odd, got[m], kept[m])
+    width = out.shape[0]
+    for m in range(total.shape[0]):
         columns = pl.ds(pl.multiple_of((place ^ m) * width, width), width)
-        second_out[:, columns] = jnp.where(odd, kept[m], got[m]).astype(second_out.dtype)
-
-
-def placed_kernel(*refs):
-    *blocks, out = refs
-    place = lax.axis_index("feat")
-    width = out.shape[0]
-    for m, block in enumerate(blocks):
-        columns = pl.ds(pl.multiple_of((place ^ m) * width, width), width)
-        out[:, columns] = block[...].astype(out.dtype)
+        out[:, columns] = jnp.where(odd, total[m], blocks[m - 1][...] if m else total[m])
 
 
 def small_call(kernel, outs, args, flops=0):
@@ -293,13 +302,13 @@
 
 
 def dom_sums(keep, send):
-    value = added(keep, exchanged(send, "dom", lambda s: s ^ 1))
+    value, other = keep, exchanged(send, "dom", lambda s: s ^ 1)
     mask = lax.axis_size("dom") // 2
     while mask > 1:
+        value = added(value, other)
         other = exchanged(value, "dom", lambda s, mask=mask: s ^ mask)
-        value = added(value, other)
         mask //= 2
-    return value, exchanged(value, "dom", lambda s: s ^ 1)
+    return value, other
 
 
 def shards(grad_pre2, aggregated2, weight2, pre1, aggregated1, weight1, blocks, targets):
@@ -317,7 +326,6 @@
     count = len(gathered[0])
     flops = 2 * nodes * count * width**2
     grads = jax.ShapeDtypeStruct((count, width, width), jnp.bfloat16)
-    wide = jax.ShapeDtypeStruct((width, count * width), jnp.float32)
     own, *sends = layer(tiles, gathered, weight2, blocks, slots)
     sums = boundary(own, sends)
     (held,) = gather_pieces([aggregated1], "feat")
@@ -336,16 +344,18 @@
         [seconds, *held, *grad_pre1],
         flops,
     )
-    kept, got = dom_sums(keep, send)
+    addends = dom_sums(keep, send)
     own, *sends = layer(tiles, gathered, weight1, blocks, slots)
     sums = boundary(own, sends)
     block = jax.ShapeDtypeStruct((width, width), jnp.bfloat16)
-    second, *firsts = small_call(parted_kernel, [wide, *[block] * count], [kept, got])
-    firsts = [firsts[0]] + [
-        exchanged(firsts[m], "feat", lambda s, m=m: s ^ m) for m in range(1, count)
-    ]
-    first = small_call(placed_kernel, wide, firsts)
-    (grad_input,) = join(sums, [jax.ShapeDtypeStruct((nodes, width), jnp.bfloat16)])
+    total, *back = small_call(parted_kernel, [grads, *[block] * count], addends)
+    back = [exchanged(back[m], "feat", lambda s, m=m: s ^ m) for m in range(1, count)]
+    wide = jax.ShapeDtypeStruct((width, count * width), jnp.bfloat16)
+    grad = small_call(placed_kernel, wide, [total, *back])
+    other = exchanged(grad, "dom", lambda s: s ^ 1)
+    wide = jax.ShapeDtypeStruct(wide.shape, jnp.float32)
+    outs = [wide, wide, jax.ShapeDtypeStruct((nodes, width), jnp.bfloat16)]
+    second, first, grad_input = join(sums, outs, extra=[grad, other])
     return (second, first, grad_input)
 
 

time: 101 us -> 97.3 us (0.963)
  waiting for transfers between devices: 40.8 us -> 37.1 us
    ppermute x30, waiting for transfers between devices: 40.8 us -> 37.1 us  [exchanged(): return lax.ppermute(value, axis, pairs)]
  transfers between devices with their start and end apart: 30 -> 30, of which waited for: 9 -> 10; matrix products, arithmetic and copies ran while one was open for 2% -> 2% of each run, Pallas kernels for 12% -> 12%
where the time goes in v4:
time: 97.3 us; the launch traced here: 97 us
  starting transfers between devices  38.9 us (40%)
  waiting for transfers between devices  37.1 us (38%)
  Pallas kernels  13.6 us (14%)
  local copies, waits for them, and re-layouts  6.41 us (7%)
    ppermute x30, starting transfers between devices, exchanged(): return lax.ppermute(value, axis, pairs)  38.9 us
    ppermute x30, waiting for transfers between devices, exchanged(): return lax.ppermute(value, axis, pairs)  37.1 us
    pallas_call x4, Pallas kernels, spread(): pl.pallas_call(functools.partial(spread_kernel, total is None, tiles), ou...  7.3 us
    unnamed x13, local copies, waits for them, and re-layouts  4.48 us
    pallas_call x1, Pallas kernels, prepare(): pl.pallas_call(prepare_kernel, out_shape=outs, in_specs=[ANY, pl.BlockSpe...  2.52 us
    pallas_call x4, Pallas kernels, small_call(): pl.pallas_call(kernel, out_shape=outs, in_specs=[VMEM] * len(args), out_s...  2.24 us
  transfers between devices with their start and end apart: 30, of which 10 were waited for; matrix products, arithmetic and copies ran while one was open for 2% of the time, Pallas kernels for 12%

profile of v4, /device:TPU:0, one launch (start us, length us, event | category | flops | bytes accessed | tf_op | source)
XLA Modules:
  0.0 97.0 jit_solution(6555018135544545311)
XLA Ops:
  1.6 3.0 %collective-permute-start.4 = (bf16[1280,128]{1,0:T(8,128)(2,1)S(1)}, bf16[1280,128]{1,0:T(8,128)(2,1)S(1)}, u32[]{:S(2)}, u32[]{:S(2)}) collective-permute-start(bf16[1280,128]{1,0:T(8,128)(2,1)S(1)} %slice.7.refs_0_), channel_id=1, source_target_pairs={{0,2},{1,3},{2,0},{3,1},{4,6},{5,7},{6,4},{7,5},{8,10},{9,11},{10,... | collective-permute-start | bytes 983048 | tf_op jit(solution)/shard_map/ppermute | solution.py:20
  5.7 2.0 %collective-permute-start.1 = (bf16[768,128]{1,0:T(8,128)(2,1)S(1)}, bf16[768,128]{1,0:T(8,128)(2,1)S(1)}, u32[]{:S(2)}, u32[]{:S(2)}) collective-permute-start(bf16[768,128]{1,0:T(8,128)(2,1)S(1)} %slice.8.refs_0_.refs_4_), channel_id=1, source_target_pairs={{0,2},{1,3},{2,0},{3,1},{4,6},{5,7},{6,4},{7,5},{8,10},{9,11},{10,... | collective-permute-start | bytes 589832 | tf_op jit(solution)/shard_map/ppermute | solution.py:20
  8.5 1.9 %copy-done = bf16[16,6,128,128]{3,2,1,0:T(8,128)(2,1)S(1)} copy-done((bf16[16,6,128,128]{3,2,1,0:T(8,128)(2,1)S(1)}, bf16[16,6,128,128]{3,2,1,0:T(8,128)(2,1)}, u32[]{:S(2)}) %copy-start) | copy-done | bytes 3145752
  12.2 2.5 %prepare.1 = (s32[16,6]{1,0:T(8,128)S(1)}, bf16[16,6,128,128]{3,2,1,0:T(8,128)(2,1)S(1)}, bf16[512,128]{1,0:T(8,128)(2,1)S(1)}, bf16[512,128]{1,0:T(8,128)(2,1)S(1)}) custom-call(s32[16,6]{1,0:T(8,128)S(1)} %copy.13.targets_hbm, bf16[16,6,128,128]{3,2,1,0:T(8,128)(2,1)S(1)} %copy-done, bf16[128,512]{1,0:T(8,128)(2,1)S(1)} %copy-done.4, ...), custom_call_target="tpu_custom_call" | custom-call | bytes 6291456 | tf_op jit(solution)/shard_map/prepare/pallas_call | solution.py:95
  15.4 12.5 %collective-permute-done.1.refs_2_.refs_6_ = bf16[768,128]{1,0:T(8,128)(2,1)S(1)} collective-permute-done((bf16[768,128]{1,0:T(8,128)(2,1)S(1)}, bf16[768,128]{1,0:T(8,128)(2,1)S(1)}, u32[]{:S(2)}, u32[]{:S(2)}) %collective-permute-start.1) | collective-permute-done | bytes 196640 | tf_op jit(solution)/shard_map/ppermute | solution.py:20
  27.8 2.2 %spread.4.refs_4_ = f32[48,128,128]{2,1,0:T(8,128)S(1)} custom-call(s32[16,6]{1,0:T(8,128)S(1)} %get-tuple-element.27.slots_ref, bf16[512,128]{1,0:T(8,128)(2,1)S(1)} %get-tuple-element.30.weights, bf16[16,6,128,128]{3,2,1,0:T(8,128)(2,1)S(1)} %get-tuple-element.29.blocks, bf16[1280,128]{1,0:T(8,128)(2,1)S(1)} %slice.7.refs_0_, ...), custom_call_target="tpu_custom_call" | custom-call | flops 419430400 | bytes 4587520 | tf_op jit(solution)/shard_map/spread/pallas_call | solution.py:162
  30.1 1.5 %spread.5 = (f32[48,128,128]{2,1,0:T(8,128)S(1)}, bf16[8,128,128]{2,1,0:T(8,128)(2,1)S(1)}, bf16[8,128,128]{2,1,0:T(8,128)(2,1)S(1)}, bf16[8,128,128]{2,1,0:T(8,128)(2,1)S(1)}, bf16[8,128,128]{2,1,0:T(8,128)(2,1)S(1)}) custom-call(s32[16,6]{1,0:T(8,128)S(1)} %get-tuple-element.27.slots_ref, ...), custom_call_target="tpu_custom_call", output_to_operand_aliasing={{0}: (7, {})} | custom-call | flops 251658240 | bytes 2752512 | tf_op jit(solution)/shard_map/spread/pallas_call | solution.py:162
  32.9 4.5 %collective-permute-start.7 = (bf16[8,128,128]{2,1,0:T(8,128)(2,1)S(1)}, bf16[8,128,128]{2,1,0:T(8,128)(2,1)S(1)}, u32[]{:S(2)}, u32[]{:S(2)}) collective-permute-start(bf16[8,128,128]{2,1,0:T(8,128)(2,1)S(1)} %get-tuple-element.34), channel_id=1, source_target_pairs={{0,4},{4,0},{8,12},{12,8},{16,20},{20,16},{24,28},{28,24},{1,5},{5... | collective-permute-start | bytes 786440 | tf_op jit(solution)/shard_map/ppermute | solution.py:20
  38.1 7.0 %collective-permute-start.9 = (bf16[8,128,128]{2,1,0:T(8,128)(2,1)S(1)}, bf16[8,128,128]{2,1,0:T(8,128)(2,1)S(1)}, u32[]{:S(2)}, u32[]{:S(2)}) collective-permute-start(bf16[8,128,128]{2,1,0:T(8,128)(2,1)S(1)} %get-tuple-element.36), channel_id=1, source_target_pairs={{0,8},{4,12},{8,0},{12,4},{16,24},{20,28},{24,16},{28,20},{1,9},{5... | collective-permute-start | bytes 786440 | tf_op jit(solution)/shard_map/ppermute | solution.py:20
  45.8 2.2 %collective-permute-done.7.across = bf16[8,128,128]{2,1,0:T(8,128)(2,1)S(1)} collective-permute-done((bf16[8,128,128]{2,1,0:T(8,128)(2,1)S(1)}, bf16[8,128,128]{2,1,0:T(8,128)(2,1)S(1)}, u32[]{:S(2)}, u32[]{:S(2)}) %collective-permute-start.7) | collective-permute-done | bytes 262176 | tf_op jit(solution)/shard_map/ppermute | solution.py:20
  48.0 3.1 %collective-permute-done.9.apart = bf16[8,128,128]{2,1,0:T(8,128)(2,1)S(1)} collective-permute-done((bf16[8,128,128]{2,1,0:T(8,128)(2,1)S(1)}, bf16[8,128,128]{2,1,0:T(8,128)(2,1)S(1)}, u32[]{:S(2)}, u32[]{:S(2)}) %collective-permute-start.9) | collective-permute-done | bytes 262176 | tf_op jit(solution)/shard_map/ppermute | solution.py:20
  52.2 1.7 %collective-permute-start.23 = (bf16[4,128,128]{2,1,0:T(8,128)(2,1)S(1)}, bf16[4,128,128]{2,1,0:T(8,128)(2,1)S(1)}, u32[]{:S(2)}, u32[]{:S(2)}) collective-permute-start(bf16[4,128,128]{2,1,0:T(8,128)(2,1)S(1)} %get-tuple-element.46), channel_id=1, source_target_pairs={{0,4},{4,0},{8,12},{12,8},{16,20},{20,16},{24,28},{28,24},{1,5},{5... | collective-permute-start | bytes 393224 | tf_op jit(solution)/shard_map/ppermute | solution.py:20
  54.0 1.5 %collective-permute-start.14 = (bf16[1280,128]{1,0:T(8,128)(2,1)S(1)}, bf16[1280,128]{1,0:T(8,128)(2,1)S(1)}, u32[]{:S(2)}, u32[]{:S(2)}) collective-permute-start(bf16[1280,128]{1,0:T(8,128)(2,1)S(1)} %get-tuple-element.38.refs_0_.refs_4_), channel_id=1, source_target_pairs={{0,2},{1,3},{2,0},{3,1},{4,6},{5,7},{6,4},{7,5},{8,10},{9,11},{10,... | collective-permute-start | bytes 983048 | tf_op jit(solution)/shard_map/ppermute | solution.py:20
  57.3 2.8 %collective-permute-start.24 = (bf16[4,128,128]{2,1,0:T(8,128)(2,1)S(1)}, bf16[4,128,128]{2,1,0:T(8,128)(2,1)S(1)}, u32[]{:S(2)}, u32[]{:S(2)}) collective-permute-start(bf16[4,128,128]{2,1,0:T(8,128)(2,1)S(1)} %add_convert_fusion.1), channel_id=1, source_target_pairs={{0,16},{4,20},{8,24},{12,28},{16,0},{20,4},{24,8},{28,12},{1,17},{... | collective-permute-start | bytes 393224 | tf_op jit(solution)/shard_map/ppermute | solution.py:20
  60.2 4.0 %collective-permute-done.14.refs_2_ = bf16[1280,128]{1,0:T(8,128)(2,1)S(1)} collective-permute-done((bf16[1280,128]{1,0:T(8,128)(2,1)S(1)}, bf16[1280,128]{1,0:T(8,128)(2,1)S(1)}, u32[]{:S(2)}, u32[]{:S(2)}) %collective-permute-start.14) | collective-permute-done | bytes 327712 | tf_op jit(solution)/shard_map/ppermute | solution.py:20
  64.6 1.6 %collective-permute-done.11.refs_2_ = bf16[768,128]{1,0:T(8,128)(2,1)S(1)} collective-permute-done((bf16[768,128]{1,0:T(8,128)(2,1)S(1)}, bf16[768,128]{1,0:T(8,128)(2,1)S(1)}, u32[]{:S(2)}, u32[]{:S(2)}) %collective-permute-start.11) | collective-permute-done | bytes 196640 | tf_op jit(solution)/shard_map/ppermute | solution.py:20
  67.5 2.2 %spread.6.refs_4_ = f32[48,128,128]{2,1,0:T(8,128)S(1)} custom-call(s32[16,6]{1,0:T(8,128)S(1)} %get-tuple-element.27.slots_ref, bf16[512,128]{1,0:T(8,128)(2,1)S(1)} %get-tuple-element.28.weights, bf16[16,6,128,128]{3,2,1,0:T(8,128)(2,1)S(1)} %get-tuple-element.29.blocks, bf16[1280,128]{1,0:T(8,128)(2,1)S(1)} %get-tuple-element.38.refs_0_.refs_4_, ...), custom_call_target="tpu_custom_call" | custom-call | flops 419430400 | bytes 4587520 | tf_op jit(solution)/shard_map/spread/pallas_call | solution.py:162
  69.7 1.5 %spread.7 = (f32[48,128,128]{2,1,0:T(8,128)S(1)}, bf16[8,128,128]{2,1,0:T(8,128)(2,1)S(1)}, bf16[8,128,128]{2,1,0:T(8,128)(2,1)S(1)}, bf16[8,128,128]{2,1,0:T(8,128)(2,1)S(1)}, bf16[8,128,128]{2,1,0:T(8,128)(2,1)S(1)}) custom-call(s32[16,6]{1,0:T(8,128)S(1)} %get-tuple-element.27.slots_ref, ...), custom_call_target="tpu_custom_call", output_to_operand_aliasing={{0}: (7, {})} | custom-call | flops 251658240 | bytes 2752512 | tf_op jit(solution)/shard_map/spread/pallas_call | solution.py:162
  71.8 3.7 %collective-permute-start.17 = (bf16[8,128,128]{2,1,0:T(8,128)(2,1)S(1)}, bf16[8,128,128]{2,1,0:T(8,128)(2,1)S(1)}, u32[]{:S(2)}, u32[]{:S(2)}) collective-permute-start(bf16[8,128,128]{2,1,0:T(8,128)(2,1)S(1)} %get-tuple-element.41), channel_id=1, source_target_pairs={{0,4},{4,0},{8,12},{12,8},{16,20},{20,16},{24,28},{28,24},{1,5},{5... | collective-permute-start | bytes 786440 | tf_op jit(solution)/shard_map/ppermute | solution.py:20
  76.2 4.5 %collective-permute-start.19 = (bf16[8,128,128]{2,1,0:T(8,128)(2,1)S(1)}, bf16[8,128,128]{2,1,0:T(8,128)(2,1)S(1)}, u32[]{:S(2)}, u32[]{:S(2)}) collective-permute-start(bf16[8,128,128]{2,1,0:T(8,128)(2,1)S(1)} %get-tuple-element.43), channel_id=1, source_target_pairs={{0,8},{4,12},{8,0},{12,4},{16,24},{20,28},{24,16},{28,20},{1,9},{5... | collective-permute-start | bytes 786440 | tf_op jit(solution)/shard_map/ppermute | solution.py:20
  82.5 1.5 %collective-permute-start.27 = (bf16[128,128]{1,0:T(8,128)(2,1)S(1)}, bf16[128,128]{1,0:T(8,128)(2,1)S(1)}, u32[]{:S(2)}, u32[]{:S(2)}) collective-permute-start(bf16[128,128]{1,0:T(8,128)(2,1)S(1)} %get-tuple-element.49), channel_id=1, source_target_pairs={{0,2},{1,3},{2,0},{3,1},{4,6},{5,7},{6,4},{7,5},{8,10},{9,11},{10,... | collective-permute-start | bytes 98312 | tf_op jit(solution)/shard_map/ppermute | solution.py:20
  84.0 2.5 %collective-permute-done.27.refs_1_ = bf16[128,128]{1,0:T(8,128)(2,1)S(1)} collective-permute-done((bf16[128,128]{1,0:T(8,128)(2,1)S(1)}, bf16[128,128]{1,0:T(8,128)(2,1)S(1)}, u32[]{:S(2)}, u32[]{:S(2)}) %collective-permute-start.27) | collective-permute-done | bytes 32800 | tf_op jit(solution)/shard_map/ppermute | solution.py:20
  86.8 3.3 %collective-permute-done.28.refs_2_ = bf16[128,128]{1,0:T(8,128)(2,1)S(1)} collective-permute-done((bf16[128,128]{1,0:T(8,128)(2,1)S(1)}, bf16[128,128]{1,0:T(8,128)(2,1)S(1)}, u32[]{:S(2)}, u32[]{:S(2)}) %collective-permute-start.28) | collective-permute-done | bytes 32800 | tf_op jit(solution)/shard_map/ppermute | solution.py:20
  90.3 5.5 %collective-permute-done.29.refs_1_ = bf16[128,512]{1,0:T(8,128)(2,1)S(1)} collective-permute-done((bf16[128,512]{1,0:T(8,128)(2,1)S(1)}, bf16[128,512]{1,0:T(8,128)(2,1)S(1)}, u32[]{:S(2)}, u32[]{:S(2)}) %collective-permute-start.29) | collective-permute-done | bytes 131104 | tf_op jit(solution)/shard_map/ppermute | solution.py:20
  (64 shorter events, 17.7 us)
Async XLA Ops:
  1.6 13.1 %collective-permute-start.4 = (bf16[1280,128]{1,0:T(8,128)(2,1)S(1)}, bf16[1280,128]{1,0:T(8,128)(2,1)S(1)}, u32[]{:S(2)}, u32[]{:S(2)}) collective-permute-start(bf16[1280,128]{1,0:T(8,128)(2,1)S(1)} %slice.7.refs_0_), channel_id=1, source_target_pairs={{0,2},{1,3},{2,0},{3,1},{4,6},{5,7},{6,4},{7,5},{8,10},{9,11},{10,... | collective-permute-start | bytes 983048 | tf_op jit(solution)/shard_map/ppermute | solution.py:20
  4.7 28.2 %collective-permute-start.21 = (bf16[2048,128]{1,0:T(8,128)(2,1)}, bf16[2048,128]{1,0:T(8,128)(2,1)S(1)}, u32[]{:S(2)}, u32[]{:S(2)}) collective-permute-start(bf16[2048,128]{1,0:T(8,128)(2,1)} %refs_0_.5), channel_id=1, source_target_pairs={{0,2},{1,3},{2,0},{3,1},{4,6},{5,7},{6,4},{7,5},{8,10},{9,11},{10,... | collective-permute-start | bytes 1572872 | tf_op jit(solution)/shard_map/ppermute | solution.py:20
  5.7 22.1 %collective-permute-start.1 = (bf16[768,128]{1,0:T(8,128)(2,1)S(1)}, bf16[768,128]{1,0:T(8,128)(2,1)S(1)}, u32[]{:S(2)}, u32[]{:S(2)}) collective-permute-start(bf16[768,128]{1,0:T(8,128)(2,1)S(1)} %slice.8.refs_0_.refs_4_), channel_id=1, source_target_pairs={{0,2},{1,3},{2,0},{3,1},{4,6},{5,7},{6,4},{7,5},{8,10},{9,11},{10,... | collective-permute-start | bytes 589832 | tf_op jit(solution)/shard_map/ppermute | solution.py:20
  7.7 20.1 %collective-permute-start.3 = (bf16[1280,128]{1,0:T(8,128)(2,1)S(1)}, bf16[1280,128]{1,0:T(8,128)(2,1)S(1)}, u32[]{:S(2)}, u32[]{:S(2)}) collective-permute-start(bf16[1280,128]{1,0:T(8,128)(2,1)S(1)} %slice.7.refs_0_), channel_id=1, source_target_pairs={{0,1},{1,0},{2,3},{3,2},{4,5},{5,4},{6,7},{7,6},{8,9},{9,8},{10,11... | collective-permute-start | bytes 983048 | tf_op jit(solution)/shard_map/ppermute | solution.py:20
  14.7 13.1 %collective-permute-start.5 = (bf16[1280,128]{1,0:T(8,128)(2,1)S(1)}, bf16[1280,128]{1,0:T(8,128)(2,1)S(1)}, u32[]{:S(2)}, u32[]{:S(2)}) collective-permute-start(bf16[1280,128]{1,0:T(8,128)(2,1)S(1)} %collective-permute-done.4.refs_2_), channel_id=1, source_target_pairs={{0,1},{1,0},{2,3},{3,2},{4,5},{5,4},{6,7},{7,6},{8,9},{9,8},{10,11... | collective-permute-start | bytes 983048 | tf_op jit(solution)/shard_map/ppermute | solution.py:20
  15.3 14.8 %collective-permute-start = (bf16[768,128]{1,0:T(8,128)(2,1)S(1)}, bf16[768,128]{1,0:T(8,128)(2,1)S(1)}, u32[]{:S(2)}, u32[]{:S(2)}) collective-permute-start(bf16[768,128]{1,0:T(8,128)(2,1)S(1)} %slice.8.refs_0_.refs_4_), channel_id=1, source_target_pairs={{0,1},{1,0},{2,3},{3,2},{4,5},{5,4},{6,7},{7,6},{8,9},{9,8},{10,11... | collective-permute-start | bytes 589832 | tf_op jit(solution)/shard_map/ppermute | solution.py:20
  31.6 6.5 %collective-permute-start.6 = (bf16[8,128,128]{2,1,0:T(8,128)(2,1)S(1)}, bf16[8,128,128]{2,1,0:T(8,128)(2,1)S(1)}, u32[]{:S(2)}, u32[]{:S(2)}) collective-permute-start(bf16[8,128,128]{2,1,0:T(8,128)(2,1)S(1)} %get-tuple-element.33), channel_id=1, source_target_pairs={{4,8},{8,4},{12,16},{16,12},{20,24},{24,20},{5,9},{9,5},{13,17},{1... | collective-permute-start | bytes 786440 | tf_op jit(solution)/shard_map/ppermute | solution.py:20
  32.3 19.2 %collective-permute-start.20 = (bf16[2048,128]{1,0:T(8,128)(2,1)S(1)}, bf16[2048,128]{1,0:T(8,128)(2,1)S(1)}, u32[]{:S(2)}, u32[]{:S(2)}) collective-permute-start(bf16[2048,128]{1,0:T(8,128)(2,1)S(1)} %copy-done.3), channel_id=1, source_target_pairs={{0,1},{1,0},{2,3},{3,2},{4,5},{5,4},{6,7},{7,6},{8,9},{9,8},{10,11... | collective-permute-start | bytes 1572872 | tf_op jit(solution)/shard_map/ppermute | solution.py:20
  32.8 18.6 %collective-permute-start.22 = (bf16[2048,128]{1,0:T(8,128)(2,1)S(1)}, bf16[2048,128]{1,0:T(8,128)(2,1)S(1)}, u32[]{:S(2)}, u32[]{:S(2)}) collective-permute-start(bf16[2048,128]{1,0:T(8,128)(2,1)S(1)} %collective-permute-done.21.refs_2_), channel_id=1, source_target_pairs={{0,1},{1,0},{2,3},{3,2},{4,5},{5,4},{6,7},{7,6},{8,9},{9,8},{10,11... | collective-permute-start | bytes 1572872 | tf_op jit(solution)/shard_map/ppermute | solution.py:20
  32.9 15.1 %collective-permute-start.7 = (bf16[8,128,128]{2,1,0:T(8,128)(2,1)S(1)}, bf16[8,128,128]{2,1,0:T(8,128)(2,1)S(1)}, u32[]{:S(2)}, u32[]{:S(2)}) collective-permute-start(bf16[8,128,128]{2,1,0:T(8,128)(2,1)S(1)} %get-tuple-element.34), channel_id=1, source_target_pairs={{0,4},{4,0},{8,12},{12,8},{16,20},{20,16},{24,28},{28,24},{1,5},{5... | collective-permute-start | bytes 786440 | tf_op jit(solution)/shard_map/ppermute | solution.py:20
  37.4 10.6 %collective-permute-start.8 = (bf16[8,128,128]{2,1,0:T(8,128)(2,1)S(1)}, bf16[8,128,128]{2,1,0:T(8,128)(2,1)S(1)}, u32[]{:S(2)}, u32[]{:S(2)}) collective-permute-start(bf16[8,128,128]{2,1,0:T(8,128)(2,1)S(1)} %get-tuple-element.35), channel_id=1, source_target_pairs={{8,16},{12,20},{16,8},{20,12},{9,17},{13,21},{17,9},{21,13},{10,18... | collective-permute-start | bytes 786440 | tf_op jit(solution)/shard_map/ppermute | solution.py:20
  38.1 13.0 %collective-permute-start.9 = (bf16[8,128,128]{2,1,0:T(8,128)(2,1)S(1)}, bf16[8,128,128]{2,1,0:T(8,128)(2,1)S(1)}, u32[]{:S(2)}, u32[]{:S(2)}) collective-permute-start(bf16[8,128,128]{2,1,0:T(8,128)(2,1)S(1)} %get-tuple-element.36), channel_id=1, source_target_pairs={{0,8},{4,12},{8,0},{12,4},{16,24},{20,28},{24,16},{28,20},{1,9},{5... | collective-permute-start | bytes 786440 | tf_op jit(solution)/shard_map/ppermute | solution.py:20
  52.2 5.0 %collective-permute-start.23 = (bf16[4,128,128]{2,1,0:T(8,128)(2,1)S(1)}, bf16[4,128,128]{2,1,0:T(8,128)(2,1)S(1)}, u32[]{:S(2)}, u32[]{:S(2)}) collective-permute-start(bf16[4,128,128]{2,1,0:T(8,128)(2,1)S(1)} %get-tuple-element.46), channel_id=1, source_target_pairs={{0,4},{4,0},{8,12},{12,8},{16,20},{20,16},{24,28},{28,24},{1,5},{5... | collective-permute-start | bytes 393224 | tf_op jit(solution)/shard_map/ppermute | solution.py:20
  54.0 10.2 %collective-permute-start.14 = (bf16[1280,128]{1,0:T(8,128)(2,1)S(1)}, bf16[1280,128]{1,0:T(8,128)(2,1)S(1)}, u32[]{:S(2)}, u32[]{:S(2)}) collective-permute-start(bf16[1280,128]{1,0:T(8,128)(2,1)S(1)} %get-tuple-element.38.refs_0_.refs_4_), channel_id=1, source_target_pairs={{0,2},{1,3},{2,0},{3,1},{4,6},{5,7},{6,4},{7,5},{8,10},{9,11},{10,... | collective-permute-start | bytes 983048 | tf_op jit(solution)/shard_map/ppermute | solution.py:20
  55.5 10.8 %collective-permute-start.11 = (bf16[768,128]{1,0:T(8,128)(2,1)S(1)}, bf16[768,128]{1,0:T(8,128)(2,1)S(1)}, u32[]{:S(2)}, u32[]{:S(2)}) collective-permute-start(bf16[768,128]{1,0:T(8,128)(2,1)S(1)} %get-tuple-element.37.refs_0_.refs_5_), channel_id=1, source_target_pairs={{0,2},{1,3},{2,0},{3,1},{4,6},{5,7},{6,4},{7,5},{8,10},{9,11},{10,... | collective-permute-start | bytes 589832 | tf_op jit(solution)/shard_map/ppermute | solution.py:20
  57.3 8.9 %collective-permute-start.24 = (bf16[4,128,128]{2,1,0:T(8,128)(2,1)S(1)}, bf16[4,128,128]{2,1,0:T(8,128)(2,1)S(1)}, u32[]{:S(2)}, u32[]{:S(2)}) collective-permute-start(bf16[4,128,128]{2,1,0:T(8,128)(2,1)S(1)} %add_convert_fusion.1), channel_id=1, source_target_pairs={{0,16},{4,20},{8,24},{12,28},{16,0},{20,4},{24,8},{28,12},{1,17},{... | collective-permute-start | bytes 393224 | tf_op jit(solution)/shard_map/ppermute | solution.py:20
  60.2 7.3 %collective-permute-start.13 = (bf16[1280,128]{1,0:T(8,128)(2,1)S(1)}, bf16[1280,128]{1,0:T(8,128)(2,1)S(1)}, u32[]{:S(2)}, u32[]{:S(2)}) collective-permute-start(bf16[1280,128]{1,0:T(8,128)(2,1)S(1)} %get-tuple-element.38.refs_0_.refs_4_), channel_id=1, source_target_pairs={{0,1},{1,0},{2,3},{3,2},{4,5},{5,4},{6,7},{7,6},{8,9},{9,8},{10,11... | collective-permute-start | bytes 983048 | tf_op jit(solution)/shard_map/ppermute | solution.py:20
  64.1 5.5 %collective-permute-start.10 = (bf16[768,128]{1,0:T(8,128)(2,1)S(1)}, bf16[768,128]{1,0:T(8,128)(2,1)S(1)}, u32[]{:S(2)}, u32[]{:S(2)}) collective-permute-start(bf16[768,128]{1,0:T(8,128)(2,1)S(1)} %get-tuple-element.37.refs_0_.refs_5_), channel_id=1, source_target_pairs={{0,1},{1,0},{2,3},{3,2},{4,5},{5,4},{6,7},{7,6},{8,9},{9,8},{10,11... | collective-permute-start | bytes 589832 | tf_op jit(solution)/shard_map/ppermute | solution.py:20
  66.3 14.4 %collective-permute-start.25 = (bf16[4,128,128]{2,1,0:T(8,128)(2,1)S(1)}, bf16[4,128,128]{2,1,0:T(8,128)(2,1)S(1)}, u32[]{:S(2)}, u32[]{:S(2)}) collective-permute-start(bf16[4,128,128]{2,1,0:T(8,128)(2,1)S(1)} %add_convert_fusion.value), channel_id=1, source_target_pairs={{0,8},{4,12},{8,0},{12,4},{16,24},{20,28},{24,16},{28,20},{1,9},{5... | collective-permute-start | bytes 393224 | tf_op jit(solution)/shard_map/ppermute | solution.py:20
  71.2 24.6 %collective-permute-start.16 = (bf16[8,128,128]{2,1,0:T(8,128)(2,1)S(1)}, bf16[8,128,128]{2,1,0:T(8,128)(2,1)S(1)}, u32[]{:S(2)}, u32[]{:S(2)}) collective-permute-start(bf16[8,128,128]{2,1,0:T(8,128)(2,1)S(1)} %get-tuple-element.40), channel_id=1, source_target_pairs={{4,8},{8,4},{12,16},{16,12},{20,24},{24,20},{5,9},{9,5},{13,17},{1... | collective-permute-start | bytes 786440 | tf_op jit(solution)/shard_map/ppermute | solution.py:20
  71.8 23.9 %collective-permute-start.17 = (bf16[8,128,128]{2,1,0:T(8,128)(2,1)S(1)}, bf16[8,128,128]{2,1,0:T(8,128)(2,1)S(1)}, u32[]{:S(2)}, u32[]{:S(2)}) collective-permute-start(bf16[8,128,128]{2,1,0:T(8,128)(2,1)S(1)} %get-tuple-element.41), channel_id=1, source_target_pairs={{0,4},{4,0},{8,12},{12,8},{16,20},{20,16},{24,28},{28,24},{1,5},{5... | collective-permute-start | bytes 786440 | tf_op jit(solution)/shard_map/ppermute | solution.py:20
  75.5 20.2 %collective-permute-start.18 = (bf16[8,128,128]{2,1,0:T(8,128)(2,1)S(1)}, bf16[8,128,128]{2,1,0:T(8,128)(2,1)S(1)}, u32[]{:S(2)}, u32[]{:S(2)}) collective-permute-start(bf16[8,128,128]{2,1,0:T(8,128)(2,1)S(1)} %get-tuple-element.42), channel_id=1, source_target_pairs={{8,16},{12,20},{16,8},{20,12},{9,17},{13,21},{17,9},{21,13},{10,18... | collective-permute-start | bytes 786440 | tf_op jit(solution)/shard_map/ppermute | solution.py:20
  76.2 19.6 %collective-permute-start.19 = (bf16[8,128,128]{2,1,0:T(8,128)(2,1)S(1)}, bf16[8,128,128]{2,1,0:T(8,128)(2,1)S(1)}, u32[]{:S(2)}, u32[]{:S(2)}) collective-permute-start(bf16[8,128,128]{2,1,0:T(8,128)(2,1)S(1)} %get-tuple-element.43), channel_id=1, source_target_pairs={{0,8},{4,12},{8,0},{12,4},{16,24},{20,28},{24,16},{28,20},{1,9},{5... | collective-permute-start | bytes 786440 | tf_op jit(solution)/shard_map/ppermute | solution.py:20
  90.2 5.6 %collective-permute-start.29 = (bf16[128,512]{1,0:T(8,128)(2,1)S(1)}, bf16[128,512]{1,0:T(8,128)(2,1)S(1)}, u32[]{:S(2)}, u32[]{:S(2)}) collective-permute-start(bf16[128,512]{1,0:T(8,128)(2,1)S(1)} %shard_map.106.refs_0_), channel_id=1, source_target_pairs={{0,4},{4,0},{8,12},{12,8},{16,20},{20,16},{24,28},{28,24},{1,5},{5... | collective-permute-start | bytes 393224 | tf_op jit(solution)/shard_map/ppermute | solution.py:20
  (12 other events, 59.7 us)

commit v5 on v4

--- a/solution.py
+++ b/solution.py
@@ -184,7 +184,8 @@
     if masked:
         mask, *outs = refs
     else:
-        grad, other, second, first, *outs = refs
+        grad, other, *results, second, first, out, sems = refs
+        outs = [out]
 
         @pl.when(odd)
         def _():
@@ -195,6 +196,19 @@
         def _():
             second[...] = other[...].astype(second.dtype)
             first[...] = grad[...].astype(first.dtype)
+
+        quarter = out.shape[0] // 4
+        copies = [
+            pltpu.make_async_copy(second, results[0], sems.at[0]),
+            pltpu.make_async_copy(first, results[1], sems.at[1]),
+        ]
+        for n in range(4):
+            rows = pl.ds(n * quarter, quarter)
+            copies.append(
+                pltpu.make_async_copy(out.at[rows], results[2].at[rows], sems.at[2 + n])
+            )
+        copies[0].start()
+        copies[1].start()
 
     places = [(out, i) for out in outs for i in range(out.shape[0] // size)]
 
@@ -215,6 +229,11 @@
                 far = [apart, next_apart] if is_upper else [next_apart, apart]
                 for tile in range(tile_count):
                     write(tile, near[tile // half], far[tile // half])
+                    if not masked and (tile + 1) % (tile_count // 4) == 0:
+                        copies[2 + tile // (tile_count // 4)].start()
+
+    for copy in () if masked else copies:
+        copy.wait()
 
 
 def boundary(own, sends):
@@ -229,7 +248,10 @@
         functools.partial(join_kernel, masked, 2 * sums[1].shape[0]),
         out_shape=outs,
         in_specs=[VMEM] * len(args),
-        out_specs=[VMEM] * len(outs),
+        out_specs=[VMEM if masked else ANY] * len(outs),
+        scratch_shapes=[]
+        if masked
+        else [*(pltpu.VMEM(o.shape, o.dtype) for o in outs), pltpu.SemaphoreType.DMA((6,))],
         compiler_params=pltpu.CompilerParams(vmem_limit_bytes=8 << 20),
         cost_estimate=pl.CostEstimate(
             flops=0, bytes_accessed=12 * sums[1].size, transcendentals=0

time: 97.3 us -> 97.2 us (level)
  no operation moved by 1% of the time
where the time goes in v5:
time: 97.2 us; the launch traced here: 96.8 us
  starting transfers between devices  38.9 us (40%)
  waiting for transfers between devices  37.1 us (38%)
  Pallas kernels  13.5 us (14%)
  local copies, waits for them, and re-layouts  6.41 us (7%)
    ppermute x30, starting transfers between devices, exchanged(): return lax.ppermute(value, axis, pairs)  38.9 us
    ppermute x30, waiting for transfers between devices, exchanged(): return lax.ppermute(value, axis, pairs)  37.1 us
    pallas_call x4, Pallas kernels, spread(): pl.pallas_call(functools.partial(spread_kernel, total is None, tiles), ou...  7.3 us
    unnamed x13, local copies, waits for them, and re-layouts  4.48 us
    pallas_call x1, Pallas kernels, prepare(): pl.pallas_call(prepare_kernel, out_shape=outs, in_specs=[ANY, pl.BlockSpe...  2.52 us
    pallas_call x4, Pallas kernels, small_call(): pl.pallas_call(kernel, out_shape=outs, in_specs=[VMEM] * len(args), out_s...  2.24 us
  transfers between devices with their start and end apart: 30, of which 10 were waited for; matrix products, arithmetic and copies ran while one was open for 2% of the time, Pallas kernels for 12%

profile of v5, /device:TPU:0, one launch (start us, length us, event | category | flops | bytes accessed | tf_op | source)
XLA Modules:
  0.0 96.8 jit_solution(13456500060468842156)
XLA Ops:
  1.6 3.0 %collective-permute-start.4 = (bf16[1280,128]{1,0:T(8,128)(2,1)S(1)}, bf16[1280,128]{1,0:T(8,128)(2,1)S(1)}, u32[]{:S(2)}, u32[]{:S(2)}) collective-permute-start(bf16[1280,128]{1,0:T(8,128)(2,1)S(1)} %slice.7.refs_0_), channel_id=1, source_target_pairs={{0,2},{1,3},{2,0},{3,1},{4,6},{5,7},{6,4},{7,5},{8,10},{9,11},{10,... | collective-permute-start | bytes 983048 | tf_op jit(solution)/shard_map/ppermute | solution.py:20
  5.7 2.0 %collective-permute-start.1 = (bf16[768,128]{1,0:T(8,128)(2,1)S(1)}, bf16[768,128]{1,0:T(8,128)(2,1)S(1)}, u32[]{:S(2)}, u32[]{:S(2)}) collective-permute-start(bf16[768,128]{1,0:T(8,128)(2,1)S(1)} %slice.8.refs_0_.refs_4_), channel_id=1, source_target_pairs={{0,2},{1,3},{2,0},{3,1},{4,6},{5,7},{6,4},{7,5},{8,10},{9,11},{10,... | collective-permute-start | bytes 589832 | tf_op jit(solution)/shard_map/ppermute | solution.py:20
  8.5 1.9 %copy-done = bf16[16,6,128,128]{3,2,1,0:T(8,128)(2,1)S(1)} copy-done((bf16[16,6,128,128]{3,2,1,0:T(8,128)(2,1)S(1)}, bf16[16,6,128,128]{3,2,1,0:T(8,128)(2,1)}, u32[]{:S(2)}) %copy-start) | copy-done | bytes 3145752
  12.2 2.5 %prepare.1 = (s32[16,6]{1,0:T(8,128)S(1)}, bf16[16,6,128,128]{3,2,1,0:T(8,128)(2,1)S(1)}, bf16[512,128]{1,0:T(8,128)(2,1)S(1)}, bf16[512,128]{1,0:T(8,128)(2,1)S(1)}) custom-call(s32[16,6]{1,0:T(8,128)S(1)} %copy.13.targets_hbm, bf16[16,6,128,128]{3,2,1,0:T(8,128)(2,1)S(1)} %copy-done, bf16[128,512]{1,0:T(8,128)(2,1)S(1)} %copy-done.4, ...), custom_call_target="tpu_custom_call" | custom-call | bytes 6291456 | tf_op jit(solution)/shard_map/prepare/pallas_call | solution.py:95
  15.4 12.5 %collective-permute-done.1.refs_2_.refs_6_ = bf16[768,128]{1,0:T(8,128)(2,1)S(1)} collective-permute-done((bf16[768,128]{1,0:T(8,128)(2,1)S(1)}, bf16[768,128]{1,0:T(8,128)(2,1)S(1)}, u32[]{:S(2)}, u32[]{:S(2)}) %collective-permute-start.1) | collective-permute-done | bytes 196640 | tf_op jit(solution)/shard_map/ppermute | solution.py:20
  27.8 2.2 %spread.4.refs_4_ = f32[48,128,128]{2,1,0:T(8,128)S(1)} custom-call(s32[16,6]{1,0:T(8,128)S(1)} %get-tuple-element.27.slots_ref, bf16[512,128]{1,0:T(8,128)(2,1)S(1)} %get-tuple-element.30.weights, bf16[16,6,128,128]{3,2,1,0:T(8,128)(2,1)S(1)} %get-tuple-element.29.blocks, bf16[1280,128]{1,0:T(8,128)(2,1)S(1)} %slice.7.refs_0_, ...), custom_call_target="tpu_custom_call" | custom-call | flops 419430400 | bytes 4587520 | tf_op jit(solution)/shard_map/spread/pallas_call | solution.py:162
  30.1 1.5 %spread.5 = (f32[48,128,128]{2,1,0:T(8,128)S(1)}, bf16[8,128,128]{2,1,0:T(8,128)(2,1)S(1)}, bf16[8,128,128]{2,1,0:T(8,128)(2,1)S(1)}, bf16[8,128,128]{2,1,0:T(8,128)(2,1)S(1)}, bf16[8,128,128]{2,1,0:T(8,128)(2,1)S(1)}) custom-call(s32[16,6]{1,0:T(8,128)S(1)} %get-tuple-element.27.slots_ref, ...), custom_call_target="tpu_custom_call", output_to_operand_aliasing={{0}: (7, {})} | custom-call | flops 251658240 | bytes 2752512 | tf_op jit(solution)/shard_map/spread/pallas_call | solution.py:162
  32.9 4.5 %collective-permute-start.7 = (bf16[8,128,128]{2,1,0:T(8,128)(2,1)S(1)}, bf16[8,128,128]{2,1,0:T(8,128)(2,1)S(1)}, u32[]{:S(2)}, u32[]{:S(2)}) collective-permute-start(bf16[8,128,128]{2,1,0:T(8,128)(2,1)S(1)} %get-tuple-element.34), channel_id=1, source_target_pairs={{0,4},{4,0},{8,12},{12,8},{16,20},{20,16},{24,28},{28,24},{1,5},{5... | collective-permute-start | bytes 786440 | tf_op jit(solution)/shard_map/ppermute | solution.py:20
  38.1 7.0 %collective-permute-start.9 = (bf16[8,128,128]{2,1,0:T(8,128)(2,1)S(1)}, bf16[8,128,128]{2,1,0:T(8,128)(2,1)S(1)}, u32[]{:S(2)}, u32[]{:S(2)}) collective-permute-start(bf16[8,128,128]{2,1,0:T(8,128)(2,1)S(1)} %get-tuple-element.36), channel_id=1, source_target_pairs={{0,8},{4,12},{8,0},{12,4},{16,24},{20,28},{24,16},{28,20},{1,9},{5... | collective-permute-start | bytes 786440 | tf_op jit(solution)/shard_map/ppermute | solution.py:20
  45.8 2.2 %collective-permute-done.7.across = bf16[8,128,128]{2,1,0:T(8,128)(2,1)S(1)} collective-permute-done((bf16[8,128,128]{2,1,0:T(8,128)(2,1)S(1)}, bf16[8,128,128]{2,1,0:T(8,128)(2,1)S(1)}, u32[]{:S(2)}, u32[]{:S(2)}) %collective-permute-start.7) | collective-permute-done | bytes 262176 | tf_op jit(solution)/shard_map/ppermute | solution.py:20
  48.0 3.1 %collective-permute-done.9.apart = bf16[8,128,128]{2,1,0:T(8,128)(2,1)S(1)} collective-permute-done((bf16[8,128,128]{2,1,0:T(8,128)(2,1)S(1)}, bf16[8,128,128]{2,1,0:T(8,128)(2,1)S(1)}, u32[]{:S(2)}, u32[]{:S(2)}) %collective-permute-start.9) | collective-permute-done | bytes 262176 | tf_op jit(solution)/shard_map/ppermute | solution.py:20
  52.2 1.7 %collective-permute-start.23 = (bf16[4,128,128]{2,1,0:T(8,128)(2,1)S(1)}, bf16[4,128,128]{2,1,0:T(8,128)(2,1)S(1)}, u32[]{:S(2)}, u32[]{:S(2)}) collective-permute-start(bf16[4,128,128]{2,1,0:T(8,128)(2,1)S(1)} %get-tuple-element.46), channel_id=1, source_target_pairs={{0,4},{4,0},{8,12},{12,8},{16,20},{20,16},{24,28},{28,24},{1,5},{5... | collective-permute-start | bytes 393224 | tf_op jit(solution)/shard_map/ppermute | solution.py:20
  54.0 1.5 %collective-permute-start.14 = (bf16[1280,128]{1,0:T(8,128)(2,1)S(1)}, bf16[1280,128]{1,0:T(8,128)(2,1)S(1)}, u32[]{:S(2)}, u32[]{:S(2)}) collective-permute-start(bf16[1280,128]{1,0:T(8,128)(2,1)S(1)} %get-tuple-element.38.refs_0_.refs_4_), channel_id=1, source_target_pairs={{0,2},{1,3},{2,0},{3,1},{4,6},{5,7},{6,4},{7,5},{8,10},{9,11},{10,... | collective-permute-start | bytes 983048 | tf_op jit(solution)/shard_map/ppermute | solution.py:20
  57.3 2.8 %collective-permute-start.24 = (bf16[4,128,128]{2,1,0:T(8,128)(2,1)S(1)}, bf16[4,128,128]{2,1,0:T(8,128)(2,1)S(1)}, u32[]{:S(2)}, u32[]{:S(2)}) collective-permute-start(bf16[4,128,128]{2,1,0:T(8,128)(2,1)S(1)} %add_convert_fusion.1), channel_id=1, source_target_pairs={{0,16},{4,20},{8,24},{12,28},{16,0},{20,4},{24,8},{28,12},{1,17},{... | collective-permute-start | bytes 393224 | tf_op jit(solution)/shard_map/ppermute | solution.py:20
  60.2 4.0 %collective-permute-done.14.refs_2_ = bf16[1280,128]{1,0:T(8,128)(2,1)S(1)} collective-permute-done((bf16[1280,128]{1,0:T(8,128)(2,1)S(1)}, bf16[1280,128]{1,0:T(8,128)(2,1)S(1)}, u32[]{:S(2)}, u32[]{:S(2)}) %collective-permute-start.14) | collective-permute-done | bytes 327712 | tf_op jit(solution)/shard_map/ppermute | solution.py:20
  64.6 1.6 %collective-permute-done.11.refs_2_ = bf16[768,128]{1,0:T(8,128)(2,1)S(1)} collective-permute-done((bf16[768,128]{1,0:T(8,128)(2,1)S(1)}, bf16[768,128]{1,0:T(8,128)(2,1)S(1)}, u32[]{:S(2)}, u32[]{:S(2)}) %collective-permute-start.11) | collective-permute-done | bytes 196640 | tf_op jit(solution)/shard_map/ppermute | solution.py:20
  67.5 2.2 %spread.6.refs_4_ = f32[48,128,128]{2,1,0:T(8,128)S(1)} custom-call(s32[16,6]{1,0:T(8,128)S(1)} %get-tuple-element.27.slots_ref, bf16[512,128]{1,0:T(8,128)(2,1)S(1)} %get-tuple-element.28.weights, bf16[16,6,128,128]{3,2,1,0:T(8,128)(2,1)S(1)} %get-tuple-element.29.blocks, bf16[1280,128]{1,0:T(8,128)(2,1)S(1)} %get-tuple-element.38.refs_0_.refs_4_, ...), custom_call_target="tpu_custom_call" | custom-call | flops 419430400 | bytes 4587520 | tf_op jit(solution)/shard_map/spread/pallas_call | solution.py:162
  69.7 1.5 %spread.7 = (f32[48,128,128]{2,1,0:T(8,128)S(1)}, bf16[8,128,128]{2,1,0:T(8,128)(2,1)S(1)}, bf16[8,128,128]{2,1,0:T(8,128)(2,1)S(1)}, bf16[8,128,128]{2,1,0:T(8,128)(2,1)S(1)}, bf16[8,128,128]{2,1,0:T(8,128)(2,1)S(1)}) custom-call(s32[16,6]{1,0:T(8,128)S(1)} %get-tuple-element.27.slots_ref, ...), custom_call_target="tpu_custom_call", output_to_operand_aliasing={{0}: (7, {})} | custom-call | flops 251658240 | bytes 2752512 | tf_op jit(solution)/shard_map/spread/pallas_call | solution.py:162
  71.8 3.7 %collective-permute-start.17 = (bf16[8,128,128]{2,1,0:T(8,128)(2,1)S(1)}, bf16[8,128,128]{2,1,0:T(8,128)(2,1)S(1)}, u32[]{:S(2)}, u32[]{:S(2)}) collective-permute-start(bf16[8,128,128]{2,1,0:T(8,128)(2,1)S(1)} %get-tuple-element.41), channel_id=1, source_target_pairs={{0,4},{4,0},{8,12},{12,8},{16,20},{20,16},{24,28},{28,24},{1,5},{5... | collective-permute-start | bytes 786440 | tf_op jit(solution)/shard_map/ppermute | solution.py:20
  76.2 4.5 %collective-permute-start.19 = (bf16[8,128,128]{2,1,0:T(8,128)(2,1)S(1)}, bf16[8,128,128]{2,1,0:T(8,128)(2,1)S(1)}, u32[]{:S(2)}, u32[]{:S(2)}) collective-permute-start(bf16[8,128,128]{2,1,0:T(8,128)(2,1)S(1)} %get-tuple-element.43), channel_id=1, source_target_pairs={{0,8},{4,12},{8,0},{12,4},{16,24},{20,28},{24,16},{28,20},{1,9},{5... | collective-permute-start | bytes 786440 | tf_op jit(solution)/shard_map/ppermute | solution.py:20
  82.5 1.5 %collective-permute-start.27 = (bf16[128,128]{1,0:T(8,128)(2,1)S(1)}, bf16[128,128]{1,0:T(8,128)(2,1)S(1)}, u32[]{:S(2)}, u32[]{:S(2)}) collective-permute-start(bf16[128,128]{1,0:T(8,128)(2,1)S(1)} %get-tuple-element.49), channel_id=1, source_target_pairs={{0,2},{1,3},{2,0},{3,1},{4,6},{5,7},{6,4},{7,5},{8,10},{9,11},{10,... | collective-permute-start | bytes 98312 | tf_op jit(solution)/shard_map/ppermute | solution.py:20
  84.0 2.5 %collective-permute-done.27.refs_1_ = bf16[128,128]{1,0:T(8,128)(2,1)S(1)} collective-permute-done((bf16[128,128]{1,0:T(8,128)(2,1)S(1)}, bf16[128,128]{1,0:T(8,128)(2,1)S(1)}, u32[]{:S(2)}, u32[]{:S(2)}) %collective-permute-start.27) | collective-permute-done | bytes 32800 | tf_op jit(solution)/shard_map/ppermute | solution.py:20
  86.8 3.3 %collective-permute-done.28.refs_2_ = bf16[128,128]{1,0:T(8,128)(2,1)S(1)} collective-permute-done((bf16[128,128]{1,0:T(8,128)(2,1)S(1)}, bf16[128,128]{1,0:T(8,128)(2,1)S(1)}, u32[]{:S(2)}, u32[]{:S(2)}) %collective-permute-start.28) | collective-permute-done | bytes 32800 | tf_op jit(solution)/shard_map/ppermute | solution.py:20
  90.3 5.5 %collective-permute-done.29.refs_1_ = bf16[128,512]{1,0:T(8,128)(2,1)S(1)} collective-permute-done((bf16[128,512]{1,0:T(8,128)(2,1)S(1)}, bf16[128,512]{1,0:T(8,128)(2,1)S(1)}, u32[]{:S(2)}, u32[]{:S(2)}) %collective-permute-start.29) | collective-permute-done | bytes 131104 | tf_op jit(solution)/shard_map/ppermute | solution.py:20
  (64 shorter events, 17.6 us)
Async XLA Ops:
  1.6 13.1 %collective-permute-start.4 = (bf16[1280,128]{1,0:T(8,128)(2,1)S(1)}, bf16[1280,128]{1,0:T(8,128)(2,1)S(1)}, u32[]{:S(2)}, u32[]{:S(2)}) collective-permute-start(bf16[1280,128]{1,0:T(8,128)(2,1)S(1)} %slice.7.refs_0_), channel_id=1, source_target_pairs={{0,2},{1,3},{2,0},{3,1},{4,6},{5,7},{6,4},{7,5},{8,10},{9,11},{10,... | collective-permute-start | bytes 983048 | tf_op jit(solution)/shard_map/ppermute | solution.py:20
  4.7 28.2 %collective-permute-start.21 = (bf16[2048,128]{1,0:T(8,128)(2,1)}, bf16[2048,128]{1,0:T(8,128)(2,1)S(1)}, u32[]{:S(2)}, u32[]{:S(2)}) collective-permute-start(bf16[2048,128]{1,0:T(8,128)(2,1)} %refs_0_.5), channel_id=1, source_target_pairs={{0,2},{1,3},{2,0},{3,1},{4,6},{5,7},{6,4},{7,5},{8,10},{9,11},{10,... | collective-permute-start | bytes 1572872 | tf_op jit(solution)/shard_map/ppermute | solution.py:20
  5.7 22.1 %collective-permute-start.1 = (bf16[768,128]{1,0:T(8,128)(2,1)S(1)}, bf16[768,128]{1,0:T(8,128)(2,1)S(1)}, u32[]{:S(2)}, u32[]{:S(2)}) collective-permute-start(bf16[768,128]{1,0:T(8,128)(2,1)S(1)} %slice.8.refs_0_.refs_4_), channel_id=1, source_target_pairs={{0,2},{1,3},{2,0},{3,1},{4,6},{5,7},{6,4},{7,5},{8,10},{9,11},{10,... | collective-permute-start | bytes 589832 | tf_op jit(solution)/shard_map/ppermute | solution.py:20
  7.7 20.1 %collective-permute-start.3 = (bf16[1280,128]{1,0:T(8,128)(2,1)S(1)}, bf16[1280,128]{1,0:T(8,128)(2,1)S(1)}, u32[]{:S(2)}, u32[]{:S(2)}) collective-permute-start(bf16[1280,128]{1,0:T(8,128)(2,1)S(1)} %slice.7.refs_0_), channel_id=1, source_target_pairs={{0,1},{1,0},{2,3},{3,2},{4,5},{5,4},{6,7},{7,6},{8,9},{9,8},{10,11... | collective-permute-start | bytes 983048 | tf_op jit(solution)/shard_map/ppermute | solution.py:20
  14.7 13.1 %collective-permute-start.5 = (bf16[1280,128]{1,0:T(8,128)(2,1)S(1)}, bf16[1280,128]{1,0:T(8,128)(2,1)S(1)}, u32[]{:S(2)}, u32[]{:S(2)}) collective-permute-start(bf16[1280,128]{1,0:T(8,128)(2,1)S(1)} %collective-permute-done.4.refs_2_), channel_id=1, source_target_pairs={{0,1},{1,0},{2,3},{3,2},{4,5},{5,4},{6,7},{7,6},{8,9},{9,8},{10,11... | collective-permute-start | bytes 983048 | tf_op jit(solution)/shard_map/ppermute | solution.py:20
  15.3 14.8 %collective-permute-start = (bf16[768,128]{1,0:T(8,128)(2,1)S(1)}, bf16[768,128]{1,0:T(8,128)(2,1)S(1)}, u32[]{:S(2)}, u32[]{:S(2)}) collective-permute-start(bf16[768,128]{1,0:T(8,128)(2,1)S(1)} %slice.8.refs_0_.refs_4_), channel_id=1, source_target_pairs={{0,1},{1,0},{2,3},{3,2},{4,5},{5,4},{6,7},{7,6},{8,9},{9,8},{10,11... | collective-permute-start | bytes 589832 | tf_op jit(solution)/shard_map/ppermute | solution.py:20
  31.6 6.5 %collective-permute-start.6 = (bf16[8,128,128]{2,1,0:T(8,128)(2,1)S(1)}, bf16[8,128,128]{2,1,0:T(8,128)(2,1)S(1)}, u32[]{:S(2)}, u32[]{:S(2)}) collective-permute-start(bf16[8,128,128]{2,1,0:T(8,128)(2,1)S(1)} %get-tuple-element.33), channel_id=1, source_target_pairs={{4,8},{8,4},{12,16},{16,12},{20,24},{24,20},{5,9},{9,5},{13,17},{1... | collective-permute-start | bytes 786440 | tf_op jit(solution)/shard_map/ppermute | solution.py:20
  32.3 19.2 %collective-permute-start.20 = (bf16[2048,128]{1,0:T(8,128)(2,1)S(1)}, bf16[2048,128]{1,0:T(8,128)(2,1)S(1)}, u32[]{:S(2)}, u32[]{:S(2)}) collective-permute-start(bf16[2048,128]{1,0:T(8,128)(2,1)S(1)} %copy-done.3), channel_id=1, source_target_pairs={{0,1},{1,0},{2,3},{3,2},{4,5},{5,4},{6,7},{7,6},{8,9},{9,8},{10,11... | collective-permute-start | bytes 1572872 | tf_op jit(solution)/shard_map/ppermute | solution.py:20
  32.8 18.6 %collective-permute-start.22 = (bf16[2048,128]{1,0:T(8,128)(2,1)S(1)}, bf16[2048,128]{1,0:T(8,128)(2,1)S(1)}, u32[]{:S(2)}, u32[]{:S(2)}) collective-permute-start(bf16[2048,128]{1,0:T(8,128)(2,1)S(1)} %collective-permute-done.21.refs_2_), channel_id=1, source_target_pairs={{0,1},{1,0},{2,3},{3,2},{4,5},{5,4},{6,7},{7,6},{8,9},{9,8},{10,11... | collective-permute-start | bytes 1572872 | tf_op jit(solution)/shard_map/ppermute | solution.py:20
  32.9 15.1 %collective-permute-start.7 = (bf16[8,128,128]{2,1,0:T(8,128)(2,1)S(1)}, bf16[8,128,128]{2,1,0:T(8,128)(2,1)S(1)}, u32[]{:S(2)}, u32[]{:S(2)}) collective-permute-start(bf16[8,128,128]{2,1,0:T(8,128)(2,1)S(1)} %get-tuple-element.34), channel_id=1, source_target_pairs={{0,4},{4,0},{8,12},{12,8},{16,20},{20,16},{24,28},{28,24},{1,5},{5... | collective-permute-start | bytes 786440 | tf_op jit(solution)/shard_map/ppermute | solution.py:20
  37.4 10.6 %collective-permute-start.8 = (bf16[8,128,128]{2,1,0:T(8,128)(2,1)S(1)}, bf16[8,128,128]{2,1,0:T(8,128)(2,1)S(1)}, u32[]{:S(2)}, u32[]{:S(2)}) collective-permute-start(bf16[8,128,128]{2,1,0:T(8,128)(2,1)S(1)} %get-tuple-element.35), channel_id=1, source_target_pairs={{8,16},{12,20},{16,8},{20,12},{9,17},{13,21},{17,9},{21,13},{10,18... | collective-permute-start | bytes 786440 | tf_op jit(solution)/shard_map/ppermute | solution.py:20
  38.1 13.0 %collective-permute-start.9 = (bf16[8,128,128]{2,1,0:T(8,128)(2,1)S(1)}, bf16[8,128,128]{2,1,0:T(8,128)(2,1)S(1)}, u32[]{:S(2)}, u32[]{:S(2)}) collective-permute-start(bf16[8,128,128]{2,1,0:T(8,128)(2,1)S(1)} %get-tuple-element.36), channel_id=1, source_target_pairs={{0,8},{4,12},{8,0},{12,4},{16,24},{20,28},{24,16},{28,20},{1,9},{5... | collective-permute-start | bytes 786440 | tf_op jit(solution)/shard_map/ppermute | solution.py:20
  52.2 5.0 %collective-permute-start.23 = (bf16[4,128,128]{2,1,0:T(8,128)(2,1)S(1)}, bf16[4,128,128]{2,1,0:T(8,128)(2,1)S(1)}, u32[]{:S(2)}, u32[]{:S(2)}) collective-permute-start(bf16[4,128,128]{2,1,0:T(8,128)(2,1)S(1)} %get-tuple-element.46), channel_id=1, source_target_pairs={{0,4},{4,0},{8,12},{12,8},{16,20},{20,16},{24,28},{28,24},{1,5},{5... | collective-permute-start | bytes 393224 | tf_op jit(solution)/shard_map/ppermute | solution.py:20
  54.0 10.2 %collective-permute-start.14 = (bf16[1280,128]{1,0:T(8,128)(2,1)S(1)}, bf16[1280,128]{1,0:T(8,128)(2,1)S(1)}, u32[]{:S(2)}, u32[]{:S(2)}) collective-permute-start(bf16[1280,128]{1,0:T(8,128)(2,1)S(1)} %get-tuple-element.38.refs_0_.refs_4_), channel_id=1, source_target_pairs={{0,2},{1,3},{2,0},{3,1},{4,6},{5,7},{6,4},{7,5},{8,10},{9,11},{10,... | collective-permute-start | bytes 983048 | tf_op jit(solution)/shard_map/ppermute | solution.py:20
  55.5 10.8 %collective-permute-start.11 = (bf16[768,128]{1,0:T(8,128)(2,1)S(1)}, bf16[768,128]{1,0:T(8,128)(2,1)S(1)}, u32[]{:S(2)}, u32[]{:S(2)}) collective-permute-start(bf16[768,128]{1,0:T(8,128)(2,1)S(1)} %get-tuple-element.37.refs_0_.refs_5_), channel_id=1, source_target_pairs={{0,2},{1,3},{2,0},{3,1},{4,6},{5,7},{6,4},{7,5},{8,10},{9,11},{10,... | collective-permute-start | bytes 589832 | tf_op jit(solution)/shard_map/ppermute | solution.py:20
  57.3 8.9 %collective-permute-start.24 = (bf16[4,128,128]{2,1,0:T(8,128)(2,1)S(1)}, bf16[4,128,128]{2,1,0:T(8,128)(2,1)S(1)}, u32[]{:S(2)}, u32[]{:S(2)}) collective-permute-start(bf16[4,128,128]{2,1,0:T(8,128)(2,1)S(1)} %add_convert_fusion.1), channel_id=1, source_target_pairs={{0,16},{4,20},{8,24},{12,28},{16,0},{20,4},{24,8},{28,12},{1,17},{... | collective-permute-start | bytes 393224 | tf_op jit(solution)/shard_map/ppermute | solution.py:20
  60.2 7.3 %collective-permute-start.13 = (bf16[1280,128]{1,0:T(8,128)(2,1)S(1)}, bf16[1280,128]{1,0:T(8,128)(2,1)S(1)}, u32[]{:S(2)}, u32[]{:S(2)}) collective-permute-start(bf16[1280,128]{1,0:T(8,128)(2,1)S(1)} %get-tuple-element.38.refs_0_.refs_4_), channel_id=1, source_target_pairs={{0,1},{1,0},{2,3},{3,2},{4,5},{5,4},{6,7},{7,6},{8,9},{9,8},{10,11... | collective-permute-start | bytes 983048 | tf_op jit(solution)/shard_map/ppermute | solution.py:20
  64.1 5.5 %collective-permute-start.10 = (bf16[768,128]{1,0:T(8,128)(2,1)S(1)}, bf16[768,128]{1,0:T(8,128)(2,1)S(1)}, u32[]{:S(2)}, u32[]{:S(2)}) collective-permute-start(bf16[768,128]{1,0:T(8,128)(2,1)S(1)} %get-tuple-element.37.refs_0_.refs_5_), channel_id=1, source_target_pairs={{0,1},{1,0},{2,3},{3,2},{4,5},{5,4},{6,7},{7,6},{8,9},{9,8},{10,11... | collective-permute-start | bytes 589832 | tf_op jit(solution)/shard_map/ppermute | solution.py:20
  66.3 14.4 %collective-permute-start.25 = (bf16[4,128,128]{2,1,0:T(8,128)(2,1)S(1)}, bf16[4,128,128]{2,1,0:T(8,128)(2,1)S(1)}, u32[]{:S(2)}, u32[]{:S(2)}) collective-permute-start(bf16[4,128,128]{2,1,0:T(8,128)(2,1)S(1)} %add_convert_fusion.value), channel_id=1, source_target_pairs={{0,8},{4,12},{8,0},{12,4},{16,24},{20,28},{24,16},{28,20},{1,9},{5... | collective-permute-start | bytes 393224 | tf_op jit(solution)/shard_map/ppermute | solution.py:20
  71.2 24.6 %collective-permute-start.16 = (bf16[8,128,128]{2,1,0:T(8,128)(2,1)S(1)}, bf16[8,128,128]{2,1,0:T(8,128)(2,1)S(1)}, u32[]{:S(2)}, u32[]{:S(2)}) collective-permute-start(bf16[8,128,128]{2,1,0:T(8,128)(2,1)S(1)} %get-tuple-element.40), channel_id=1, source_target_pairs={{4,8},{8,4},{12,16},{16,12},{20,24},{24,20},{5,9},{9,5},{13,17},{1... | collective-permute-start | bytes 786440 | tf_op jit(solution)/shard_map/ppermute | solution.py:20
  71.8 23.9 %collective-permute-start.17 = (bf16[8,128,128]{2,1,0:T(8,128)(2,1)S(1)}, bf16[8,128,128]{2,1,0:T(8,128)(2,1)S(1)}, u32[]{:S(2)}, u32[]{:S(2)}) collective-permute-start(bf16[8,128,128]{2,1,0:T(8,128)(2,1)S(1)} %get-tuple-element.41), channel_id=1, source_target_pairs={{0,4},{4,0},{8,12},{12,8},{16,20},{20,16},{24,28},{28,24},{1,5},{5... | collective-permute-start | bytes 786440 | tf_op jit(solution)/shard_map/ppermute | solution.py:20
  75.5 20.2 %collective-permute-start.18 = (bf16[8,128,128]{2,1,0:T(8,128)(2,1)S(1)}, bf16[8,128,128]{2,1,0:T(8,128)(2,1)S(1)}, u32[]{:S(2)}, u32[]{:S(2)}) collective-permute-start(bf16[8,128,128]{2,1,0:T(8,128)(2,1)S(1)} %get-tuple-element.42), channel_id=1, source_target_pairs={{8,16},{12,20},{16,8},{20,12},{9,17},{13,21},{17,9},{21,13},{10,18... | collective-permute-start | bytes 786440 | tf_op jit(solution)/shard_map/ppermute | solution.py:20
  76.2 19.6 %collective-permute-start.19 = (bf16[8,128,128]{2,1,0:T(8,128)(2,1)S(1)}, bf16[8,128,128]{2,1,0:T(8,128)(2,1)S(1)}, u32[]{:S(2)}, u32[]{:S(2)}) collective-permute-start(bf16[8,128,128]{2,1,0:T(8,128)(2,1)S(1)} %get-tuple-element.43), channel_id=1, source_target_pairs={{0,8},{4,12},{8,0},{12,4},{16,24},{20,28},{24,16},{28,20},{1,9},{5... | collective-permute-start | bytes 786440 | tf_op jit(solution)/shard_map/ppermute | solution.py:20
  90.2 5.6 %collective-permute-start.29 = (bf16[128,512]{1,0:T(8,128)(2,1)S(1)}, bf16[128,512]{1,0:T(8,128)(2,1)S(1)}, u32[]{:S(2)}, u32[]{:S(2)}) collective-permute-start(bf16[128,512]{1,0:T(8,128)(2,1)S(1)} %shard_map.106.refs_0_), channel_id=1, source_target_pairs={{0,4},{4,0},{8,12},{12,8},{16,20},{20,16},{24,28},{28,24},{1,5},{5... | collective-permute-start | bytes 393224 | tf_op jit(solution)/shard_map/ppermute | solution.py:20
  (12 other events, 59.7 us)
